TPU v7x, 32 devices: a whole 2x2x4 slice. The times are simulated.
32 devices in a mesh: dp: 8 (over z, y), tensor: 4 (over x, core).
Axes of the slice: x: 2, y: 2, z: 4, core: 2. Of those that a mesh axis runs over, the one named last changes fastest.
Arguments:
- queries: bfloat16 [7168, 4096], P('dp', 'tensor'), may hold values from -40 to 40
- passages: bfloat16 [7168, 4096], P('dp', 'tensor'), may hold values from -40 to 40
- matching: int32 [56, 8], P('dp'), may hold values from 0 to 55, as said below
Outputs:
- grad_queries: bfloat16 [7168, 4096], P('dp', 'tensor')
- grad_passages: bfloat16 [7168, 4096], P('dp', 'tensor')
- loss: float32 [], replicated
Inputs may be any that keep to these rules, and one draw needn't show every extreme that they name: The 56 entries of matching on one dp index name clusters of any one dp index at most 7 times, and some dp index exactly 7 times.
All inputs are finite; a program needn't handle non-finite values.
Results may differ from a plain program's by a relative error of at most 0.0038.
Values may be sent and summed in bfloat16 or wider, within the bound.
No kernel may reach another device: no remote copies, remote signals or barrier semaphores. Data moves between devices by JAX's collectives and lax.ppermute only.
A program may use at most 128 MiB of HBM per device.

v0:
```python
import jax
import jax.numpy as jnp
from jax import lax
from jax.sharding import PartitionSpec as P

D = 4096
CLUSTER = 128
PARTNERS = 8


def soft_part(logits, target):
    row_max = jnp.max(logits, axis=-1, keepdims=True)
    log_total = row_max + jnp.log(jnp.sum(jnp.exp(logits - row_max), axis=-1, keepdims=True))
    chances = jnp.exp(logits - log_total)
    cross_ent = log_total[..., 0] - jnp.sum(logits * target[None], axis=-1)
    weights = (chances - target[None]).astype(jnp.bfloat16)
    return (cross_ent, weights)


def shards(queries, passages, matching):
    data_size = lax.axis_size("dp")
    clusters = matching.shape[0]
    width_dev = queries.shape[1]
    blocks = PARTNERS + 1
    columns = blocks * CLUSTER
    requests = clusters * PARTNERS
    capacity = -(-requests // data_size)
    slot_count = data_size * capacity
    query_block = queries.reshape(clusters, CLUSTER, width_dev)
    passage_block = passages.reshape(clusters, CLUSTER, width_dev)
    flat_ids = matching.reshape(requests)
    owners = flat_ids // clusters
    local_ids = flat_ids % clusters
    same_owner = owners[:, None] == owners[None, :]
    earlier = jnp.arange(requests)[None, :] < jnp.arange(requests)[:, None]
    slot_rank = jnp.sum(jnp.where(same_owner & earlier, 1, 0), axis=1).astype(jnp.int32)
    target_slot = owners * capacity + slot_rank
    placing = jnp.arange(slot_count)[:, None] == target_slot[None, :]
    wanted = jnp.sum(jnp.where(placing, local_ids[None, :], 0), axis=1)
    asked_ids = lax.all_to_all(
        wanted.reshape(data_size, capacity), "dp", split_axis=0, concat_axis=0, tiled=True
    ).reshape(slot_count)
    outgoing = jnp.take(passage_block, asked_ids, axis=0).reshape(
        data_size, capacity, CLUSTER, width_dev
    )
    fetched = lax.all_to_all(outgoing, "dp", split_axis=0, concat_axis=0, tiled=True).reshape(
        slot_count, CLUSTER, width_dev
    )
    partner_keys = jnp.take(fetched, target_slot, axis=0).reshape(
        clusters, PARTNERS, CLUSTER, width_dev
    )
    all_keys = jnp.concatenate([passage_block[:, None], partner_keys], axis=1)
    partial_value = jnp.einsum(
        "cid,ckjd->cikj", query_block, all_keys, preferred_element_type=jnp.float32
    ).reshape(clusters, CLUSTER, columns)
    summed = lax.psum(partial_value, "tensor")
    logits = summed * D ** (-0.5)
    target = (jnp.arange(CLUSTER)[:, None] == jnp.arange(columns)[None, :]).astype(jnp.float32)
    cross_ent, weights_flat = soft_part(logits, target)
    loss_part = jnp.sum(cross_ent) / lax.axis_size("tensor")
    weights = weights_flat.reshape(clusters, CLUSTER, blocks, CLUSTER)
    loss_total = lax.psum(loss_part, ("dp", "tensor"))
    grad_q = jnp.einsum("cikj,ckjd->cid", weights, all_keys, preferred_element_type=jnp.float32)
    grad_own = jnp.einsum(
        "cij,cid->cjd", weights[:, :, 0], query_block, preferred_element_type=jnp.float32
    )
    partial_terms = jnp.einsum(
        "cikj,cid->ckjd", weights[:, :, 1:], query_block, preferred_element_type=jnp.float32
    ).astype(jnp.bfloat16)
    send_rows = (
        jnp.zeros((slot_count, CLUSTER, width_dev), jnp.bfloat16)
        .at[target_slot]
        .set(partial_terms.reshape(requests, CLUSTER, width_dev))
    )
    back_rows = lax.all_to_all(
        send_rows.reshape(data_size, capacity, CLUSTER, width_dev),
        "dp",
        split_axis=0,
        concat_axis=0,
        tiled=True,
    )
    back_terms = back_rows.reshape(slot_count, CLUSTER, width_dev).astype(jnp.float32)
    placing_back = (jnp.arange(clusters)[:, None] == asked_ids[None, :]).astype(jnp.float32)
    grad_p = grad_own + jnp.einsum(
        "cs,sjd->cjd", placing_back, back_terms, precision=lax.Precision.HIGHEST
    )
    squares = jnp.sum(grad_q * grad_q) + jnp.sum(grad_p * grad_p)
    square_total = lax.psum(squares, ("dp", "tensor"))
    all_rows = clusters * CLUSTER * data_size
    clip_limit = 0.25 * jnp.sqrt(jnp.float32(2 * all_rows * D))
    factor = jnp.minimum(jnp.float32(1.0), clip_limit / jnp.sqrt(square_total + 1e-06))
    grad_queries = (grad_q * factor).astype(jnp.bfloat16).reshape(clusters * CLUSTER, width_dev)
    grad_passages = (grad_p * factor).astype(jnp.bfloat16).reshape(clusters * CLUSTER, width_dev)
    return (grad_queries, grad_passages, loss_total / all_rows)


def solution(mesh):
    in_specs = (P("dp", "tensor"), P("dp", "tensor"), P("dp", None))
    out_specs = (P("dp", "tensor"), P("dp", "tensor"), P())
    return jax.shard_map(shards, mesh=mesh, in_specs=in_specs, out_specs=out_specs, check_vma=False)
```

profile of v0, /device:TPU:0, one launch (start us, length us, event | category | flops | bytes accessed | tf_op | source)
XLA Modules:
  0.0 944.0 jit_solution(5478094803836907478)
XLA Ops:
  7.2 0.8 sign_compare_fusion
  8.0 0.7 broadcast_divide_fusion
  8.7 0.1 ne.86
  9.0 0.2 select_reduce_fusion.1
  9.2 0.1 select_reduce_fusion
  9.3 13.5 %all_to_all.19 = s32[8,1,7]{2,1,0:T(1,128)S(1)} all-to-all(s32[8,1,7]{2,1,0:T(1,128)S(1)} %bitcast.72), channel_id=1, replica_groups=mesh['dp'=8,'tensor'=4] {'dp'}, dimensions={0} | all-to-all | bytes 448 | tf_op jit(solution)/shard_map/all_to_all | solution.py:40
  22.9 0.5 broadcast.241
  23.4 0.7 reduce.5
  24.2 8.5 gather_fusion
  32.7 13.6 %broadcast_select_fusion = bf16[8,7,128,1024]{3,2,1,0:T(8,128)(2,1)} fusion(bf16[8,7,128,1024]{3,2,1,0:T(8,128)(2,1)} %bitcast.63, pred[8,7]{1,0:T(8,128)(4,1)S(1)} %compare_and_fusion), kind=kLoop, calls=%fused_computation.6 | loop fusion | flops 7340032 | bytes 29360184 | tf_op jit(solution)/shard_map/jit(_take)/select_n | solution.py:43
  46.3 5.7 all-to-all-start.1
  52.2 0.1 and.62
  52.3 316.4 %all-to-all-done.1 = bf16[8,7,128,1024]{3,2,1,0:T(8,128)(2,1)} async-done(((bf16[8,7,128,1024]{3,2,1,0:T(8,128)(2,1)}), bf16[8,7,128,1024]{3,2,1,0:T(8,128)(2,1)}, u32[]{:S(2)}, u32[]{:S(2)}) %all-to-all-start.1) | async-done | bytes 14680096 | tf_op jit(solution)/shard_map/all_to_all | solution.py:46
  368.7 12.3 %gather_fusion.1 = bf16[56,128,1024]{2,1,0:T(8,128)(2,1)} fusion(bf16[56,128,1024]{2,1,0:T(8,128)(2,1)} %bitcast.6, s32[1024]{0:T(1024)S(1)} %pad_clamp_fusion), kind=kCustom, calls=%fused_computation.1 | custom fusion | bytes 29360352 | tf_op jit(solution)/shard_map/jit(_take)/gather | solution.py:49
  381.0 7.9 broadcast_select_fusion.1
  388.9 6.6 fusion.3
  395.7 83.5 %all-reduce.3.cloned.1.call-done = f32[7,128,1152]{1,2,0:T(8,128)} async-done(((f32[7,128,1152]{1,2,0:T(8,128)}), f32[7,128,1152]{1,2,0:T(8,128)}) %all-reduce.3.cloned.1.call-update) | async-done | bytes 4128784 | tf_op jit(solution)/shard_map/psum | solution.py:56
  479.2 2.6 multiply_reduce_fusion.2
  481.8 0.8 copy-done.2
  482.6 1.0 multiply_reduce_fusion
  483.6 0.6 subtract_reduce_fusion
  484.2 0.8 subtract_convert_fusion
  485.0 7.4 convolution_convert_fusion
  492.4 7.1 broadcast_in_dim.63
  499.5 37.0 %scatter_fusion = bf16[56,128,1024]{2,1,0:T(8,128)(2,1)} fusion(bf16[56,128,1024]{2,1,0:T(8,128)(2,1)} %broadcast_in_dim.63, s32[56]{0:T(128)S(1)} %fusion.17, bf16[56,128,1024]{2,1,0:T(8,128)(2,1)} %bitcast.61), kind=kCustom, calls=%fused_computation.2 | custom fusion | bytes 44040416 | tf_op jit(solution)/shard_map/scatter | solution.py:73
  536.4 5.7 all-to-all-start.2
  542.9 9.7 %fusion.4 = (f32[]{:T(128)}, f32[7,128,1024,1]{2,1,3,0:T(8,128)}) fusion(bf16[7,128,9,128]{1,3,2,0:T(8,128)(2,1)} %bitcast.65, bf16[7,8,128,1024]{3,2,1,0:T(8,128)(2,1)} %copy-done.3, bf16[7,1,128,1024]{3,2,1,0:T(8,128)(2,1)} %bitcast.59), kind=kOutput, calls=%fused_computation.16 | convolution fusion | flops 2124021760 | bytes 22249476 | tf_op jit(solution)/shard_map/cikj,ckjd->cid/dot_general | solution.py:63
  552.6 307.5 %all-to-all-done.2 = bf16[8,7,128,1024]{3,2,1,0:T(8,128)(2,1)} async-done(((bf16[8,7,128,1024]{3,2,1,0:T(8,128)(2,1)}), bf16[8,7,128,1024]{3,2,1,0:T(8,128)(2,1)}, u32[]{:S(2)}, u32[]{:S(2)}) %all-to-all-start.2) | async-done | bytes 14680096 | tf_op jit(solution)/shard_map/all_to_all | solution.py:75
  860.1 23.8 %fusion = f32[7,128,1024]{2,0,1:T(8,128)S(1)} fusion(bf16[56,128,1024]{2,1,0:T(8,128)(2,1)} %bitcast.24, s32[56]{0:T(128)S(1)} %reshape.252), kind=kOutput, calls=%fused_computation.4 | convolution fusion | flops 102760840 | bytes 18350304 | tf_op jit(solution)/shard_map/cs,sjd->cjd/dot_general | solution.py:84
  883.9 5.8 multiply_reduce_fusion.1
  891.0 37.6 %all-reduce = (f32[]{:T(128)}, f32[]{:T(128)}) all-reduce(f32[]{:T(128)S(6)} %add.130, f32[]{:T(128)S(6)} %div.45), channel_id=1, replica_groups=mesh['dp'=8,'tensor'=4] {'dp','tensor'}, use_global_device_ids=true, to_apply=%region_8.9 | all-reduce | flops 2 | bytes 16 | tf_op jit(solution)/shard_map/psum | solution.py:88
  930.0 6.1 fusion.5
  (30 shorter events, 0.8 us)
Async XLA Ops:
  7.2 381.7 %copy-start = (bf16[896,1024]{1,0:T(8,128)(2,1)S(1)}, bf16[896,1024]{1,0:T(8,128)(2,1)}, u32[]{:S(2)}) copy-start(bf16[896,1024]{1,0:T(8,128)(2,1)} %param.3) | copy-start | bytes 5505028
  46.3 5.9 copy-start.5
  46.3 322.4 %all-to-all-start.1 = ((bf16[8,7,128,1024]{3,2,1,0:T(8,128)(2,1)}), bf16[8,7,128,1024]{3,2,1,0:T(8,128)(2,1)}, u32[]{:S(2)}, u32[]{:S(2)}) async-start(bf16[8,7,128,1024]{3,2,1,0:T(8,128)(2,1)} %broadcast_select_fusion), calls=%async_computation.1 | async-start | bytes 29360128 | tf_op jit(solution)/shard_map/all_to_all | solution.py:46
  52.0 427.2 %all-reduce.3.cloned.1.call-start = ((), (), s32[]{:S(2)}) async-start(), calls=%async_computation.3 | async-start | bytes 8257536 | tf_op jit(solution)/shard_map/psum | solution.py:56
  380.9 7.9 copy-start.1
  388.9 6.7 copy-start.3
  479.2 3.4 copy-start.2
  485.0 7.4 copy-start.4
  536.4 323.7 %all-to-all-start.2 = ((bf16[8,7,128,1024]{3,2,1,0:T(8,128)(2,1)}), bf16[8,7,128,1024]{3,2,1,0:T(8,128)(2,1)}, u32[]{:S(2)}, u32[]{:S(2)}) async-start(bf16[8,7,128,1024]{3,2,1,0:T(8,128)(2,1)} %bitcast.57), calls=%async_computation.2 | async-start | bytes 29360128 | tf_op jit(solution)/shard_map/all_to_all | solution.py:75
Sparse Core Ops, SparseCore 0:
  395.7 83.4 all-reduce.2
where the time goes:
time: 946 us; the launch traced here: 944 us
  waiting for transfers between devices  707 us (75%)
  local copies, waits for them, and re-layouts  66.9 us (7%)
  matrix products  53.4 us (6%)
  blocking collectives  51.1 us (5%)
  other arithmetic  35.2 us (4%)
  between operations  18.6 us (2%)
  starting transfers between devices  11.5 us (1%)
    all_to_all x1, waiting for transfers between devices, shards(): lax.all_to_all(outgoing, 'dp', split_axis=0, concat_axis=0, tiled=True)  316 us
    all_to_all x1, waiting for transfers between devices, shards(): lax.all_to_all(send_rows.reshape(data_size, capacity, CLUSTER, width_dev)...  307 us
    psum x1, waiting for transfers between devices, shards(): summed = lax.psum(partial_value, 'tensor')  83.5 us
    psum x1, blocking collectives, shards(): square_total = lax.psum(squares, ('dp', 'tensor'))  37.6 us
    scatter x1, local copies, waits for them, and re-layouts, shards(): send_rows = jnp.zeros((slot_count, CLUSTER, width_dev), jnp.bfloat16).at[...  37 us
    dot_general x1, matrix products, shards(): jnp.einsum('cs,sjd->cjd', placing_back, back_terms, precision=lax.Precisi...  23.8 us
  transfers between devices with their start and end apart: 3, of which 3 were waited for; matrix products, arithmetic and copies ran while one was open for 1% of the time, Pallas kernels for 0%

commit v1 on v0

v1 whole, which is shorter than its diff:
```python
import functools

import jax
import jax.numpy as jnp
from jax import lax
from jax.experimental import pallas as pl
from jax.experimental.pallas import tpu as pltpu
from jax.sharding import PartitionSpec as P

CLUSTER = 128
PARTNERS = 8
LOW = -3.0e38
VALID = 1 << 16
VMEM_LIMIT = 56 * 1024 * 1024

VM = pl.BlockSpec(memory_space=pltpu.VMEM)
SM = pl.BlockSpec(memory_space=pltpu.SMEM)
NT = (((1,), (1,)), ((), ()))
TN = (((0,), (0,)), ((), ()))
NN = (((1,), (0,)), ((), ()))


def bits_of(size):
    return size.bit_length() - 1


def swap(value, axis, mask):
    size = lax.axis_size(axis)
    return lax.ppermute(value, axis, [(i, i ^ mask) for i in range(size)])


def call(kernel, out_shape, scratch, flops, moved, args, smem):
    return pl.pallas_call(
        kernel,
        out_shape=out_shape,
        in_specs=[SM] * smem + [VM] * (len(args) - smem),
        out_specs=jax.tree.map(lambda _: VM, out_shape),
        scratch_shapes=scratch,
        compiler_params=pltpu.CompilerParams(vmem_limit_bytes=VMEM_LIMIT),
        cost_estimate=pl.CostEstimate(flops=flops, bytes_accessed=moved, transcendentals=0),
    )(*args)


def unpack(code):
    return code >= VALID, (code >> 8) & 255, code & 255


def groups_of(mask, clusters, cap):
    base = clusters if mask == 0 else 0
    return [(0, base), (1, base + cap)]


def logits_kernel(mask, clusters, cap, ways, tab, rank, mine, other, keys, low, high, block):
    share = CLUSTER // ways
    me = rank[0]

    def one(rows, key, slot):
        block[...] = lax.dot_general(rows, key, NT, preferred_element_type=jnp.float32)
        for at in range(ways):
            start = pl.multiple_of((me ^ at) * share, share)
            (high if at % 2 else low)[at // 2, slot] = block[pl.ds(start, share), :]

    if mask == 0:

        @pl.loop(0, clusters)
        def _(c):
            one(mine[c], keys[c], c)

    for requester, first in groups_of(mask, clusters, cap):
        rows_ref = other if requester else mine

        @pl.loop(0, cap)
        def _(j):
            _, c, e = unpack(tab[requester, mask * cap + j])
            one(rows_ref[c], keys[e], first + j)


def each_slot(visit, chunks, clusters, cap, tab):
    for mask, ref in enumerate(chunks):
        if mask == 0:
            for c in range(clusters):
                visit(mask, ref, c, c, None)
        for requester, first in groups_of(mask, clusters, cap):

            @pl.loop(0, cap)
            def _(j):
                ok, c, _ = unpack(tab[requester, mask * cap + j])
                at = jnp.where(ok, requester * clusters + c, 2 * clusters)
                visit(mask, ref, first + j, at, ok)


def stats_kernel(parts, clusters, cap, scale, tab, *refs):
    chunks, stats, top, total = refs[:parts], refs[parts], refs[parts + 1], refs[parts + 2]
    top[...] = jnp.full_like(top, LOW)
    total[...] = jnp.zeros_like(total)

    def raise_top(mask, ref, slot, at, ok):
        top[at] = jnp.maximum(top[at], ref[slot] * scale)

    each_slot(raise_top, chunks, clusters, cap, tab)
    for c in range(2 * clusters + 1):
        top[c] = jnp.broadcast_to(jnp.max(top[c], axis=-1, keepdims=True), top.shape[1:])

    def add_total(mask, ref, slot, at, ok):
        total[at] = total[at] + jnp.exp(ref[slot] * scale - top[at])

    each_slot(add_total, chunks, clusters, cap, tab)
    lane = lax.broadcasted_iota(jnp.int32, stats.shape, 1)
    out = jnp.zeros(stats.shape, jnp.float32)
    for c in range(2 * clusters):
        out = jnp.where(lane == c, top[c], out)
        sums = jnp.sum(total[c], axis=-1, keepdims=True)
        out = jnp.where(lane == 2 * clusters + c, sums, out)
    stats[...] = out


def weights_kernel(parts, clusters, cap, scale, tab, rank, *refs):
    chunks, here, there = refs[:parts], refs[parts], refs[parts + 1]
    outs, loss, level = refs[parts + 2 : 2 * parts + 2], refs[2 * parts + 2], refs[2 * parts + 3]
    shape = here.shape
    row = lax.broadcasted_iota(jnp.int32, shape, 0) + rank[0] * shape[0]
    lane = lax.broadcasted_iota(jnp.int32, shape, 1)
    target = (row == lane).astype(jnp.float32)
    for c in range(2 * clusters):
        p = (c + clusters) % (2 * clusters)
        top_a, top_b = here[:, c : c + 1], there[:, p : p + 1]
        k = 2 * clusters
        sum_a, sum_b = here[:, k + c : k + c + 1], there[:, k + p : k + p + 1]
        top = jnp.maximum(top_a, top_b)
        total = sum_a * jnp.exp(top_a - top) + sum_b * jnp.exp(top_b - top)
        level[c] = jnp.broadcast_to(top + jnp.log(total), shape)
    level[2 * clusters] = jnp.zeros(shape, jnp.float32)
    loss[...] = jnp.zeros(shape, jnp.float32)

    def weigh(mask, ref, slot, at, ok):
        logits = ref[slot] * scale
        chances = jnp.exp(logits - level[at])
        if ok is None:
            chances = chances - target
            loss[...] += jnp.where(lane == 0, level[at], 0.0) - logits * target
        else:
            chances = jnp.where(ok, chances, 0.0)
        outs[mask][slot] = chances.astype(jnp.bfloat16)

    each_slot(weigh, chunks, clusters, cap, tab)


def whole_weights(pieces, order, me, slot, wide):
    share = CLUSTER // len(order)
    for piece, at in zip(pieces, order):
        start = pl.multiple_of((me ^ at) * share, share)
        wide[pl.ds(start, share), :] = piece[slot]
    return wide[...]


def term_kernel(mask, clusters, cap, order, arrived, tab, rank, mine, other, *refs):
    ways = len(order)
    pieces, came, out = refs[:ways], refs[ways : ways + arrived], refs[ways + arrived]
    wide, total = refs[ways + arrived + 1 :]
    me = rank[0]
    if mask == 0:

        @pl.loop(0, clusters)
        def _(c):
            w = whole_weights(pieces, order, me, c, wide)
            total[c] = lax.dot_general(w, mine[c], TN, preferred_element_type=jnp.float32)

    else:
        total[...] = jnp.zeros_like(total)
    for requester, first in groups_of(mask, clusters, cap):
        rows_ref = other if requester else mine

        @pl.loop(0, cap)
        def _(j):
            _, c, e = unpack(tab[requester, mask * cap + j])
            w = whole_weights(pieces, order, me, first + j, wide)
            total[e] += lax.dot_general(w, rows_ref[c], TN, preferred_element_type=jnp.float32)

    @pl.loop(0, clusters)
    def _(c):
        value = total[c]
        for ref in came:
            value = value + ref[c].astype(jnp.float32)
        out[c] = value.astype(out.dtype)


def query_kernel(requester, parts, clusters, cap, order, tab, rank, *refs):
    ways = len(order)
    keys = refs[:parts]
    pieces = [refs[parts + m * ways : parts + (m + 1) * ways] for m in range(parts)]
    out, wide, total = refs[parts + parts * ways :]
    me = rank[0]
    if requester == 0:

        @pl.loop(0, clusters)
        def _(c):
            w = whole_weights(pieces[0], order, me, c, wide)
            total[c] = lax.dot_general(w, keys[0][c], NN, preferred_element_type=jnp.float32)

    else:
        total[...] = jnp.zeros_like(total)
    for mask in range(parts):
        first = groups_of(mask, clusters, cap)[requester][1]

        @pl.loop(0, cap)
        def _(j):
            _, c, e = unpack(tab[requester, mask * cap + j])
            w = whole_weights(pieces[mask], order, me, first + j, wide)
            total[c] += lax.dot_general(w, keys[mask][e], NN, preferred_element_type=jnp.float32)

    @pl.loop(0, clusters)
    def _(c):
        out[c] = total[c].astype(out.dtype)


def shards(queries, passages, matching):
    bf16, f32 = jnp.bfloat16, jnp.float32
    size, ways = lax.axis_size("dp"), lax.axis_size("tensor")
    clusters, width = matching.shape[0], queries.shape[1]
    requests = clusters * PARTNERS
    cap = -(-requests // size)
    parts = size // 2
    share = CLUSTER // ways
    scale = (width * ways) ** (-0.5)
    cube = (clusters, CLUSTER, width)
    mine, own_keys = queries.reshape(cube), passages.reshape(cube)
    here = lax.axis_index("dp").astype(jnp.int32)
    rank = lax.axis_index("tensor").astype(jnp.int32).reshape(1)

    held = {0: own_keys}
    for bit in reversed(range(bits_of(parts))):
        for mask in sorted(held):
            held[mask | (1 << bit)] = swap(held[mask], "dp", 1 << bit)
    keys = [held[m] for m in range(parts)]
    both = jnp.stack([matching, swap(matching, "dp", parts)]).reshape(2, requests)
    other = swap(mine, "dp", parts)

    owner, local = both // clusters, both % clusters
    earlier = jnp.arange(requests)[None, :] < jnp.arange(requests)[:, None]
    same = owner[:, :, None] == owner[:, None, :]
    place = (owner ^ here) * cap + jnp.sum(jnp.where(same & earlier[None], 1, 0), axis=2)
    asker = (jnp.arange(requests) // PARTNERS)[None, :]
    code = VALID + asker * 256 + local
    slots = jnp.arange(parts * cap)[None, :, None] == place[:, None, :]
    tab = jnp.sum(jnp.where(slots, code[:, None, :], 0), axis=2).astype(jnp.int32)

    count = [2 * cap + (clusters if m == 0 else 0) for m in range(parts)]
    unit = 2 * CLUSTER * CLUSTER * width
    block_bytes = CLUSTER * width * 2
    chunks = []
    for m in range(parts):
        half = jax.ShapeDtypeStruct((ways // 2, count[m], share, CLUSTER), f32)
        keep, give = call(
            functools.partial(logits_kernel, m, clusters, cap, ways),
            (half, half),
            [pltpu.VMEM((CLUSTER, CLUSTER), f32)],
            count[m] * unit,
            3 * clusters * block_bytes,
            (tab, rank, mine, other, keys[m]),
            2,
        )
        got = swap(give, "tensor", 1)
        bit = 1
        while (1 << bit) < ways:
            keep = keep + got
            pairs = keep.reshape((keep.shape[0] // 2, 2) + keep.shape[1:])
            keep = pairs[:, 0]
            got = swap(pairs[:, 1], "tensor", 1 << bit)
            bit += 1
        chunks.append((keep + got)[0])

    tile = jax.ShapeDtypeStruct((share, CLUSTER), f32)
    levels = pltpu.VMEM((2 * clusters + 1, share, CLUSTER), f32)
    stats = call(
        functools.partial(stats_kernel, parts, clusters, cap, scale),
        tile, [levels, levels], 0, 2 << 20, (tab, *chunks), 1,
    )
    facing = swap(stats, "dp", parts)
    *weights, loss_rows = call(
        functools.partial(weights_kernel, parts, clusters, cap, scale),
        [jax.ShapeDtypeStruct(c.shape, bf16) for c in chunks] + [tile],
        [levels], 0, 2 << 20, (tab, rank, *chunks, stats, facing), 2,
    )
    order = [0]
    for bit in reversed(range(bits_of(ways))):
        order += [at | (1 << bit) for at in order]
    pieces = []
    for m in range(parts):
        group = [weights[m]]
        for bit in reversed(range(bits_of(ways))):
            group += [swap(piece, "tensor", 1 << bit) for piece in group]
        pieces.append(group)

    grow = [pltpu.VMEM((CLUSTER, CLUSTER), bf16), pltpu.VMEM(cube, f32)]
    terms, came = {}, {}
    for m in sorted(range(parts), key=lambda m: (bin(m)[::-1].find("1") if m else 99, -m)):
        low = bits_of(m & -m) if m else bits_of(parts)
        came = [swap(terms[m | (1 << b)], "dp", 1 << b) for b in range(low)]
        add = came if m else []
        terms[m] = call(
            functools.partial(term_kernel, m, clusters, cap, order, len(add)),
            jax.ShapeDtypeStruct(cube, bf16 if m else f32),
            grow, count[m] * unit, 4 * clusters * block_bytes,
            (tab, rank, mine, other, *pieces[m], *add), 2,
        )
    grads = {}
    for requester in (1, 0):
        grads[requester] = call(
            functools.partial(query_kernel, requester, parts, clusters, cap, order),
            jax.ShapeDtypeStruct(cube, bf16 if requester else f32),
            grow, parts * cap * unit, (parts + 2) * clusters * block_bytes,
            (tab, rank, *keys, *[p for group in pieces for p in group]), 2,
        )
    grad_q = grads[0] + swap(grads[1], "dp", parts).astype(f32)
    grad_p = terms[0]
    for part in came:
        grad_p = grad_p + part.astype(f32)

    squares = jnp.sum(grad_q * grad_q) + jnp.sum(grad_p * grad_p)
    sums = jnp.stack([jnp.sum(loss_rows), squares])
    for bit in range(bits_of(ways)):
        sums = sums + swap(sums, "tensor", 1 << bit)
    for bit in range(bits_of(size)):
        sums = sums + swap(sums, "dp", 1 << bit)
    all_rows = clusters * CLUSTER * size
    clip_limit = 0.25 * jnp.sqrt(jnp.float32(2 * all_rows * width * ways))
    factor = jnp.minimum(jnp.float32(1.0), clip_limit / jnp.sqrt(sums[1] + 1e-06))
    flat = queries.shape
    grad_queries = (grad_q * factor).astype(bf16).reshape(flat)
    grad_passages = (grad_p * factor).astype(bf16).reshape(flat)
    return (grad_queries, grad_passages, sums[0] / all_rows)


def solution(mesh):
    in_specs = (P("dp", "tensor"), P("dp", "tensor"), P("dp", None))
    out_specs = (P("dp", "tensor"), P("dp", "tensor"), P())
    return jax.shard_map(shards, mesh=mesh, in_specs=in_specs, out_specs=out_specs, check_vma=False)
```

time: 946 us -> 350 us (0.37)
  waiting for transfers between devices: 707 us -> 182 us
  Pallas kernels: 0 us -> 94.7 us
  local copies, waits for them, and re-layouts: 66.9 us -> 8.43 us
  matrix products: 53.4 us -> 0 us
  blocking collectives: 51.1 us -> 0 us
  starting transfers between devices: 11.5 us -> 36.7 us
  between operations: 18.6 us -> 4.67 us
  other arithmetic: 35.2 us -> 22.8 us
    all_to_all x2 -> x0, waiting for transfers between devices: 624 us -> none  [the longest x1 316 us: shards(): lax.all_to_all(outgoing, 'dp', split_axis=0, concat_axis=0, tiled=True)]
    ppermute x0 -> x35, waiting for transfers between devices: none -> 182 us  [swap(): return lax.ppermute(value, axis, [(i, i ^ mask) for i in range(size)])]
    pallas_call x0 -> x12, Pallas kernels: none -> 94.7 us  [call(): pl.pallas_call(kernel, out_shape=out_shape, in_specs=[SM] * smem + [VM] *...]
    psum x1 -> x0, waiting for transfers between devices: 83.5 us -> none  [shards(): summed = lax.psum(partial_value, 'tensor')]
    dot_general x5 -> x0, matrix products: 53.4 us -> none  [the longest x1 23.8 us: shards(): jnp.einsum('cs,sjd->cjd', placing_back, back_terms, precision=lax.Precisi...]
    psum x1 -> x0, blocking collectives: 37.6 us -> none  [shards(): square_total = lax.psum(squares, ('dp', 'tensor'))]
    scatter x1 -> x0, local copies, waits for them, and re-layouts: 37 us -> none  [shards(): send_rows = jnp.zeros((slot_count, CLUSTER, width_dev), jnp.bfloat16).at[...]
    ppermute x0 -> x35, starting transfers between devices: none -> 36.7 us  [swap(): return lax.ppermute(value, axis, [(i, i ^ mask) for i in range(size)])]
  transfers between devices with their start and end apart: 3 -> 35, of which waited for: 3 -> 18; matrix products, arithmetic and copies ran while one was open for 1% -> 3% of each run, Pallas kernels for 0% -> 23%
where the time goes in v1:
time: 350 us
  waiting for transfers between devices  182 us (52%)
  Pallas kernels  94.7 us (27%)
  starting transfers between devices  36.7 us (10%)
  other arithmetic  22.8 us (7%)
  local copies, waits for them, and re-layouts  8.43 us (2%)
  between operations  4.67 us (1%)
    ppermute x35, waiting for transfers between devices, swap(): return lax.ppermute(value, axis, [(i, i ^ mask) for i in range(size)])  182 us
    pallas_call x12, Pallas kernels, call(): pl.pallas_call(kernel, out_shape=out_shape, in_specs=[SM] * smem + [VM] *...  94.7 us
    ppermute x35, starting transfers between devices, swap(): return lax.ppermute(value, axis, [(i, i ^ mask) for i in range(size)])  36.7 us
    convert_element_type x1, other arithmetic, shards(): grad_passages = (grad_p * factor).astype(bf16).reshape(flat)  7.77 us
    reduce_sum x2, other arithmetic, shards(): squares = jnp.sum(grad_q * grad_q) + jnp.sum(grad_p * grad_p)  7.25 us
  transfers between devices with their start and end apart: 35, of which 18 were waited for; matrix products, arithmetic and copies ran while one was open for 3% of the time, Pallas kernels for 23%

profile of v1, /device:TPU:0, one launch (start us, length us, event | category | flops | bytes accessed | tf_op | source)
XLA Modules:
  0.0 349.9 jit_solution(11770972747234972377)
XLA Ops:
  0.6 4.1 %collective-permute-start.4 = (bf16[7,128,1024]{2,1,0:T(8,128)(2,1)}, bf16[7,128,1024]{2,1,0:T(8,128)(2,1)S(1)}, u32[]{:S(2)}, u32[]{:S(2)}) collective-permute-start(bf16[7,128,1024]{2,1,0:T(8,128)(2,1)} %bitcast.57), channel_id=1, source_target_pairs={{0,16},{4,20},{8,24},{12,28},{16,0},{20,4},{24,8},{28,12},{1,17},{... | collective-permute-start | bytes 5505032 | tf_op jit(solution)/shard_map/ppermute | solution.py:29
  9.0 75.5 %collective-permute-done = s32[7,8]{1,0:T(8,128)S(1)} collective-permute-done((s32[7,8]{1,0:T(8,128)}, s32[7,8]{1,0:T(8,128)S(1)}, u32[]{:S(2)}, u32[]{:S(2)}) %collective-permute-start) | collective-permute-done | bytes 256 | tf_op jit(solution)/shard_map/ppermute | solution.py:29
  87.2 6.9 %shard_map.60 = (f32[2,14,32,128]{3,2,1,0:T(8,128)}, f32[2,14,32,128]{3,2,1,0:T(8,128)}) custom-call(s32[2,28]{1,0:T(2,128)} %copy.12.tab, s32[1]{0:T(128)} %bitcast.rank, bf16[7,128,1024]{2,1,0:T(8,128)(2,1)} %bitcast.58, bf16[7,128,1024]{2,1,0:T(8,128)(2,1)} %copy-done, bf16[7,128,1024]{2,1,0:T(8,128)(2,1)} %collective-permute-done.2.keys.refs_2_), custom_call_target="tpu_custom_call" | custom-call | flops 469762048 | bytes 5505024 | tf_op jit(solution)/shard_map/pallas_call | solution.py:33
  95.7 8.7 %shard_map.58 = (f32[2,21,32,128]{3,2,1,0:T(8,128)}, f32[2,21,32,128]{3,2,1,0:T(8,128)}) custom-call(s32[2,28]{1,0:T(2,128)} %copy.12.tab, s32[1]{0:T(128)} %bitcast.rank, bf16[7,128,1024]{2,1,0:T(8,128)(2,1)} %bitcast.59, bf16[7,128,1024]{2,1,0:T(8,128)(2,1)} %copy-done, bf16[7,128,1024]{2,1,0:T(8,128)(2,1)} %bitcast.68), custom_call_target="tpu_custom_call" | custom-call | flops 704643072 | bytes 5505024 | tf_op jit(solution)/shard_map/pallas_call | solution.py:33
  104.6 6.8 %shard_map.59 = (f32[2,14,32,128]{3,2,1,0:T(8,128)}, f32[2,14,32,128]{3,2,1,0:T(8,128)}) custom-call(s32[2,28]{1,0:T(2,128)} %copy.12.tab, s32[1]{0:T(128)} %bitcast.rank, bf16[7,128,1024]{2,1,0:T(8,128)(2,1)} %bitcast.60, bf16[7,128,1024]{2,1,0:T(8,128)(2,1)} %copy-done, bf16[7,128,1024]{2,1,0:T(8,128)(2,1)} %collective-permute-done.1.keys.refs_1_), custom_call_target="tpu_custom_call" | custom-call | flops 469762048 | bytes 5505024 | tf_op jit(solution)/shard_map/pallas_call | solution.py:33
  111.8 1.8 collective-permute-start.10
  116.0 20.7 %collective-permute-done.3.keys.refs_3_ = bf16[7,128,1024]{2,1,0:T(8,128)(2,1)S(1)} collective-permute-done((bf16[7,128,1024]{2,1,0:T(8,128)(2,1)}, bf16[7,128,1024]{2,1,0:T(8,128)(2,1)S(1)}, u32[]{:S(2)}, u32[]{:S(2)}) %collective-permute-start.3) | collective-permute-done | bytes 1835040 | tf_op jit(solution)/shard_map/ppermute | solution.py:29
  138.0 6.9 %shard_map.61 = (f32[2,14,32,128]{3,2,1,0:T(8,128)}, f32[2,14,32,128]{3,2,1,0:T(8,128)}) custom-call(s32[2,28]{1,0:T(2,128)} %copy.12.tab, s32[1]{0:T(128)} %bitcast.rank, bf16[7,128,1024]{2,1,0:T(8,128)(2,1)} %bitcast.61, bf16[7,128,1024]{2,1,0:T(8,128)(2,1)} %copy-done, bf16[7,128,1024]{2,1,0:T(8,128)(2,1)} %copy-done.2), custom_call_target="tpu_custom_call" | custom-call | flops 469762048 | bytes 5505024 | tf_op jit(solution)/shard_map/pallas_call | solution.py:33
  150.5 5.2 %collective-permute-done.12 = f32[1,14,32,128]{3,2,1,0:T(8,128)S(1)} collective-permute-done((f32[1,14,32,128]{3,2,1,0:T(8,128)S(1)}, f32[1,14,32,128]{3,2,1,0:T(8,128)S(1)}, u32[]{:S(2)}, u32[]{:S(2)}) %collective-permute-start.12) | collective-permute-done | bytes 229408 | tf_op jit(solution)/shard_map/ppermute | solution.py:29
  156.4 3.6 %shard_map.62.refs_4_ = f32[32,128]{1,0:T(8,128)} custom-call(s32[2,28]{1,0:T(2,128)} %copy.12.tab, f32[21,32,128]{2,1,0:T(8,128)} %fusion.1.refs_0_, f32[14,32,128]{2,1,0:T(8,128)} %fusion.7.refs_1_, f32[14,32,128]{2,1,0:T(8,128)} %fusion.5.refs_2_, f32[14,32,128]{2,1,0:T(8,128)} %fusion.3.refs_3_), custom_call_target="tpu_custom_call" | custom-call | bytes 2097152 | tf_op jit(solution)/shard_map/pallas_call | solution.py:33
  160.0 2.6 collective-permute-start.13
  162.7 2.2 collective-permute-done.13.refs_5_
  165.5 4.0 %shard_map.63 = (bf16[21,32,128]{2,1,0:T(8,128)(2,1)}, bf16[14,32,128]{2,1,0:T(8,128)(2,1)}, bf16[14,32,128]{2,1,0:T(8,128)(2,1)}, bf16[14,32,128]{2,1,0:T(8,128)(2,1)}, f32[32,128]{1,0:T(8,128)}) custom-call(s32[2,28]{1,0:T(2,128)} %copy.12.tab, s32[1]{0:T(128)} %bitcast.rank, f32[21,32,128]{2,1,0:T(8,128)} %fusion.1.refs_0_, ...), custom_call_target="tpu_custom_call" | custom-call | bytes 2097152 | tf_op jit(solution)/shard_map/pallas_call | solution.py:33
  171.2 3.3 collective-permute-done.23.refs_17_.refs_1_
  176.5 7.5 %shard_map.68 = bf16[7,128,1024]{2,1,0:T(8,128)(2,1)} custom-call(s32[2,28]{1,0:T(2,128)} %copy.12.tab, s32[1]{0:T(128)} %bitcast.rank, bf16[7,128,1024]{2,1,0:T(8,128)(2,1)} %bitcast.62, bf16[7,128,1024]{2,1,0:T(8,128)(2,1)} %copy-done, bf16[14,32,128]{2,1,0:T(8,128)(2,1)} %get-tuple-element.27.refs_16_.refs_0_, bf16[14,32,128]{2,1,0:T(8,128)(2,1)} %copy-done.13, ...), custom_call_target="tpu_custom_call" | custom-call | flops 469762048 | bytes 7340032 | tf_op jit(solution)/shard_map/pallas_call | solution.py:33
  189.4 5.9 %collective-permute-done.17.refs_9_.refs_1_ = bf16[14,32,128]{2,1,0:T(8,128)(2,1)S(1)} collective-permute-done((bf16[14,32,128]{2,1,0:T(8,128)(2,1)S(1)}, bf16[14,32,128]{2,1,0:T(8,128)(2,1)S(1)}, u32[]{:S(2)}, u32[]{:S(2)}) %collective-permute-start.17) | collective-permute-done | bytes 114720 | tf_op jit(solution)/shard_map/ppermute | solution.py:29
  199.9 11.5 %shard_map.65 = bf16[7,128,1024]{2,1,0:T(8,128)(2,1)} custom-call(s32[2,28]{1,0:T(2,128)} %copy.12.tab, s32[1]{0:T(128)} %bitcast.rank, bf16[7,128,1024]{2,1,0:T(8,128)(2,1)} %bitcast.69, bf16[7,128,1024]{2,1,0:T(8,128)(2,1)} %collective-permute-done.1.keys.refs_1_, bf16[7,128,1024]{2,1,0:T(8,128)(2,1)} %collective-permute-done.2.keys.refs_2_, ...), custom_call_target="tpu_custom_call" | custom-call | flops 939524096 | bytes 11010048 | tf_op jit(solution)/shard_map/pallas_call | solution.py:33
  211.4 2.7 collective-permute-start.26
  214.1 7.4 %shard_map.67 = bf16[7,128,1024]{2,1,0:T(8,128)(2,1)} custom-call(s32[2,28]{1,0:T(2,128)} %copy.12.tab, s32[1]{0:T(128)} %bitcast.rank, bf16[7,128,1024]{2,1,0:T(8,128)(2,1)} %bitcast.63, bf16[7,128,1024]{2,1,0:T(8,128)(2,1)} %copy-done, bf16[14,32,128]{2,1,0:T(8,128)(2,1)} %get-tuple-element.25.refs_8_.refs_0_, bf16[14,32,128]{2,1,0:T(8,128)(2,1)} %copy-done.17, ...), custom_call_target="tpu_custom_call" | custom-call | flops 469762048 | bytes 7340032 | tf_op jit(solution)/shard_map/pallas_call | solution.py:33
  222.0 5.0 %collective-permute-done.28.refs_4_ = bf16[7,128,1024]{2,1,0:T(8,128)(2,1)S(1)} collective-permute-done((bf16[7,128,1024]{2,1,0:T(8,128)(2,1)}, bf16[7,128,1024]{2,1,0:T(8,128)(2,1)S(1)}, u32[]{:S(2)}, u32[]{:S(2)}) %collective-permute-start.28) | collective-permute-done | bytes 1835040 | tf_op jit(solution)/shard_map/ppermute | solution.py:29
  228.3 8.2 %shard_map.69 = bf16[7,128,1024]{2,1,0:T(8,128)(2,1)} custom-call(s32[2,28]{1,0:T(2,128)} %copy.12.tab, s32[1]{0:T(128)} %bitcast.rank, bf16[7,128,1024]{2,1,0:T(8,128)(2,1)} %bitcast.64, bf16[7,128,1024]{2,1,0:T(8,128)(2,1)} %copy-done, bf16[14,32,128]{2,1,0:T(8,128)(2,1)} %get-tuple-element.26.refs_12_.refs_0_, bf16[14,32,128]{2,1,0:T(8,128)(2,1)} %copy-done.10, ...), custom_call_target="tpu_custom_call" | custom-call | flops 469762048 | bytes 7340032 | tf_op jit(solution)/shard_map/pallas_call | solution.py:33
  238.7 9.7 %shard_map.66 = f32[7,128,1024]{2,1,0:T(8,128)} custom-call(s32[2,28]{1,0:T(2,128)} %copy.12.tab, s32[1]{0:T(128)} %bitcast.rank, bf16[7,128,1024]{2,1,0:T(8,128)(2,1)} %bitcast.65, bf16[7,128,1024]{2,1,0:T(8,128)(2,1)} %copy-done, bf16[21,32,128]{2,1,0:T(8,128)(2,1)} %get-tuple-element.24.refs_4_.refs_0_, bf16[21,32,128]{2,1,0:T(8,128)(2,1)} %copy-done.5, ...), custom_call_target="tpu_custom_call" | custom-call | flops 704643072 | bytes 7340032 | tf_op jit(solution)/shard_map/pallas_call | solution.py:33
  248.4 13.6 %shard_map.64 = f32[7,128,1024]{2,1,0:T(8,128)} custom-call(s32[2,28]{1,0:T(2,128)} %copy.12.tab, s32[1]{0:T(128)} %bitcast.rank, bf16[7,128,1024]{2,1,0:T(8,128)(2,1)} %bitcast.70, bf16[7,128,1024]{2,1,0:T(8,128)(2,1)} %collective-permute-done.1.keys.refs_1_, bf16[7,128,1024]{2,1,0:T(8,128)(2,1)} %collective-permute-done.2.keys.refs_2_, ...), custom_call_target="tpu_custom_call" | custom-call | flops 939524096 | bytes 11010048 | tf_op jit(solution)/shard_map/pallas_call | solution.py:33
  262.0 32.1 %collective-permute-done.26 = bf16[7,128,1024]{2,1,0:T(8,128)(2,1)S(1)} collective-permute-done((bf16[7,128,1024]{2,1,0:T(8,128)(2,1)}, bf16[7,128,1024]{2,1,0:T(8,128)(2,1)S(1)}, u32[]{:S(2)}, u32[]{:S(2)}) %collective-permute-start.26) | collective-permute-done | bytes 1835040 | tf_op jit(solution)/shard_map/ppermute | solution.py:29
  294.0 3.6 %multiply_reduce_fusion.1 = f32[]{:T(128)} fusion(f32[7,128,1024]{2,1,0:T(8,128)} %shard_map.64, bf16[7,128,1024]{2,1,0:T(8,128)(2,1)S(1)} %collective-permute-done.26), kind=kLoop, calls=%fused_computation.4 | loop fusion | flops 3670015 | bytes 5505028 | tf_op jit(solution)/shard_map/reduce_sum | solution.py:319
  297.6 17.9 %collective-permute-done.29 = bf16[7,128,1024]{2,1,0:T(8,128)(2,1)} collective-permute-done((bf16[7,128,1024]{2,1,0:T(8,128)(2,1)}, bf16[7,128,1024]{2,1,0:T(8,128)(2,1)}, u32[]{:S(2)}, u32[]{:S(2)}) %collective-permute-start.29) | collective-permute-done | bytes 1835040 | tf_op jit(solution)/shard_map/ppermute | solution.py:29
  315.6 3.7 %multiply_reduce_fusion = f32[]{:T(128)} fusion(bf16[7,128,1024]{2,1,0:T(8,128)(2,1)} %collective-permute-done.29, f32[7,128,1024]{2,1,0:T(8,128)S(1)} %copy-done.1, bf16[7,128,1024]{2,1,0:T(8,128)(2,1)} %collective-permute-done.27), kind=kLoop, calls=%fused_computation.2 | loop fusion | flops 5505023 | bytes 7340036 | tf_op jit(solution)/shard_map/reduce_sum | solution.py:319
  324.8 1.9 collective-permute-done.31
  328.9 2.0 collective-permute-done.32
  330.9 3.5 %collective-permute-done.33 = f32[2]{0:T(128)S(1)} collective-permute-done((f32[2]{0:T(128)S(1)}, f32[2]{0:T(128)S(1)}, u32[]{:S(2)}, u32[]{:S(2)}) %collective-permute-start.33) | collective-permute-done | bytes 40 | tf_op jit(solution)/shard_map/ppermute | solution.py:29
  334.4 3.1 collective-permute-start.34
  341.0 7.8 %multiply_convert_fusion = (bf16[7,128,1024]{2,1,0:T(8,128)(2,1)}, bf16[7,128,1024]{2,1,0:T(8,128)(2,1)}) fusion(f32[]{:T(128)} %bitcast.21, bf16[7,128,1024]{2,1,0:T(8,128)(2,1)} %collective-permute-done.29, f32[7,128,1024]{2,1,0:T(8,128)} %shard_map.66, bf16[7,128,1024]{2,1,0:T(8,128)(2,1)} %collective-permute-done.27, f32[7,128,1024]{2,1,0:T(8,128)} %shard_map.64, ...), kind=kLoop, calls=%fused_computation | loop fusion | flops 9175040 | bytes 16515076 | tf_op jit(solution)/shard_map/convert_element_type | solution.py:330
  (130 shorter events, 45.9 us)
Async XLA Ops:
  0.6 85.4 %collective-permute-start.4 = (bf16[7,128,1024]{2,1,0:T(8,128)(2,1)}, bf16[7,128,1024]{2,1,0:T(8,128)(2,1)S(1)}, u32[]{:S(2)}, u32[]{:S(2)}) collective-permute-start(bf16[7,128,1024]{2,1,0:T(8,128)(2,1)} %bitcast.57), channel_id=1, source_target_pairs={{0,16},{4,20},{8,24},{12,28},{16,0},{20,4},{24,8},{28,12},{1,17},{... | collective-permute-start | bytes 5505032 | tf_op jit(solution)/shard_map/ppermute | solution.py:29
  4.7 81.3 %collective-permute-start.2 = (bf16[7,128,1024]{2,1,0:T(8,128)(2,1)}, bf16[7,128,1024]{2,1,0:T(8,128)(2,1)}, u32[]{:S(2)}, u32[]{:S(2)}) collective-permute-start(bf16[7,128,1024]{2,1,0:T(8,128)(2,1)} %bitcast.66), channel_id=1, source_target_pairs={{0,8},{4,12},{8,0},{12,4},{16,24},{20,28},{24,16},{28,20},{1,9},{5... | collective-permute-start | bytes 5505032 | tf_op jit(solution)/shard_map/ppermute | solution.py:29
  6.3 98.2 %collective-permute-start.1 = (bf16[7,128,1024]{2,1,0:T(8,128)(2,1)}, bf16[7,128,1024]{2,1,0:T(8,128)(2,1)}, u32[]{:S(2)}, u32[]{:S(2)}) collective-permute-start(bf16[7,128,1024]{2,1,0:T(8,128)(2,1)} %bitcast.67), channel_id=1, source_target_pairs={{0,4},{4,0},{8,12},{12,8},{16,20},{20,16},{24,28},{28,24},{1,5},{5... | collective-permute-start | bytes 5505032 | tf_op jit(solution)/shard_map/ppermute | solution.py:29
  7.8 76.7 %collective-permute-start = (s32[7,8]{1,0:T(8,128)}, s32[7,8]{1,0:T(8,128)S(1)}, u32[]{:S(2)}, u32[]{:S(2)}) collective-permute-start(s32[7,8]{1,0:T(8,128)} %param.5), channel_id=1, source_target_pairs={{0,16},{4,20},{8,24},{12,28},{16,0},{20,4},{24,8},{28,12},{1,17},{... | collective-permute-start | bytes 680 | tf_op jit(solution)/shard_map/ppermute | solution.py:29
  94.1 17.6 %collective-permute-start.9 = (f32[2,14,32,128]{3,2,1,0:T(8,128)}, f32[2,14,32,128]{3,2,1,0:T(8,128)S(1)}, u32[]{:S(2)}, u32[]{:S(2)}) collective-permute-start(f32[2,14,32,128]{3,2,1,0:T(8,128)} %get-tuple-element.21), channel_id=1, source_target_pairs={{0,1},{1,0},{2,3},{3,2},{4,5},{5,4},{6,7},{7,6},{8,9},{9,8},{10,11... | collective-permute-start | bytes 1376264 | tf_op jit(solution)/shard_map/ppermute | solution.py:29
  94.1 42.6 %collective-permute-start.3 = (bf16[7,128,1024]{2,1,0:T(8,128)(2,1)}, bf16[7,128,1024]{2,1,0:T(8,128)(2,1)S(1)}, u32[]{:S(2)}, u32[]{:S(2)}) collective-permute-start(bf16[7,128,1024]{2,1,0:T(8,128)(2,1)} %collective-permute-done.2.keys.refs_2_), channel_id=1, source_target_pairs={{0,4},{4,0},{8,12},{12,8},{16,20},{20,16},{24,28},{28,24},{1,5},{5... | collective-permute-start | bytes 5505032 | tf_op jit(solution)/shard_map/ppermute | solution.py:29
  104.3 11.1 %collective-permute-start.5 = (f32[2,21,32,128]{3,2,1,0:T(8,128)}, f32[2,21,32,128]{3,2,1,0:T(8,128)S(1)}, u32[]{:S(2)}, u32[]{:S(2)}) collective-permute-start(f32[2,21,32,128]{3,2,1,0:T(8,128)} %get-tuple-element.17), channel_id=1, source_target_pairs={{0,1},{1,0},{2,3},{3,2},{4,5},{5,4},{6,7},{7,6},{8,9},{9,8},{10,11... | collective-permute-start | bytes 2064392 | tf_op jit(solution)/shard_map/ppermute | solution.py:29
  111.4 2.2 collective-permute-start.7
  111.8 33.0 %collective-permute-start.10 = (f32[1,14,32,128]{3,2,1,0:T(8,128)S(1)}, f32[1,14,32,128]{3,2,1,0:T(8,128)S(1)}, u32[]{:S(2)}, u32[]{:S(2)}) collective-permute-start(f32[1,14,32,128]{3,2,1,0:T(8,128)S(1)} %slice_bitcast_fusion.4), channel_id=1, source_target_pairs={{0,2},{1,3},{2,0},{3,1},{4,6},{5,7},{6,4},{7,5},{8,10},{9,11},{10,... | collective-permute-start | bytes 688136 | tf_op jit(solution)/shard_map/ppermute | solution.py:29
  113.7 31.9 %collective-permute-start.8 = (f32[1,14,32,128]{3,2,1,0:T(8,128)S(1)}, f32[1,14,32,128]{3,2,1,0:T(8,128)S(1)}, u32[]{:S(2)}, u32[]{:S(2)}) collective-permute-start(f32[1,14,32,128]{3,2,1,0:T(8,128)S(1)} %slice_bitcast_fusion.6), channel_id=1, source_target_pairs={{0,2},{1,3},{2,0},{3,1},{4,6},{5,7},{6,4},{7,5},{8,10},{9,11},{10,... | collective-permute-start | bytes 688136 | tf_op jit(solution)/shard_map/ppermute | solution.py:29
  115.6 34.2 %collective-permute-start.6 = (f32[1,21,32,128]{3,2,1,0:T(8,128)S(1)}, f32[1,21,32,128]{3,2,1,0:T(8,128)S(1)}, u32[]{:S(2)}, u32[]{:S(2)}) collective-permute-start(f32[1,21,32,128]{3,2,1,0:T(8,128)S(1)} %slice_bitcast_fusion), channel_id=1, source_target_pairs={{0,2},{1,3},{2,0},{3,1},{4,6},{5,7},{6,4},{7,5},{8,10},{9,11},{10,... | collective-permute-start | bytes 1032200 | tf_op jit(solution)/shard_map/ppermute | solution.py:29
  144.8 2.0 collective-permute-start.11
  148.0 7.7 %collective-permute-start.12 = (f32[1,14,32,128]{3,2,1,0:T(8,128)S(1)}, f32[1,14,32,128]{3,2,1,0:T(8,128)S(1)}, u32[]{:S(2)}, u32[]{:S(2)}) collective-permute-start(f32[1,14,32,128]{3,2,1,0:T(8,128)S(1)} %slice_bitcast_fusion.2), channel_id=1, source_target_pairs={{0,2},{1,3},{2,0},{3,1},{4,6},{5,7},{6,4},{7,5},{8,10},{9,11},{10,... | collective-permute-start | bytes 688136 | tf_op jit(solution)/shard_map/ppermute | solution.py:29
  160.0 4.8 %collective-permute-start.13 = (f32[32,128]{1,0:T(8,128)}, f32[32,128]{1,0:T(8,128)S(1)}, u32[]{:S(2)}, u32[]{:S(2)}) collective-permute-start(f32[32,128]{1,0:T(8,128)} %shard_map.62.refs_4_), channel_id=1, source_target_pairs={{0,16},{4,20},{8,24},{12,28},{16,0},{20,4},{24,8},{28,12},{1,17},{... | collective-permute-start | bytes 49160 | tf_op jit(solution)/shard_map/ppermute | solution.py:29
  169.5 5.1 %collective-permute-start.23 = (bf16[14,32,128]{2,1,0:T(8,128)(2,1)}, bf16[14,32,128]{2,1,0:T(8,128)(2,1)S(1)}, u32[]{:S(2)}, u32[]{:S(2)}) collective-permute-start(bf16[14,32,128]{2,1,0:T(8,128)(2,1)} %get-tuple-element.27.refs_16_.refs_0_), channel_id=1, source_target_pairs={{0,2},{1,3},{2,0},{3,1},{4,6},{5,7},{6,4},{7,5},{8,10},{9,11},{10,... | collective-permute-start | bytes 344072 | tf_op jit(solution)/shard_map/ppermute | solution.py:29
  171.2 3.3 collective-permute-start.24
  184.0 43.1 %collective-permute-start.28 = (bf16[7,128,1024]{2,1,0:T(8,128)(2,1)}, bf16[7,128,1024]{2,1,0:T(8,128)(2,1)S(1)}, u32[]{:S(2)}, u32[]{:S(2)}) collective-permute-start(bf16[7,128,1024]{2,1,0:T(8,128)(2,1)} %shard_map.68), channel_id=1, source_target_pairs={{0,4},{4,0},{8,12},{12,8},{16,20},{20,16},{24,28},{28,24},{1,5},{5... | collective-permute-start | bytes 5505032 | tf_op jit(solution)/shard_map/ppermute | solution.py:29
  185.6 2.1 collective-permute-start.18
  185.6 9.7 %collective-permute-start.14 = (bf16[21,32,128]{2,1,0:T(8,128)(2,1)S(1)}, bf16[21,32,128]{2,1,0:T(8,128)(2,1)S(1)}, u32[]{:S(2)}, u32[]{:S(2)}) collective-permute-start(bf16[21,32,128]{2,1,0:T(8,128)(2,1)S(1)} %copy-done.4), channel_id=1, source_target_pairs={{0,2},{1,3},{2,0},{3,1},{4,6},{5,7},{6,4},{7,5},{8,10},{9,11},{10,... | collective-permute-start | bytes 516104 | tf_op jit(solution)/shard_map/ppermute | solution.py:29
  187.3 8.0 %collective-permute-start.17 = (bf16[14,32,128]{2,1,0:T(8,128)(2,1)S(1)}, bf16[14,32,128]{2,1,0:T(8,128)(2,1)S(1)}, u32[]{:S(2)}, u32[]{:S(2)}) collective-permute-start(bf16[14,32,128]{2,1,0:T(8,128)(2,1)S(1)} %copy-done.12), channel_id=1, source_target_pairs={{0,2},{1,3},{2,0},{3,1},{4,6},{5,7},{6,4},{7,5},{8,10},{9,11},{10,... | collective-permute-start | bytes 344072 | tf_op jit(solution)/shard_map/ppermute | solution.py:29
  187.7 8.1 %collective-permute-start.21 = (bf16[14,32,128]{2,1,0:T(8,128)(2,1)S(1)}, bf16[14,32,128]{2,1,0:T(8,128)(2,1)S(1)}, u32[]{:S(2)}, u32[]{:S(2)}) collective-permute-start(bf16[14,32,128]{2,1,0:T(8,128)(2,1)S(1)} %copy-done.8), channel_id=1, source_target_pairs={{0,1},{1,0},{2,3},{3,2},{4,5},{5,4},{6,7},{7,6},{8,9},{9,8},{10,11... | collective-permute-start | bytes 344072 | tf_op jit(solution)/shard_map/ppermute | solution.py:29
  187.7 9.6 %collective-permute-start.20 = (bf16[14,32,128]{2,1,0:T(8,128)(2,1)S(1)}, bf16[14,32,128]{2,1,0:T(8,128)(2,1)S(1)}, u32[]{:S(2)}, u32[]{:S(2)}) collective-permute-start(bf16[14,32,128]{2,1,0:T(8,128)(2,1)S(1)} %copy-done.8), channel_id=1, source_target_pairs={{0,2},{1,3},{2,0},{3,1},{4,6},{5,7},{6,4},{7,5},{8,10},{9,11},{10,... | collective-permute-start | bytes 344072 | tf_op jit(solution)/shard_map/ppermute | solution.py:29
  195.3 2.0 collective-permute-start.15
  195.3 3.3 collective-permute-start.16
  195.8 1.5 collective-permute-start.19
  211.4 82.6 %collective-permute-start.26 = (bf16[7,128,1024]{2,1,0:T(8,128)(2,1)}, bf16[7,128,1024]{2,1,0:T(8,128)(2,1)S(1)}, u32[]{:S(2)}, u32[]{:S(2)}) collective-permute-start(bf16[7,128,1024]{2,1,0:T(8,128)(2,1)} %shard_map.65), channel_id=1, source_target_pairs={{0,16},{4,20},{8,24},{12,28},{16,0},{20,4},{24,8},{28,12},{1,17},{... | collective-permute-start | bytes 5505032 | tf_op jit(solution)/shard_map/ppermute | solution.py:29
  221.5 76.1 %collective-permute-start.27 = (bf16[7,128,1024]{2,1,0:T(8,128)(2,1)}, bf16[7,128,1024]{2,1,0:T(8,128)(2,1)}, u32[]{:S(2)}, u32[]{:S(2)}) collective-permute-start(bf16[7,128,1024]{2,1,0:T(8,128)(2,1)} %shard_map.67), channel_id=1, source_target_pairs={{0,4},{4,0},{8,12},{12,8},{16,20},{20,16},{24,28},{28,24},{1,5},{5... | collective-permute-start | bytes 5505032 | tf_op jit(solution)/shard_map/ppermute | solution.py:29
  236.5 79.1 %collective-permute-start.29 = (bf16[7,128,1024]{2,1,0:T(8,128)(2,1)}, bf16[7,128,1024]{2,1,0:T(8,128)(2,1)}, u32[]{:S(2)}, u32[]{:S(2)}) collective-permute-start(bf16[7,128,1024]{2,1,0:T(8,128)(2,1)} %shard_map.69), channel_id=1, source_target_pairs={{0,8},{4,12},{8,0},{12,4},{16,24},{20,28},{24,16},{28,20},{1,9},{5... | collective-permute-start | bytes 5505032 | tf_op jit(solution)/shard_map/ppermute | solution.py:29
  323.1 3.5 %collective-permute-start.31 = (f32[2]{0:T(128)S(1)}, f32[2]{0:T(128)S(1)}, u32[]{:S(2)}, u32[]{:S(2)}) collective-permute-start(f32[2]{0:T(128)S(1)} %fusion.13), channel_id=1, source_target_pairs={{0,2},{1,3},{2,0},{3,1},{4,6},{5,7},{6,4},{7,5},{8,10},{9,11},{10,... | collective-permute-start | bytes 32 | tf_op jit(solution)/shard_map/ppermute | solution.py:29
  327.3 3.5 %collective-permute-start.32 = (f32[2]{0:T(128)S(1)}, f32[2]{0:T(128)S(1)}, u32[]{:S(2)}, u32[]{:S(2)}) collective-permute-start(f32[2]{0:T(128)S(1)} %fusion.14), channel_id=1, source_target_pairs={{0,4},{4,0},{8,12},{12,8},{16,20},{20,16},{24,28},{28,24},{1,5},{5... | collective-permute-start | bytes 32 | tf_op jit(solution)/shard_map/ppermute | solution.py:29
  330.9 3.5 %collective-permute-start.33 = (f32[2]{0:T(128)S(1)}, f32[2]{0:T(128)S(1)}, u32[]{:S(2)}, u32[]{:S(2)}) collective-permute-start(f32[2]{0:T(128)S(1)} %add.132), channel_id=1, source_target_pairs={{0,8},{4,12},{8,0},{12,4},{16,24},{20,28},{24,16},{28,20},{1,9},{5... | collective-permute-start | bytes 32 | tf_op jit(solution)/shard_map/ppermute | solution.py:29
  334.4 4.6 %collective-permute-start.34 = (f32[2]{0:T(128)S(1)}, f32[2]{0:T(128)S(1)}, u32[]{:S(2)}, u32[]{:S(2)}) collective-permute-start(f32[2]{0:T(128)S(1)} %add.133), channel_id=1, source_target_pairs={{0,16},{4,20},{8,24},{12,28},{16,0},{20,4},{24,8},{28,12},{1,17},{... | collective-permute-start | bytes 32 | tf_op jit(solution)/shard_map/ppermute | solution.py:29
  (27 other events, 171.1 us)

commit v2 on v1

v2 whole, which is shorter than its diff:
```python
import functools

import jax
import jax.numpy as jnp
from jax import lax
from jax.experimental import pallas as pl
from jax.experimental.pallas import tpu as pltpu
from jax.sharding import PartitionSpec as P

CLUSTER = 128
PARTNERS = 8
LOW = -3.0e38
VALID = 1 << 16
VMEM_LIMIT = 56 * 1024 * 1024
SLACK = 4 * 1024 * 1024
COST = 1000

VM = pl.BlockSpec(memory_space=pltpu.VMEM)
SM = pl.BlockSpec(memory_space=pltpu.SMEM)
ANY = pl.BlockSpec(memory_space=pl.ANY)
NT = (((1,), (1,)), ((), ()))
TN = (((0,), (0,)), ((), ()))
NN = (((1,), (0,)), ((), ()))


def bits_of(size):
    return size.bit_length() - 1


def swap(value, axis, mask):
    size = lax.axis_size(axis)
    return lax.ppermute(value, axis, [(i, i ^ mask) for i in range(size)])


def size_of(shape):
    return shape.size * shape.dtype.itemsize


def call(name, kernel, out_shape, scratch, flops, args, smem, waits=()):
    outs = jax.tree.leaves(out_shape)
    moved = sum(size_of(a) for a in args[smem:]) + sum(size_of(o) for o in outs)
    held = moved + sum(size_of(jax.ShapeDtypeStruct(x.shape, x.dtype)) for x in scratch)

    def body(*refs):
        kernel(*refs[: len(args)], *refs[len(args) + len(waits) :])

    return pl.pallas_call(
        body,
        name=name,
        out_shape=out_shape,
        in_specs=[SM] * smem + [VM] * (len(args) - smem) + [ANY] * len(waits),
        out_specs=jax.tree.map(lambda _: VM, out_shape),
        scratch_shapes=scratch,
        compiler_params=pltpu.CompilerParams(vmem_limit_bytes=min(held + SLACK, VMEM_LIMIT)),
        cost_estimate=pl.CostEstimate(flops=flops // COST, bytes_accessed=moved // COST, transcendentals=0),
    )(*args, *waits)


def unpack(code):
    return code >= VALID, (code >> 8) & 255, code & 255


def layout(parts, clusters, cap):
    plans = [
        [(m, 0) for m in range(min(parts, 2))],
        [(m, 1) for m in range(min(parts, 2))] + [(2, r) for r in (0, 1) if parts > 2],
        [(m, r) for m in range(3, parts) for r in (0, 1)],
    ]
    chunks = []
    for plan in plans:
        groups, first = [], clusters if (0, 0) in plan else 0
        for mask, requester in plan:
            groups.append((mask, requester, first))
            first += cap
        if groups:
            chunks.append((tuple(groups), first))
    return tuple(chunks)


def share_rows(me, at, share):
    return pl.ds(pl.multiple_of((me ^ at) * share, share), share)


def rows_of(ref, c, me, ways, cut=slice(None)):
    share = CLUSTER // ways
    blocks = [ref[c, share_rows(me, at, share), cut] for at in range(ways)]
    return jnp.concatenate(blocks, axis=0)


def logits_kernel(groups, splits, clusters, cap, ways, tab_a, tab_b, rank, *refs):
    tab = (tab_a, tab_b)
    share = CLUSTER // ways
    me = rank[0]
    askers = sorted({r for _, r, _ in groups})
    rows = dict(zip(askers, refs))
    at_ref, keys = len(askers), {}
    for m, split in splits:
        keys[m] = refs[at_ref : at_ref + split]
        at_ref += split
    low, high, done = refs[at_ref:]
    done[...] = jnp.zeros_like(done)

    def one(row_ref, c, mask, e, slot):
        row = rows_of(row_ref, c, me, ways)
        wide = keys[mask][0].shape[-1]
        block = None
        for i, key in enumerate(keys[mask]):
            part = lax.dot_general(
                row[:, i * wide : (i + 1) * wide], key[e], NT, preferred_element_type=jnp.float32
            )
            block = part if block is None else block + part
        for at in range(ways):
            (high if at % 2 else low)[at // 2, slot] = block[at * share : (at + 1) * share]

    if any(first and (mask, r) == (0, 0) for mask, r, first in groups):

        @pl.loop(0, clusters)
        def _(c):
            one(rows[0], c, 0, c, c)

    @pl.loop(0, cap)
    def _(j):
        for mask, requester, first in groups:
            _, c, e = unpack(tab[requester][mask * cap + j])
            one(rows[requester], c, mask, e, first + j)


def each_slot(visit, chunks, plans, clusters, cap, tab):
    for n, (groups, _) in enumerate(plans):
        if any(first and (mask, r) == (0, 0) for mask, r, first in groups):
            for c in range(clusters):
                visit(n, chunks[n], c, c, None)

        @pl.loop(0, cap)
        def _(j):
            for mask, requester, first in groups:
                ok, c, _ = unpack(tab[requester][mask * cap + j])
                at = jnp.where(ok, requester * clusters + c, 2 * clusters)
                visit(n, chunks[n], first + j, at, ok)


def stats_kernel(plans, clusters, cap, scale, tab_a, tab_b, *refs):
    tab = (tab_a, tab_b)
    parts = len(plans)
    chunks, stats, top, total = refs[:parts], refs[parts], refs[parts + 1], refs[parts + 2]
    top[...] = jnp.full_like(top, LOW)
    total[...] = jnp.zeros_like(total)

    def raise_top(n, ref, slot, at, ok):
        top[at] = jnp.maximum(top[at], ref[slot] * scale)

    each_slot(raise_top, chunks, plans, clusters, cap, tab)
    for c in range(2 * clusters + 1):
        top[c] = jnp.broadcast_to(jnp.max(top[c], axis=-1, keepdims=True), top.shape[1:])

    def add_total(n, ref, slot, at, ok):
        total[at] = total[at] + jnp.exp(ref[slot] * scale - top[at])

    each_slot(add_total, chunks, plans, clusters, cap, tab)
    lane = lax.broadcasted_iota(jnp.int32, stats.shape, 1)
    out = jnp.zeros(stats.shape, jnp.float32)
    for c in range(2 * clusters):
        out = jnp.where(lane == c, top[c], out)
        sums = jnp.sum(total[c], axis=-1, keepdims=True)
        out = jnp.where(lane == 2 * clusters + c, sums, out)
    stats[...] = out


def weights_kernel(plans, clusters, cap, scale, tab_a, tab_b, rank, here, there, *refs):
    tab = (tab_a, tab_b)
    parts = len(plans)
    chunks, outs = refs[:parts], refs[parts : 2 * parts]
    loss, level = refs[2 * parts :]
    shape = here.shape
    row = lax.broadcasted_iota(jnp.int32, shape, 0) + rank[0] * shape[0]
    lane = lax.broadcasted_iota(jnp.int32, shape, 1)
    target = (row == lane).astype(jnp.float32)
    k = 2 * clusters
    for c in range(k):
        p = (c + clusters) % k
        top_a, top_b = here[:, c : c + 1], there[:, p : p + 1]
        sum_a, sum_b = here[:, k + c : k + c + 1], there[:, k + p : k + p + 1]
        top = jnp.maximum(top_a, top_b)
        total = sum_a * jnp.exp(top_a - top) + sum_b * jnp.exp(top_b - top)
        level[c] = jnp.broadcast_to(top + jnp.log(total), shape)
    level[k] = jnp.zeros(shape, jnp.float32)
    loss[...] = jnp.zeros(shape, jnp.float32)

    def weigh(n, ref, slot, at, ok):
        logits = ref[slot] * scale
        chances = jnp.exp(logits - level[at])
        if ok is None:
            chances = chances - target
            loss[...] += jnp.where(lane == 0, level[at], 0.0) - logits * target
        else:
            chances = jnp.where(ok, chances, 0.0)
        outs[n][slot] = chances.astype(jnp.bfloat16)

    each_slot(weigh, chunks, plans, clusters, cap, tab)


def whole_weights(pieces, order, slot):
    by_distance = sorted(zip(order, pieces), key=lambda pair: pair[0])
    return jnp.concatenate([piece[slot] for _, piece in by_distance], axis=0)


def take_pieces(refs, count, ways):
    return [refs[i * ways : (i + 1) * ways] for i in range(count)], refs[count * ways :]


def grad_kernel(tasks, used, splits, clusters, cap, order, tab_a, tab_b, rank, *refs):
    tab, ways, me = (tab_a, tab_b), len(order), rank[0]
    share = CLUSTER // ways
    mine, other = refs[:2]
    keys, at_ref = {}, 2
    for m, split in splits:
        keys[m] = refs[at_ref : at_ref + split]
        at_ref += split
    pieces, refs = take_pieces(refs[at_ref:], used, ways)
    total = refs[-1]
    come_at, out_at = 0, sum(task[3] for task in tasks)
    for kind, groups, lo, arrived, outputs in tasks:
        came = refs[come_at : come_at + arrived]
        outs = refs[out_at : out_at + outputs]
        come_at, out_at = come_at + arrived, out_at + outputs
        wide = outs[0].shape[-1]
        span = wide * outputs

        def term(n, requester, slot, mask, c, e, fresh):
            w = whole_weights(pieces[n], order, slot)
            row = rows_of(other if requester else mine, c, me, ways, slice(lo, lo + span))
            part = lax.dot_general(w, row, TN, preferred_element_type=jnp.float32)
            total[e, :, :span] = part if fresh else total[e, :, :span] + part

        def query(n, requester, slot, mask, c, e, fresh):
            w = whole_weights(pieces[n], order, slot)
            piece = keys[mask][0].shape[-1]
            for i, key in enumerate(keys[mask]):
                at = slice(i * piece, (i + 1) * piece)
                part = lax.dot_general(w, key[e], NN, preferred_element_type=jnp.float32)
                total[c, :, at] = part if fresh else total[c, :, at] + part

        visit = term if kind == "term" else query
        own = [g for g in groups if g[1:3] == (0, 0) and g[3]]
        if own:

            @pl.loop(0, clusters)
            def _(c):
                visit(own[0][0], 0, c, 0, c, c, True)

        else:
            total[:, :, :span] = jnp.zeros(total.shape[:2] + (span,), jnp.float32)

        @pl.loop(0, cap)
        def _(j):
            for n, mask, requester, first in groups:
                _, c, e = unpack(tab[requester][mask * cap + j])
                visit(n, requester, first + j, mask, c, e, False)

        @pl.loop(0, clusters)
        def _(c):
            for i, out in enumerate(outs):
                value = total[c, :, i * wide : (i + 1) * wide]
                for ref in came:
                    value = value + ref[c].astype(jnp.float32)
                if kind == "term":
                    out[c] = value.astype(out.dtype)
                else:
                    for at in range(ways):
                        block = value[at * share : (at + 1) * share]
                        out[c, share_rows(me, at, share), :] = block.astype(out.dtype)


def sum_kernel(before, base, *refs):
    parts, (out, squares) = refs[:-2], refs[-2:]
    squares[...] = before[...]

    @pl.loop(0, out.shape[0])
    def _(c):
        value = base[c]
        for ref in parts:
            if ref.shape == base.shape:
                value = value + ref[c].astype(jnp.float32)
        sides = [ref for ref in parts if ref.shape != base.shape]
        wide = out.shape[-1] // 2
        for i in range(0, len(sides), 2):
            pair = [ref[c].astype(jnp.float32) for ref in sides[i : i + 2]]
            value = value + jnp.concatenate(pair, axis=-1)
        out[c] = value
        square = jnp.sum((value * value).reshape(-1, 8, value.shape[-1]), axis=0)
        lanes = [square[:, i : i + CLUSTER] for i in range(0, value.shape[-1], CLUSTER)]
        squares[...] += sum(lanes)


def summed(before, base, *parts):
    shapes = tuple(jax.ShapeDtypeStruct(a.shape, a.dtype) for a in (base, before))
    return call("summed", sum_kernel, shapes, [], 0, (before, base, *parts), 0)


def split_of(mask):
    return 2 if mask > 1 else 1


def shards(queries, passages, matching):
    bf16, f32 = jnp.bfloat16, jnp.float32
    size, ways = lax.axis_size("dp"), lax.axis_size("tensor")
    clusters, width = matching.shape[0], queries.shape[1]
    requests = clusters * PARTNERS
    cap = -(-requests // size)
    parts = size // 2
    share = CLUSTER // ways
    scale = (width * ways) ** (-0.5)
    cube = (clusters, CLUSTER, width)
    mine, own_keys = queries.reshape(cube), passages.reshape(cube)
    here = lax.axis_index("dp").astype(jnp.int32)
    rank = lax.axis_index("tensor").astype(jnp.int32).reshape(1)
    plans = layout(parts, clusters, cap)

    halves = jnp.split(own_keys, 2, axis=-1)
    held = {}
    for bit in reversed(range(1, bits_of(parts))):
        first = swap(halves[0], "dp", 1 << bit)
        first, second = lax.optimization_barrier((first, halves[1]))
        held[1 << bit] = [first, swap(second, "dp", 1 << bit)]
        for mask in [m for m in held if m >> (bit + 1)]:
            held[mask | (1 << bit)] = [swap(h, "dp", 1 << bit) for h in held[mask]]
    if parts > 1:
        far = list(held)
        held[1] = [swap(own_keys, "dp", 1)]
    held[0] = [own_keys]
    other = swap(mine, "dp", parts)

    def table(asked):
        asked = asked.reshape(requests)
        owner, local = asked // clusters, asked % clusters
        earlier = jnp.arange(requests)[None, :] < jnp.arange(requests)[:, None]
        same = owner[:, None] == owner[None, :]
        place = (owner ^ here) * cap + jnp.sum(jnp.where(same & earlier, 1, 0), axis=1)
        code = VALID + jnp.arange(requests) // PARTNERS * 256 + local
        slots = jnp.arange(parts * cap)[:, None] == place[None, :]
        return jnp.sum(jnp.where(slots, code[None, :], 0), axis=1).astype(jnp.int32)

    tab = (table(matching), table(swap(matching, "dp", parts)))

    unit = 2 * CLUSTER * CLUSTER * width
    rows = {0: mine, 1: other}
    chunks, waits = [], ()
    for n, (groups, count) in enumerate(plans):
        if n == 1 and parts > 1:
            for mask in far:
                last, _ = lax.optimization_barrier((held[mask][-1], waits[0]))
                held[mask | 1] = [swap(h, "dp", 1) for h in held[mask][:-1] + [last]]
        masks = sorted({m for m, _, _ in groups})
        askers = sorted({r for _, r, _ in groups})
        splits = tuple((m, len(held[m])) for m in masks)
        half = jax.ShapeDtypeStruct((ways // 2, count, share, CLUSTER), f32)
        keep, give, done = call(
            f"logits_{n}",
            functools.partial(logits_kernel, groups, splits, clusters, cap, ways),
            (half, half, jax.ShapeDtypeStruct((8, CLUSTER), f32)),
            [], count * unit,
            (tab[0], tab[max(askers)], rank, *[rows[r] for r in askers],
             *[k for m in masks for k in held[m]]),
            3, waits,
        )
        waits = (done,)
        got = swap(give, "tensor", 1)
        bit = 1
        while (1 << bit) < ways:
            keep = keep + got
            pairs = keep.reshape((keep.shape[0] // 2, 2) + keep.shape[1:])
            keep = pairs[:, 0]
            got = swap(pairs[:, 1], "tensor", 1 << bit)
            bit += 1
        chunks.append((keep + got)[0])

    tile = jax.ShapeDtypeStruct((share, CLUSTER), f32)
    levels = pltpu.VMEM((2 * clusters + 1, share, CLUSTER), f32)
    stats = call(
        "row_stats",
        functools.partial(stats_kernel, plans, clusters, cap, scale),
        tile, [levels, levels], 0, (*tab, *chunks), 2,
    )
    facing = swap(stats, "dp", parts)
    *weights, loss_rows = call(
        "weights",
        functools.partial(weights_kernel, plans, clusters, cap, scale),
        [jax.ShapeDtypeStruct(chunks[n].shape, bf16) for n in range(len(plans))] + [tile],
        [levels], 0, (*tab, rank, stats, facing, *chunks), 3,
    )
    order = [0]
    for bit in reversed(range(bits_of(ways))):
        order += [at | (1 << bit) for at in order]
    pieces = [None] * len(plans)
    for n in reversed(range(len(plans))):
        pieces[n] = [weights[n]]
        for bit in reversed(range(bits_of(ways))):
            pieces[n] += [swap(piece, "tensor", 1 << bit) for piece in pieces[n]]

    def chosen(wanted):
        groups = [
            (n, m, r, first)
            for n, (plan, _) in enumerate(plans)
            for m, r, first in plan
            if wanted(m, r)
        ]
        used = sorted({g[0] for g in groups})
        groups = tuple((used.index(n), m, r, first) for n, m, r, first in groups)
        return groups, len(used), [p for n in used for p in pieces[n]]

    def gradients(name, wanted, waits=()):
        found, used, args = chosen(
            lambda m, r: any(w[1] == (m if w[0] == "term" else r) for w in wanted)
        )
        asked = sorted({g[1] for g in found}) if any(w[0] == "query" for w in wanted) else []
        tasks, shapes, came = [], [], []
        for w in wanted:
            groups = tuple(g for g in found if w[1] == (g[1] if w[0] == "term" else g[2]))
            lo, wide, outputs, add = w[2:] if w[0] == "term" else (0, width, 1, [])
            kept = bf16 if w[1] else f32
            tasks.append((w[0], groups, lo, len(add), outputs))
            shapes += [jax.ShapeDtypeStruct(cube[:2] + (wide,), kept)] * outputs
            came += add
        splits = tuple((m, len(held[m])) for m in asked)
        return call(
            name,
            functools.partial(grad_kernel, tasks, used, splits, clusters, cap, order),
            shapes, [pltpu.VMEM(cube, f32)], unit * cap * len(tasks),
            (*tab, rank, mine, other, *[k for m in asked for k in held[m]], *args, *came),
            3, waits,
        )

    def lowest(m):
        return bits_of(m & -m) if m else bits_of(parts)

    half = width // 2
    odd = [m for m in range(3, parts, 2)]
    lead = [("term", m, 0, half, 2, []) for m in odd] + [("query", 1)]
    lead += [("term", 1, 0, width, 1, [])] if parts > 1 else []
    made = gradients("grads_lead", lead)
    terms = {m: made[2 * i : 2 * i + 2] for i, m in enumerate(odd)}
    far_q, near = made[2 * len(odd)], made[2 * len(odd) + 1 :]
    own_p, own_q = gradients("grads_own", [("term", 0, 0, width, 1, []), ("query", 0)], (far_q,))
    came = []
    for m in sorted(range(2, parts, 2), key=lambda m: (lowest(m), -m)):
        came = [[swap(t, "dp", 1 << b) for t in terms[m | (1 << b)]] for b in range(lowest(m))]
        terms[m] = []
        for i in range(2):
            add = [got[i] for got in came]
            terms[m] += gradients(f"term_{m}_{i}", [("term", m, i * half, half, 1, add)])
    if near:
        if came:
            near = [lax.optimization_barrier((near[0], came[0][-1]))[0]]
        terms[1] = near
    came = [swap(t, "dp", 1 << b) for b in range(bits_of(parts)) for t in terms[1 << b]]
    far_q = swap(far_q, "dp", parts)
    zero = jnp.zeros((8, CLUSTER), f32)
    grad_q, squares = summed(zero, own_q, far_q)
    grad_p, squares = summed(squares, own_p, *came)

    sums = jnp.stack([jnp.sum(loss_rows.reshape(-1, 8, CLUSTER), axis=0), squares])
    for bit in range(bits_of(ways)):
        sums = sums + swap(sums, "tensor", 1 << bit)
    for bit in range(bits_of(size)):
        sums = sums + swap(sums, "dp", 1 << bit)
    sums = jnp.sum(sums, axis=(1, 2))
    all_rows = clusters * CLUSTER * size
    clip_limit = 0.25 * jnp.sqrt(jnp.float32(2 * all_rows * width * ways))
    factor = jnp.minimum(jnp.float32(1.0), clip_limit / jnp.sqrt(sums[1] + 1e-06))
    flat = queries.shape
    grad_queries = (grad_q * factor).astype(bf16).reshape(flat)
    grad_passages = (grad_p * factor).astype(bf16).reshape(flat)
    return (grad_queries, grad_passages, sums[0] / all_rows)


def solution(mesh):
    in_specs = (P("dp", "tensor"), P("dp", "tensor"), P("dp", None))
    out_specs = (P("dp", "tensor"), P("dp", "tensor"), P())
    return jax.shard_map(shards, mesh=mesh, in_specs=in_specs, out_specs=out_specs, check_vma=False)
```

time: 350 us -> 295 us (0.84)
  Pallas kernels: 94.7 us -> 49.7 us
  other arithmetic: 22.8 us -> 4.26 us
  waiting for transfers between devices: 182 us -> 199 us
  starting transfers between devices: 36.7 us -> 33.1 us
    pallas_call x12 -> x11, Pallas kernels: 94.7 us -> 49.7 us  [call(): pl.pallas_call(body, name=name, out_shape=out_shape, in_specs=[SM] * smem...]
    ppermute x35 -> x34, waiting for transfers between devices: 182 us -> 199 us  [swap(): return lax.ppermute(value, axis, [(i, i ^ mask) for i in range(size)])]
    reduce_sum x5 -> x6, other arithmetic: 8.61 us -> 0.69 us  [the longest x2 0.36 us: table(): jnp.sum(jnp.where(same & earlier, 1, 0), axis=1)]
    convert_element_type x1, other arithmetic: 7.77 us -> 2.98 us  [shards(): grad_passages = (grad_p * factor).astype(bf16).reshape(flat)]
    unnamed x48 -> x8, local copies, waits for them, and re-layouts: 6.23 us -> 1.51 us
    ppermute x35 -> x34, starting transfers between devices: 36.7 us -> 33.1 us  [swap(): return lax.ppermute(value, axis, [(i, i ^ mask) for i in range(size)])]
  transfers between devices with their start and end apart: 35 -> 34, of which waited for: 18 -> 21; matrix products, arithmetic and copies ran while one was open for 3% -> 2% of each run, Pallas kernels for 23% -> 12%
where the time goes in v2:
time: 295 us
  waiting for transfers between devices  199 us (67%)
  Pallas kernels  49.7 us (17%)
  starting transfers between devices  33.1 us (11%)
  local copies, waits for them, and re-layouts  5.47 us (2%)
  other arithmetic  4.26 us (1%)
  between operations  3.38 us (1%)
    ppermute x34, waiting for transfers between devices, swap(): return lax.ppermute(value, axis, [(i, i ^ mask) for i in range(size)])  199 us
    pallas_call x11, Pallas kernels, call(): pl.pallas_call(body, name=name, out_shape=out_shape, in_specs=[SM] * smem...  49.7 us
    ppermute x34, starting transfers between devices, swap(): return lax.ppermute(value, axis, [(i, i ^ mask) for i in range(size)])  33.1 us
  transfers between devices with their start and end apart: 34, of which 21 were waited for; matrix products, arithmetic and copies ran while one was open for 2% of the time, Pallas kernels for 12%

profile of v2, /device:TPU:0, one launch (start us, length us, event | category | flops | bytes accessed | tf_op | source)
XLA Modules:
  0.0 294.9 jit_solution(13455030552824829709)
XLA Ops:
  0.6 4.1 %collective-permute-start = (s32[7,8]{1,0:T(8,128)}, s32[7,8]{1,0:T(8,128)S(1)}, u32[]{:S(2)}, u32[]{:S(2)}) collective-permute-start(s32[7,8]{1,0:T(8,128)} %param.5), channel_id=1, source_target_pairs={{0,16},{4,20},{8,24},{12,28},{16,0},{20,4},{24,8},{28,12},{1,17},{... | collective-permute-start | bytes 680 | tf_op jit(solution)/shard_map/ppermute | solution.py:32
  6.3 2.8 fusion.13
  11.6 36.8 %collective-permute-done.3.refs_7_ = bf16[7,128,512]{2,1,0:T(8,128)(2,1)S(1)} collective-permute-done((bf16[7,128,512]{2,1,0:T(8,128)(2,1)}, bf16[7,128,512]{2,1,0:T(8,128)(2,1)S(1)}, u32[]{:S(2)}, u32[]{:S(2)}) %collective-permute-start.3) | collective-permute-done | bytes 917536 | tf_op jit(solution)/shard_map/ppermute | solution.py:32
  50.3 5.5 %logits_0.1 = (f32[2,21,32,128]{3,2,1,0:T(8,128)S(1)}, f32[2,21,32,128]{3,2,1,0:T(8,128)S(1)}, f32[8,128]{1,0:T(8,128)S(1)}) custom-call(s32[28]{0:T(128)S(1)} %select_reduce_fusion.3.refs_0_.refs_1_, s32[28]{0:T(128)S(1)} %select_reduce_fusion.3.refs_0_.refs_1_, s32[1]{0:T(128)} %bitcast.refs_2_, bf16[7,128,1024]{2,1,0:T(8,128)(2,1)S(1)} %bitcast.48, ...), custom_call_target="tpu_custom_call" | custom-call | flops 704643 | bytes 6885 | tf_op jit(solution)/shard_map/logits_0/pallas_call | solution.py:47
  56.6 32.4 %collective-permute-done.4.refs_8_ = bf16[7,128,512]{2,1,0:T(8,128)(2,1)} collective-permute-done((bf16[7,128,512]{2,1,0:T(8,128)(2,1)}, bf16[7,128,512]{2,1,0:T(8,128)(2,1)}, u32[]{:S(2)}, u32[]{:S(2)}) %collective-permute-start.4) | collective-permute-done | bytes 917536 | tf_op jit(solution)/shard_map/ppermute | solution.py:32
  89.8 2.2 collective-permute-done.1.refs_4_
  91.9 5.4 %logits_1.1 = (f32[2,28,32,128]{3,2,1,0:T(8,128)S(1)}, f32[2,28,32,128]{3,2,1,0:T(8,128)S(1)}, f32[8,128]{1,0:T(8,128)S(1)}) custom-call(s32[28]{0:T(128)S(1)} %select_reduce_fusion.3.refs_0_.refs_1_, s32[28]{0:T(128)S(1)} %select_reduce_fusion.2.refs_1_, s32[1]{0:T(128)} %bitcast.refs_2_, bf16[7,128,1024]{2,1,0:T(8,128)(2,1)S(1)} %bitcast.49, ...), custom_call_target="tpu_custom_call" | custom-call | flops 939524 | bytes 11014 | tf_op jit(solution)/shard_map/logits_1/pallas_call | solution.py:47
  99.2 10.7 %collective-permute-done.6.refs_6_.refs_10_ = bf16[7,128,512]{2,1,0:T(8,128)(2,1)S(1)} collective-permute-done((bf16[7,128,512]{2,1,0:T(8,128)(2,1)}, bf16[7,128,512]{2,1,0:T(8,128)(2,1)S(1)}, u32[]{:S(2)}, u32[]{:S(2)}) %collective-permute-start.6) | collective-permute-done | bytes 917536 | tf_op jit(solution)/shard_map/ppermute | solution.py:32
  109.9 4.1 %logits_2.1 = (f32[2,14,32,128]{3,2,1,0:T(8,128)S(1)}, f32[2,14,32,128]{3,2,1,0:T(8,128)S(1)}, f32[8,128]{1,0:T(8,128)}) custom-call(s32[28]{0:T(128)S(1)} %select_reduce_fusion.3.refs_0_.refs_1_, s32[28]{0:T(128)S(1)} %select_reduce_fusion.2.refs_1_, s32[1]{0:T(128)} %bitcast.refs_2_, bf16[7,128,1024]{2,1,0:T(8,128)(2,1)S(1)} %bitcast.50, ...), custom_call_target="tpu_custom_call" | custom-call | flops 469762 | bytes 6426 | tf_op jit(solution)/shard_map/logits_2/pallas_call | solution.py:47
  117.5 10.1 %collective-permute-done.10 = f32[1,28,32,128]{3,2,1,0:T(8,128)S(1)} collective-permute-done((f32[1,28,32,128]{3,2,1,0:T(8,128)S(1)}, f32[1,28,32,128]{3,2,1,0:T(8,128)S(1)}, u32[]{:S(2)}, u32[]{:S(2)}) %collective-permute-start.10) | collective-permute-done | bytes 458784 | tf_op jit(solution)/shard_map/ppermute | solution.py:32
  127.7 4.5 %collective-permute-done.12 = f32[1,14,32,128]{3,2,1,0:T(8,128)S(1)} collective-permute-done((f32[1,14,32,128]{3,2,1,0:T(8,128)S(1)}, f32[1,14,32,128]{3,2,1,0:T(8,128)S(1)}, u32[]{:S(2)}, u32[]{:S(2)}) %collective-permute-start.12) | collective-permute-done | bytes 229408 | tf_op jit(solution)/shard_map/ppermute | solution.py:32
  135.2 3.3 %collective-permute-done.13.refs_4_ = f32[32,128]{1,0:T(8,128)S(1)} collective-permute-done((f32[32,128]{1,0:T(8,128)S(1)}, f32[32,128]{1,0:T(8,128)S(1)}, u32[]{:S(2)}, u32[]{:S(2)}) %collective-permute-start.13) | collective-permute-done | bytes 16416 | tf_op jit(solution)/shard_map/ppermute | solution.py:32
  138.5 1.9 weights.1
  144.3 4.8 %collective-permute-done.17.refs_16_.refs_6_ = bf16[28,32,128]{2,1,0:T(8,128)(2,1)S(1)} collective-permute-done((bf16[28,32,128]{2,1,0:T(8,128)(2,1)S(1)}, bf16[28,32,128]{2,1,0:T(8,128)(2,1)S(1)}, u32[]{:S(2)}, u32[]{:S(2)}) %collective-permute-start.17) | collective-permute-done | bytes 229408 | tf_op jit(solution)/shard_map/ppermute | solution.py:32
  149.6 1.9 collective-permute-done.14.refs_12_
  154.1 11.2 %grads_lead.1 = (bf16[7,128,512]{2,1,0:T(8,128)(2,1)S(1)}, bf16[7,128,512]{2,1,0:T(8,128)(2,1)S(1)}, bf16[7,128,1024]{2,1,0:T(8,128)(2,1)S(1)}, bf16[7,128,1024]{2,1,0:T(8,128)(2,1)S(1)}) custom-call(s32[28]{0:T(128)S(1)} %select_reduce_fusion.3.refs_0_.refs_1_, s32[28]{0:T(128)S(1)} %select_reduce_fusion.2.refs_1_, s32[1]{0:T(128)} %bitcast.refs_2_, ...), custom_call_target="tpu_custom_call" | custom-call | flops 704643 | bytes 18579 | tf_op jit(solution)/shard_map/grads_lead/pallas_call | solution.py:47
  168.9 19.8 %collective-permute-done.24.refs_9_ = bf16[7,128,512]{2,1,0:T(8,128)(2,1)S(1)} collective-permute-done((bf16[7,128,512]{2,1,0:T(8,128)(2,1)S(1)}, bf16[7,128,512]{2,1,0:T(8,128)(2,1)S(1)}, u32[]{:S(2)}, u32[]{:S(2)}) %collective-permute-start.24) | collective-permute-done | bytes 917536 | tf_op jit(solution)/shard_map/ppermute | solution.py:32
  189.3 3.6 %term_2_1.1 = bf16[7,128,512]{2,1,0:T(8,128)(2,1)S(1)} custom-call(s32[28]{0:T(128)S(1)} %select_reduce_fusion.3.refs_0_.refs_1_, s32[28]{0:T(128)S(1)} %select_reduce_fusion.2.refs_1_, s32[1]{0:T(128)} %bitcast.refs_2_, bf16[7,128,1024]{2,1,0:T(8,128)(2,1)S(1)} %bitcast.52, bf16[7,128,1024]{2,1,0:T(8,128)(2,1)} %collective-permute-done.1.refs_4_, ...), custom_call_target="tpu_custom_call" | custom-call | flops 234881 | bytes 6422 | tf_op jit(solution)/shard_map/term_2_1/pallas_call | solution.py:47
  192.9 2.6 collective-permute-start.28
  195.4 12.9 %collective-permute-done.26.refs_9_ = bf16[7,128,512]{2,1,0:T(8,128)(2,1)S(1)} collective-permute-done((bf16[7,128,512]{2,1,0:T(8,128)(2,1)S(1)}, bf16[7,128,512]{2,1,0:T(8,128)(2,1)S(1)}, u32[]{:S(2)}, u32[]{:S(2)}) %collective-permute-start.26) | collective-permute-done | bytes 917536 | tf_op jit(solution)/shard_map/ppermute | solution.py:32
  208.3 3.6 %term_2_0.1 = bf16[7,128,512]{2,1,0:T(8,128)(2,1)S(1)} custom-call(s32[28]{0:T(128)S(1)} %select_reduce_fusion.3.refs_0_.refs_1_, s32[28]{0:T(128)S(1)} %select_reduce_fusion.2.refs_1_, s32[1]{0:T(128)} %bitcast.refs_2_, bf16[7,128,1024]{2,1,0:T(8,128)(2,1)S(1)} %bitcast.53, bf16[7,128,1024]{2,1,0:T(8,128)(2,1)} %collective-permute-done.1.refs_4_, ...), custom_call_target="tpu_custom_call" | custom-call | flops 234881 | bytes 6422 | tf_op jit(solution)/shard_map/term_2_0/pallas_call | solution.py:47
  211.9 2.5 collective-permute-start.27
  214.5 11.4 %grads_own.1 = (f32[7,128,1024]{2,1,0:T(8,128)S(1)}, f32[7,128,1024]{2,1,0:T(8,128)S(1)}) custom-call(s32[28]{0:T(128)S(1)} %select_reduce_fusion.3.refs_0_.refs_1_, s32[28]{0:T(128)S(1)} %select_reduce_fusion.2.refs_1_, s32[1]{0:T(128)} %bitcast.refs_2_, bf16[7,128,1024]{2,1,0:T(8,128)(2,1)S(1)} %bitcast.54, ...), custom_call_target="tpu_custom_call" | custom-call | flops 469762 | bytes 20414 | tf_op jit(solution)/shard_map/grads_own/pallas_call | solution.py:47
  225.8 22.4 %collective-permute-done.23.refs_2_ = bf16[7,128,1024]{2,1,0:T(8,128)(2,1)S(1)} collective-permute-done((bf16[7,128,1024]{2,1,0:T(8,128)(2,1)S(1)}, bf16[7,128,1024]{2,1,0:T(8,128)(2,1)S(1)}, u32[]{:S(2)}, u32[]{:S(2)}) %collective-permute-start.23) | collective-permute-done | bytes 1835040 | tf_op jit(solution)/shard_map/ppermute | solution.py:32
  248.8 5.2 %collective-permute-done.28.refs_4_ = bf16[7,128,512]{2,1,0:T(8,128)(2,1)S(1)} collective-permute-done((bf16[7,128,512]{2,1,0:T(8,128)(2,1)S(1)}, bf16[7,128,512]{2,1,0:T(8,128)(2,1)S(1)}, u32[]{:S(2)}, u32[]{:S(2)}) %collective-permute-start.28) | collective-permute-done | bytes 917536 | tf_op jit(solution)/shard_map/ppermute | solution.py:32
  254.0 17.2 %collective-permute-done.27.refs_3_ = bf16[7,128,512]{2,1,0:T(8,128)(2,1)S(1)} collective-permute-done((bf16[7,128,512]{2,1,0:T(8,128)(2,1)S(1)}, bf16[7,128,512]{2,1,0:T(8,128)(2,1)S(1)}, u32[]{:S(2)}, u32[]{:S(2)}) %collective-permute-start.27) | collective-permute-done | bytes 917536 | tf_op jit(solution)/shard_map/ppermute | solution.py:32
  274.7 2.2 collective-permute-done.30
  278.2 2.4 collective-permute-done.31
  280.5 3.6 %collective-permute-done.32 = f32[2,8,128]{2,1,0:T(8,128)S(1)} collective-permute-done((f32[2,8,128]{2,1,0:T(8,128)S(1)}, f32[2,8,128]{2,1,0:T(8,128)S(1)}, u32[]{:S(2)}, u32[]{:S(2)}) %collective-permute-start.32) | collective-permute-done | bytes 8224 | tf_op jit(solution)/shard_map/ppermute | solution.py:32
  284.2 1.7 collective-permute-start.33
  285.9 2.9 collective-permute-done.33
  290.8 3.0 %multiply_convert_fusion = (bf16[7,128,1024]{2,1,0:T(8,128)(2,1)}, bf16[7,128,1024]{2,1,0:T(8,128)(2,1)}) fusion(f32[7,128,1024]{2,1,0:T(8,128)S(1)} %get-tuple-element.54, f32[]{:T(128)} %bitcast.18, f32[7,128,1024]{2,1,0:T(8,128)S(1)} %get-tuple-element.45), kind=kLoop, calls=%fused_computation | loop fusion | flops 3670016 | bytes 11010052 | tf_op jit(solution)/shard_map/convert_element_type | solution.py:472
  (93 shorter events, 32.9 us)
Async XLA Ops:
  0.6 47.7 %collective-permute-start = (s32[7,8]{1,0:T(8,128)}, s32[7,8]{1,0:T(8,128)S(1)}, u32[]{:S(2)}, u32[]{:S(2)}) collective-permute-start(s32[7,8]{1,0:T(8,128)} %param.5), channel_id=1, source_target_pairs={{0,16},{4,20},{8,24},{12,28},{16,0},{20,4},{24,8},{28,12},{1,17},{... | collective-permute-start | bytes 680 | tf_op jit(solution)/shard_map/ppermute | solution.py:32
  4.7 44.1 %collective-permute-start.2 = (bf16[7,128,1024]{2,1,0:T(8,128)(2,1)}, bf16[7,128,1024]{2,1,0:T(8,128)(2,1)}, u32[]{:S(2)}, u32[]{:S(2)}) collective-permute-start(bf16[7,128,1024]{2,1,0:T(8,128)(2,1)} %bitcast.55), channel_id=1, source_target_pairs={{0,4},{4,0},{8,12},{12,8},{16,20},{20,16},{24,28},{28,24},{1,5},{5... | collective-permute-start | bytes 5505032 | tf_op jit(solution)/shard_map/ppermute | solution.py:32
  9.1 39.3 %collective-permute-start.3 = (bf16[7,128,512]{2,1,0:T(8,128)(2,1)}, bf16[7,128,512]{2,1,0:T(8,128)(2,1)S(1)}, u32[]{:S(2)}, u32[]{:S(2)}) collective-permute-start(bf16[7,128,512]{2,1,0:T(8,128)(2,1)} %get-tuple-element.56), channel_id=1, source_target_pairs={{0,8},{4,12},{8,0},{12,4},{16,24},{20,28},{24,16},{28,20},{1,9},{5... | collective-permute-start | bytes 2752520 | tf_op jit(solution)/shard_map/ppermute | solution.py:32
  10.7 81.3 %collective-permute-start.1 = (bf16[7,128,1024]{2,1,0:T(8,128)(2,1)S(1)}, bf16[7,128,1024]{2,1,0:T(8,128)(2,1)}, u32[]{:S(2)}, u32[]{:S(2)}) collective-permute-start(bf16[7,128,1024]{2,1,0:T(8,128)(2,1)S(1)} %bitcast.47), channel_id=1, source_target_pairs={{0,16},{4,20},{8,24},{12,28},{16,0},{20,4},{24,8},{28,12},{1,17},{... | collective-permute-start | bytes 5505032 | tf_op jit(solution)/shard_map/ppermute | solution.py:32
  48.4 40.7 %collective-permute-start.4 = (bf16[7,128,512]{2,1,0:T(8,128)(2,1)}, bf16[7,128,512]{2,1,0:T(8,128)(2,1)}, u32[]{:S(2)}, u32[]{:S(2)}) collective-permute-start(bf16[7,128,512]{2,1,0:T(8,128)(2,1)} %get-tuple-element.30), channel_id=1, source_target_pairs={{0,8},{4,12},{8,0},{12,4},{16,24},{20,28},{24,16},{28,20},{1,9},{5... | collective-permute-start | bytes 2752520 | tf_op jit(solution)/shard_map/ppermute | solution.py:32
  55.8 41.6 %collective-permute-start.7 = (f32[2,21,32,128]{3,2,1,0:T(8,128)S(1)}, f32[2,21,32,128]{3,2,1,0:T(8,128)S(1)}, u32[]{:S(2)}, u32[]{:S(2)}) collective-permute-start(f32[2,21,32,128]{3,2,1,0:T(8,128)S(1)} %get-tuple-element.34), channel_id=1, source_target_pairs={{0,1},{1,0},{2,3},{3,2},{4,5},{5,4},{6,7},{7,6},{8,9},{9,8},{10,11... | collective-permute-start | bytes 2064392 | tf_op jit(solution)/shard_map/ppermute | solution.py:32
  55.9 43.3 %collective-permute-start.5 = (bf16[7,128,512]{2,1,0:T(8,128)(2,1)S(1)}, bf16[7,128,512]{2,1,0:T(8,128)(2,1)S(1)}, u32[]{:S(2)}, u32[]{:S(2)}) collective-permute-start(bf16[7,128,512]{2,1,0:T(8,128)(2,1)S(1)} %collective-permute-done.3.refs_7_), channel_id=1, source_target_pairs={{0,4},{4,0},{8,12},{12,8},{16,20},{20,16},{24,28},{28,24},{1,5},{5... | collective-permute-start | bytes 2752520 | tf_op jit(solution)/shard_map/ppermute | solution.py:32
  89.0 20.8 %collective-permute-start.6 = (bf16[7,128,512]{2,1,0:T(8,128)(2,1)}, bf16[7,128,512]{2,1,0:T(8,128)(2,1)S(1)}, u32[]{:S(2)}, u32[]{:S(2)}) collective-permute-start(bf16[7,128,512]{2,1,0:T(8,128)(2,1)} %collective-permute-done.4.refs_8_), channel_id=1, source_target_pairs={{0,4},{4,0},{8,12},{12,8},{16,20},{20,16},{24,28},{28,24},{1,5},{5... | collective-permute-start | bytes 2752520 | tf_op jit(solution)/shard_map/ppermute | solution.py:32
  97.4 16.6 %collective-permute-start.9 = (f32[2,28,32,128]{3,2,1,0:T(8,128)S(1)}, f32[2,28,32,128]{3,2,1,0:T(8,128)S(1)}, u32[]{:S(2)}, u32[]{:S(2)}) collective-permute-start(f32[2,28,32,128]{3,2,1,0:T(8,128)S(1)} %get-tuple-element.36), channel_id=1, source_target_pairs={{0,1},{1,0},{2,3},{3,2},{4,5},{5,4},{6,7},{7,6},{8,9},{9,8},{10,11... | collective-permute-start | bytes 2752520 | tf_op jit(solution)/shard_map/ppermute | solution.py:32
  97.6 18.2 %collective-permute-start.8 = (f32[1,21,32,128]{3,2,1,0:T(8,128)S(1)}, f32[1,21,32,128]{3,2,1,0:T(8,128)S(1)}, u32[]{:S(2)}, u32[]{:S(2)}) collective-permute-start(f32[1,21,32,128]{3,2,1,0:T(8,128)S(1)} %slice_bitcast_fusion.2), channel_id=1, source_target_pairs={{0,2},{1,3},{2,0},{3,1},{4,6},{5,7},{6,4},{7,5},{8,10},{9,11},{10,... | collective-permute-start | bytes 1032200 | tf_op jit(solution)/shard_map/ppermute | solution.py:32
  114.0 1.8 collective-permute-start.11
  114.2 13.4 %collective-permute-start.10 = (f32[1,28,32,128]{3,2,1,0:T(8,128)S(1)}, f32[1,28,32,128]{3,2,1,0:T(8,128)S(1)}, u32[]{:S(2)}, u32[]{:S(2)}) collective-permute-start(f32[1,28,32,128]{3,2,1,0:T(8,128)S(1)} %slice_bitcast_fusion), channel_id=1, source_target_pairs={{0,2},{1,3},{2,0},{3,1},{4,6},{5,7},{6,4},{7,5},{8,10},{9,11},{10,... | collective-permute-start | bytes 1376264 | tf_op jit(solution)/shard_map/ppermute | solution.py:32
  115.9 16.2 %collective-permute-start.12 = (f32[1,14,32,128]{3,2,1,0:T(8,128)S(1)}, f32[1,14,32,128]{3,2,1,0:T(8,128)S(1)}, u32[]{:S(2)}, u32[]{:S(2)}) collective-permute-start(f32[1,14,32,128]{3,2,1,0:T(8,128)S(1)} %slice_bitcast_fusion.4), channel_id=1, source_target_pairs={{0,2},{1,3},{2,0},{3,1},{4,6},{5,7},{6,4},{7,5},{8,10},{9,11},{10,... | collective-permute-start | bytes 688136 | tf_op jit(solution)/shard_map/ppermute | solution.py:32
  133.8 4.7 %collective-permute-start.13 = (f32[32,128]{1,0:T(8,128)S(1)}, f32[32,128]{1,0:T(8,128)S(1)}, u32[]{:S(2)}, u32[]{:S(2)}) collective-permute-start(f32[32,128]{1,0:T(8,128)S(1)} %row_stats.1.refs_3_), channel_id=1, source_target_pairs={{0,16},{4,20},{8,24},{12,28},{16,0},{20,4},{24,8},{28,12},{1,17},{... | collective-permute-start | bytes 49160 | tf_op jit(solution)/shard_map/ppermute | solution.py:32
  140.5 8.6 %collective-permute-start.17 = (bf16[28,32,128]{2,1,0:T(8,128)(2,1)S(1)}, bf16[28,32,128]{2,1,0:T(8,128)(2,1)S(1)}, u32[]{:S(2)}, u32[]{:S(2)}) collective-permute-start(bf16[28,32,128]{2,1,0:T(8,128)(2,1)S(1)} %get-tuple-element.41.refs_15_.refs_5_), channel_id=1, source_target_pairs={{0,2},{1,3},{2,0},{3,1},{4,6},{5,7},{6,4},{7,5},{8,10},{9,11},{10,... | collective-permute-start | bytes 688136 | tf_op jit(solution)/shard_map/ppermute | solution.py:32
  142.1 9.5 %collective-permute-start.14 = (bf16[21,32,128]{2,1,0:T(8,128)(2,1)S(1)}, bf16[21,32,128]{2,1,0:T(8,128)(2,1)S(1)}, u32[]{:S(2)}, u32[]{:S(2)}) collective-permute-start(bf16[21,32,128]{2,1,0:T(8,128)(2,1)S(1)} %get-tuple-element.40.refs_11_), channel_id=1, source_target_pairs={{0,2},{1,3},{2,0},{3,1},{4,6},{5,7},{6,4},{7,5},{8,10},{9,11},{10,... | collective-permute-start | bytes 516104 | tf_op jit(solution)/shard_map/ppermute | solution.py:32
  142.6 6.5 %collective-permute-start.21 = (bf16[14,32,128]{2,1,0:T(8,128)(2,1)S(1)}, bf16[14,32,128]{2,1,0:T(8,128)(2,1)S(1)}, u32[]{:S(2)}, u32[]{:S(2)}) collective-permute-start(bf16[14,32,128]{2,1,0:T(8,128)(2,1)S(1)} %get-tuple-element.42.refs_19_), channel_id=1, source_target_pairs={{0,1},{1,0},{2,3},{3,2},{4,5},{5,4},{6,7},{7,6},{8,9},{9,8},{10,11... | collective-permute-start | bytes 344072 | tf_op jit(solution)/shard_map/ppermute | solution.py:32
  142.6 10.2 %collective-permute-start.20 = (bf16[14,32,128]{2,1,0:T(8,128)(2,1)S(1)}, bf16[14,32,128]{2,1,0:T(8,128)(2,1)S(1)}, u32[]{:S(2)}, u32[]{:S(2)}) collective-permute-start(bf16[14,32,128]{2,1,0:T(8,128)(2,1)S(1)} %get-tuple-element.42.refs_19_), channel_id=1, source_target_pairs={{0,2},{1,3},{2,0},{3,1},{4,6},{5,7},{6,4},{7,5},{8,10},{9,11},{10,... | collective-permute-start | bytes 344072 | tf_op jit(solution)/shard_map/ppermute | solution.py:32
  144.1 10.0 %collective-permute-start.18 = (bf16[28,32,128]{2,1,0:T(8,128)(2,1)S(1)}, bf16[28,32,128]{2,1,0:T(8,128)(2,1)S(1)}, u32[]{:S(2)}, u32[]{:S(2)}) collective-permute-start(bf16[28,32,128]{2,1,0:T(8,128)(2,1)S(1)} %get-tuple-element.41.refs_15_.refs_5_), channel_id=1, source_target_pairs={{0,1},{1,0},{2,3},{3,2},{4,5},{5,4},{6,7},{7,6},{8,9},{9,8},{10,11... | collective-permute-start | bytes 688136 | tf_op jit(solution)/shard_map/ppermute | solution.py:32
  149.1 5.0 %collective-permute-start.19 = (bf16[28,32,128]{2,1,0:T(8,128)(2,1)S(1)}, bf16[28,32,128]{2,1,0:T(8,128)(2,1)S(1)}, u32[]{:S(2)}, u32[]{:S(2)}) collective-permute-start(bf16[28,32,128]{2,1,0:T(8,128)(2,1)S(1)} %collective-permute-done.17.refs_16_.refs_6_), channel_id=1, source_target_pairs={{0,1},{1,0},{2,3},{3,2},{4,5},{5,4},{6,7},{7,6},{8,9},{9,8},{10,11... | collective-permute-start | bytes 688136 | tf_op jit(solution)/shard_map/ppermute | solution.py:32
  149.1 3.7 %collective-permute-start.15 = (bf16[21,32,128]{2,1,0:T(8,128)(2,1)S(1)}, bf16[21,32,128]{2,1,0:T(8,128)(2,1)S(1)}, u32[]{:S(2)}, u32[]{:S(2)}) collective-permute-start(bf16[21,32,128]{2,1,0:T(8,128)(2,1)S(1)} %get-tuple-element.40.refs_11_), channel_id=1, source_target_pairs={{0,1},{1,0},{2,3},{3,2},{4,5},{5,4},{6,7},{7,6},{8,9},{9,8},{10,11... | collective-permute-start | bytes 516104 | tf_op jit(solution)/shard_map/ppermute | solution.py:32
  151.6 2.6 collective-permute-start.16
  165.4 23.3 %collective-permute-start.24 = (bf16[7,128,512]{2,1,0:T(8,128)(2,1)S(1)}, bf16[7,128,512]{2,1,0:T(8,128)(2,1)S(1)}, u32[]{:S(2)}, u32[]{:S(2)}) collective-permute-start(bf16[7,128,512]{2,1,0:T(8,128)(2,1)S(1)} %get-tuple-element.50), channel_id=1, source_target_pairs={{0,4},{4,0},{8,12},{12,8},{16,20},{20,16},{24,28},{28,24},{1,5},{5... | collective-permute-start | bytes 2752520 | tf_op jit(solution)/shard_map/ppermute | solution.py:32
  166.1 82.1 %collective-permute-start.23 = (bf16[7,128,1024]{2,1,0:T(8,128)(2,1)S(1)}, bf16[7,128,1024]{2,1,0:T(8,128)(2,1)S(1)}, u32[]{:S(2)}, u32[]{:S(2)}) collective-permute-start(bf16[7,128,1024]{2,1,0:T(8,128)(2,1)S(1)} %get-tuple-element.43.refs_23_), channel_id=1, source_target_pairs={{0,16},{4,20},{8,24},{12,28},{16,0},{20,4},{24,8},{28,12},{1,17},{... | collective-permute-start | bytes 5505032 | tf_op jit(solution)/shard_map/ppermute | solution.py:32
  167.7 40.6 %collective-permute-start.26 = (bf16[7,128,512]{2,1,0:T(8,128)(2,1)S(1)}, bf16[7,128,512]{2,1,0:T(8,128)(2,1)S(1)}, u32[]{:S(2)}, u32[]{:S(2)}) collective-permute-start(bf16[7,128,512]{2,1,0:T(8,128)(2,1)S(1)} %get-tuple-element.52), channel_id=1, source_target_pairs={{0,4},{4,0},{8,12},{12,8},{16,20},{20,16},{24,28},{28,24},{1,5},{5... | collective-permute-start | bytes 2752520 | tf_op jit(solution)/shard_map/ppermute | solution.py:32
  188.6 82.5 %collective-permute-start.25 = (bf16[7,128,1024]{2,1,0:T(8,128)(2,1)S(1)}, bf16[7,128,1024]{2,1,0:T(8,128)(2,1)S(1)}, u32[]{:S(2)}, u32[]{:S(2)}) collective-permute-start(bf16[7,128,1024]{2,1,0:T(8,128)(2,1)S(1)} %get-tuple-element.51), channel_id=1, source_target_pairs={{0,4},{4,0},{8,12},{12,8},{16,20},{20,16},{24,28},{28,24},{1,5},{5... | collective-permute-start | bytes 5505032 | tf_op jit(solution)/shard_map/ppermute | solution.py:32
  192.9 61.1 %collective-permute-start.28 = (bf16[7,128,512]{2,1,0:T(8,128)(2,1)S(1)}, bf16[7,128,512]{2,1,0:T(8,128)(2,1)S(1)}, u32[]{:S(2)}, u32[]{:S(2)}) collective-permute-start(bf16[7,128,512]{2,1,0:T(8,128)(2,1)S(1)} %term_2_1.1), channel_id=1, source_target_pairs={{0,8},{4,12},{8,0},{12,4},{16,24},{20,28},{24,16},{28,20},{1,9},{5... | collective-permute-start | bytes 2752520 | tf_op jit(solution)/shard_map/ppermute | solution.py:32
  211.9 59.3 %collective-permute-start.27 = (bf16[7,128,512]{2,1,0:T(8,128)(2,1)S(1)}, bf16[7,128,512]{2,1,0:T(8,128)(2,1)S(1)}, u32[]{:S(2)}, u32[]{:S(2)}) collective-permute-start(bf16[7,128,512]{2,1,0:T(8,128)(2,1)S(1)} %term_2_0.1), channel_id=1, source_target_pairs={{0,8},{4,12},{8,0},{12,4},{16,24},{20,28},{24,16},{28,20},{1,9},{5... | collective-permute-start | bytes 2752520 | tf_op jit(solution)/shard_map/ppermute | solution.py:32
  273.2 3.7 %collective-permute-start.30 = (f32[2,8,128]{2,1,0:T(8,128)S(1)}, f32[2,8,128]{2,1,0:T(8,128)S(1)}, u32[]{:S(2)}, u32[]{:S(2)}) collective-permute-start(f32[2,8,128]{2,1,0:T(8,128)S(1)} %fusion.12), channel_id=1, source_target_pairs={{0,2},{1,3},{2,0},{3,1},{4,6},{5,7},{6,4},{7,5},{8,10},{9,11},{10,... | collective-permute-start | bytes 24584 | tf_op jit(solution)/shard_map/ppermute | solution.py:32
  276.9 3.7 %collective-permute-start.31 = (f32[2,8,128]{2,1,0:T(8,128)S(1)}, f32[2,8,128]{2,1,0:T(8,128)S(1)}, u32[]{:S(2)}, u32[]{:S(2)}) collective-permute-start(f32[2,8,128]{2,1,0:T(8,128)S(1)} %fusion.15), channel_id=1, source_target_pairs={{0,4},{4,0},{8,12},{12,8},{16,20},{20,16},{24,28},{28,24},{1,5},{5... | collective-permute-start | bytes 24584 | tf_op jit(solution)/shard_map/ppermute | solution.py:32
  280.5 3.7 %collective-permute-start.32 = (f32[2,8,128]{2,1,0:T(8,128)S(1)}, f32[2,8,128]{2,1,0:T(8,128)S(1)}, u32[]{:S(2)}, u32[]{:S(2)}) collective-permute-start(f32[2,8,128]{2,1,0:T(8,128)S(1)} %add.143), channel_id=1, source_target_pairs={{0,8},{4,12},{8,0},{12,4},{16,24},{20,28},{24,16},{28,20},{1,9},{5... | collective-permute-start | bytes 24584 | tf_op jit(solution)/shard_map/ppermute | solution.py:32
  284.2 4.5 %collective-permute-start.33 = (f32[2,8,128]{2,1,0:T(8,128)S(1)}, f32[2,8,128]{2,1,0:T(8,128)S(1)}, u32[]{:S(2)}, u32[]{:S(2)}) collective-permute-start(f32[2,8,128]{2,1,0:T(8,128)S(1)} %add.144), channel_id=1, source_target_pairs={{0,16},{4,20},{8,24},{12,28},{16,0},{20,4},{24,8},{28,12},{1,17},{... | collective-permute-start | bytes 24584 | tf_op jit(solution)/shard_map/ppermute | solution.py:32
  (6 other events, 57.8 us)

commit v3 on v2

--- a/solution.py
+++ b/solution.py
@@ -14,6 +14,8 @@
 VMEM_LIMIT = 56 * 1024 * 1024
 SLACK = 4 * 1024 * 1024
 COST = 1000
+IN_CUT = 6
+OUT_CUT = 4
 
 VM = pl.BlockSpec(memory_space=pltpu.VMEM)
 SM = pl.BlockSpec(memory_space=pltpu.SMEM)
@@ -77,6 +79,13 @@
     return tuple(chunks)
 
 
+def columns(refs):
+    start = 0
+    for ref in refs:
+        yield ref, slice(start, start + ref.shape[-1])
+        start += ref.shape[-1]
+
+
 def share_rows(me, at, share):
     return pl.ds(pl.multiple_of((me ^ at) * share, share), share)
 
@@ -102,12 +111,9 @@
 
     def one(row_ref, c, mask, e, slot):
         row = rows_of(row_ref, c, me, ways)
-        wide = keys[mask][0].shape[-1]
         block = None
-        for i, key in enumerate(keys[mask]):
-            part = lax.dot_general(
-                row[:, i * wide : (i + 1) * wide], key[e], NT, preferred_element_type=jnp.float32
-            )
+        for key, at in columns(keys[mask]):
+            part = lax.dot_general(row[:, at], key[e], NT, preferred_element_type=jnp.float32)
             block = part if block is None else block + part
         for at in range(ways):
             (high if at % 2 else low)[at // 2, slot] = block[at * share : (at + 1) * share]
@@ -223,8 +229,7 @@
         came = refs[come_at : come_at + arrived]
         outs = refs[out_at : out_at + outputs]
         come_at, out_at = come_at + arrived, out_at + outputs
-        wide = outs[0].shape[-1]
-        span = wide * outputs
+        span = sum(out.shape[-1] for out in outs)
 
         def term(n, requester, slot, mask, c, e, fresh):
             w = whole_weights(pieces[n], order, slot)
@@ -234,9 +239,7 @@
 
         def query(n, requester, slot, mask, c, e, fresh):
             w = whole_weights(pieces[n], order, slot)
-            piece = keys[mask][0].shape[-1]
-            for i, key in enumerate(keys[mask]):
-                at = slice(i * piece, (i + 1) * piece)
+            for key, at in columns(keys[mask]):
                 part = lax.dot_general(w, key[e], NN, preferred_element_type=jnp.float32)
                 total[c, :, at] = part if fresh else total[c, :, at] + part
 
@@ -259,8 +262,8 @@
 
         @pl.loop(0, clusters)
         def _(c):
-            for i, out in enumerate(outs):
-                value = total[c, :, i * wide : (i + 1) * wide]
+            for out, at in columns(outs):
+                value = total[c, :, at]
                 for ref in came:
                     value = value + ref[c].astype(jnp.float32)
                 if kind == "term":
@@ -282,7 +285,6 @@
             if ref.shape == base.shape:
                 value = value + ref[c].astype(jnp.float32)
         sides = [ref for ref in parts if ref.shape != base.shape]
-        wide = out.shape[-1] // 2
         for i in range(0, len(sides), 2):
             pair = [ref[c].astype(jnp.float32) for ref in sides[i : i + 2]]
             value = value + jnp.concatenate(pair, axis=-1)
@@ -316,7 +318,8 @@
     rank = lax.axis_index("tensor").astype(jnp.int32).reshape(1)
     plans = layout(parts, clusters, cap)
 
-    halves = jnp.split(own_keys, 2, axis=-1)
+    cut = max(1, width * IN_CUT // 8 // CLUSTER) * CLUSTER
+    halves = jnp.split(own_keys, [cut], axis=-1)
     held = {}
     for bit in reversed(range(1, bits_of(parts))):
         first = swap(halves[0], "dp", 1 << bit)
@@ -416,10 +419,10 @@
         tasks, shapes, came = [], [], []
         for w in wanted:
             groups = tuple(g for g in found if w[1] == (g[1] if w[0] == "term" else g[2]))
-            lo, wide, outputs, add = w[2:] if w[0] == "term" else (0, width, 1, [])
+            lo, wides, add = w[2:] if w[0] == "term" else (0, (width,), [])
             kept = bf16 if w[1] else f32
-            tasks.append((w[0], groups, lo, len(add), outputs))
-            shapes += [jax.ShapeDtypeStruct(cube[:2] + (wide,), kept)] * outputs
+            tasks.append((w[0], groups, lo, len(add), len(wides)))
+            shapes += [jax.ShapeDtypeStruct(cube[:2] + (wide,), kept) for wide in wides]
             came += add
         splits = tuple((m, len(held[m])) for m in asked)
         return call(
@@ -433,21 +436,24 @@
     def lowest(m):
         return bits_of(m & -m) if m else bits_of(parts)
 
-    half = width // 2
-    odd = [m for m in range(3, parts, 2)]
-    lead = [("term", m, 0, half, 2, []) for m in odd] + [("query", 1)]
-    lead += [("term", 1, 0, width, 1, [])] if parts > 1 else []
-    made = gradients("grads_lead", lead)
-    terms = {m: made[2 * i : 2 * i + 2] for i, m in enumerate(odd)}
-    far_q, near = made[2 * len(odd)], made[2 * len(odd) + 1 :]
-    own_p, own_q = gradients("grads_own", [("term", 0, 0, width, 1, []), ("query", 0)], (far_q,))
+    cut = max(1, width * OUT_CUT // 8 // CLUSTER) * CLUSTER
+    halves = ((0, cut), (cut, width - cut))
+    odd = range(3, parts, 2)
+    terms, waits = {}, ()
+    if odd:
+        made = gradients("terms_far", [("term", m, 0, (cut, width - cut), []) for m in odd])
+        terms = {m: made[2 * i : 2 * i + 2] for i, m in enumerate(odd)}
+        waits = (made[0],)
+    lead = [("query", 1)] + ([("term", 1, 0, (width,), [])] if parts > 1 else [])
+    far_q, *near = gradients("grads_lead", lead, waits)
+    own_p, own_q = gradients("grads_own", [("term", 0, 0, (width,), []), ("query", 0)], (far_q,))
     came = []
     for m in sorted(range(2, parts, 2), key=lambda m: (lowest(m), -m)):
         came = [[swap(t, "dp", 1 << b) for t in terms[m | (1 << b)]] for b in range(lowest(m))]
         terms[m] = []
-        for i in range(2):
+        for i, (lo, wide) in enumerate(halves):
             add = [got[i] for got in came]
-            terms[m] += gradients(f"term_{m}_{i}", [("term", m, i * half, half, 1, add)])
+            terms[m] += gradients(f"term_{m}_{i}", [("term", m, lo, (wide,), add)])
     if near:
         if came:
             near = [lax.optimization_barrier((near[0], came[0][-1]))[0]]

time: 295 us -> 287 us (0.973)
  waiting for transfers between devices: 199 us -> 190 us
    ppermute x34, waiting for transfers between devices: 199 us -> 190 us  [swap(): return lax.ppermute(value, axis, [(i, i ^ mask) for i in range(size)])]
    pallas_call x11 -> x12, Pallas kernels: 49.7 us -> 50.6 us  [call(): pl.pallas_call(body, name=name, out_shape=out_shape, in_specs=[SM] * smem...]
  transfers between devices with their start and end apart: 34 -> 34, of which waited for: 21 -> 20; matrix products, arithmetic and copies ran while one was open for 2% -> 2% of each run, Pallas kernels for 12% -> 15%
where the time goes in v3:
time: 287 us; the launch traced here: 286 us
  waiting for transfers between devices  190 us (66%)
  Pallas kernels  50.6 us (18%)
  starting transfers between devices  31.1 us (11%)
  local copies, waits for them, and re-layouts  6.98 us (2%)
  other arithmetic  4.26 us (1%)
  between operations  3.39 us (1%)
    ppermute x34, waiting for transfers between devices, swap(): return lax.ppermute(value, axis, [(i, i ^ mask) for i in range(size)])  190 us
    pallas_call x12, Pallas kernels, call(): pl.pallas_call(body, name=name, out_shape=out_shape, in_specs=[SM] * smem...  50.6 us
    ppermute x34, starting transfers between devices, swap(): return lax.ppermute(value, axis, [(i, i ^ mask) for i in range(size)])  31.1 us
  transfers between devices with their start and end apart: 34, of which 20 were waited for; matrix products, arithmetic and copies ran while one was open for 2% of the time, Pallas kernels for 15%

profile of v3, /device:TPU:0, one launch (start us, length us, event | category | flops | bytes accessed | tf_op | source)
XLA Modules:
  0.0 286.3 jit_solution(5032567613620232204)
XLA Ops:
  0.6 3.0 %collective-permute-start.2 = (bf16[7,128,1024]{2,1,0:T(8,128)(2,1)}, bf16[7,128,1024]{2,1,0:T(8,128)(2,1)}, u32[]{:S(2)}, u32[]{:S(2)}) collective-permute-start(bf16[7,128,1024]{2,1,0:T(8,128)(2,1)} %bitcast.56), channel_id=1, source_target_pairs={{0,4},{4,0},{8,12},{12,8},{16,20},{20,16},{24,28},{28,24},{1,5},{5... | collective-permute-start | bytes 5505032 | tf_op jit(solution)/shard_map/ppermute | solution.py:34
  3.7 2.6 collective-permute-start
  6.3 2.5 split.8
  11.3 1.8 split.9
  13.4 54.3 %collective-permute-done.3.refs_7_ = bf16[7,128,768]{2,1,0:T(8,128)(2,1)S(1)} collective-permute-done((bf16[7,128,768]{2,1,0:T(8,128)(2,1)}, bf16[7,128,768]{2,1,0:T(8,128)(2,1)S(1)}, u32[]{:S(2)}, u32[]{:S(2)}) %collective-permute-start.3) | collective-permute-done | bytes 1376288 | tf_op jit(solution)/shard_map/ppermute | solution.py:34
  70.0 5.5 %logits_0.1 = (f32[2,21,32,128]{3,2,1,0:T(8,128)S(1)}, f32[2,21,32,128]{3,2,1,0:T(8,128)S(1)}, f32[8,128]{1,0:T(8,128)S(1)}) custom-call(s32[28]{0:T(128)S(1)} %select_reduce_fusion.3.refs_0_.refs_1_, s32[28]{0:T(128)S(1)} %select_reduce_fusion.3.refs_0_.refs_1_, s32[1]{0:T(128)} %bitcast.refs_2_, bf16[7,128,1024]{2,1,0:T(8,128)(2,1)S(1)} %bitcast.48, ...), custom_call_target="tpu_custom_call" | custom-call | flops 704643 | bytes 6885 | tf_op jit(solution)/shard_map/logits_0/pallas_call | solution.py:49
  75.7 13.1 %collective-permute-done.4.refs_8_ = bf16[7,128,256]{2,1,0:T(8,128)(2,1)S(1)} collective-permute-done((bf16[7,128,256]{2,1,0:T(8,128)(2,1)}, bf16[7,128,256]{2,1,0:T(8,128)(2,1)S(1)}, u32[]{:S(2)}, u32[]{:S(2)}) %collective-permute-start.4) | collective-permute-done | bytes 458784 | tf_op jit(solution)/shard_map/ppermute | solution.py:34
  88.7 2.9 %collective-permute-done.1.refs_4_ = bf16[7,128,1024]{2,1,0:T(8,128)(2,1)} collective-permute-done((bf16[7,128,1024]{2,1,0:T(8,128)(2,1)S(1)}, bf16[7,128,1024]{2,1,0:T(8,128)(2,1)}, u32[]{:S(2)}, u32[]{:S(2)}) %collective-permute-start.1) | collective-permute-done | bytes 1835040 | tf_op jit(solution)/shard_map/ppermute | solution.py:34
  91.6 5.2 %logits_1.1 = (f32[2,28,32,128]{3,2,1,0:T(8,128)S(1)}, f32[2,28,32,128]{3,2,1,0:T(8,128)S(1)}, f32[8,128]{1,0:T(8,128)S(1)}) custom-call(s32[28]{0:T(128)S(1)} %select_reduce_fusion.3.refs_0_.refs_1_, s32[28]{0:T(128)S(1)} %select_reduce_fusion.2.refs_1_, s32[1]{0:T(128)} %bitcast.refs_2_, bf16[7,128,1024]{2,1,0:T(8,128)(2,1)S(1)} %bitcast.49, ...), custom_call_target="tpu_custom_call" | custom-call | flops 939524 | bytes 11014 | tf_op jit(solution)/shard_map/logits_1/pallas_call | solution.py:49
  99.2 10.7 %collective-permute-done.6.refs_6_.refs_10_ = bf16[7,128,256]{2,1,0:T(8,128)(2,1)S(1)} collective-permute-done((bf16[7,128,256]{2,1,0:T(8,128)(2,1)S(1)}, bf16[7,128,256]{2,1,0:T(8,128)(2,1)S(1)}, u32[]{:S(2)}, u32[]{:S(2)}) %collective-permute-start.6) | collective-permute-done | bytes 458784 | tf_op jit(solution)/shard_map/ppermute | solution.py:34
  109.9 4.1 %logits_2.1 = (f32[2,14,32,128]{3,2,1,0:T(8,128)S(1)}, f32[2,14,32,128]{3,2,1,0:T(8,128)S(1)}, f32[8,128]{1,0:T(8,128)}) custom-call(s32[28]{0:T(128)S(1)} %select_reduce_fusion.3.refs_0_.refs_1_, s32[28]{0:T(128)S(1)} %select_reduce_fusion.2.refs_1_, s32[1]{0:T(128)} %bitcast.refs_2_, bf16[7,128,1024]{2,1,0:T(8,128)(2,1)S(1)} %bitcast.50, ...), custom_call_target="tpu_custom_call" | custom-call | flops 469762 | bytes 6426 | tf_op jit(solution)/shard_map/logits_2/pallas_call | solution.py:49
  117.4 10.2 %collective-permute-done.10 = f32[1,28,32,128]{3,2,1,0:T(8,128)S(1)} collective-permute-done((f32[1,28,32,128]{3,2,1,0:T(8,128)S(1)}, f32[1,28,32,128]{3,2,1,0:T(8,128)S(1)}, u32[]{:S(2)}, u32[]{:S(2)}) %collective-permute-start.10) | collective-permute-done | bytes 458784 | tf_op jit(solution)/shard_map/ppermute | solution.py:34
  127.6 4.5 %collective-permute-done.12 = f32[1,14,32,128]{3,2,1,0:T(8,128)S(1)} collective-permute-done((f32[1,14,32,128]{3,2,1,0:T(8,128)S(1)}, f32[1,14,32,128]{3,2,1,0:T(8,128)S(1)}, u32[]{:S(2)}, u32[]{:S(2)}) %collective-permute-start.12) | collective-permute-done | bytes 229408 | tf_op jit(solution)/shard_map/ppermute | solution.py:34
  133.8 4.0 %collective-permute-start.13 = (f32[32,128]{1,0:T(8,128)S(1)}, f32[32,128]{1,0:T(8,128)S(1)}, u32[]{:S(2)}, u32[]{:S(2)}) collective-permute-start(f32[32,128]{1,0:T(8,128)S(1)} %row_stats.1.refs_3_), channel_id=1, source_target_pairs={{0,16},{4,20},{8,24},{12,28},{16,0},{20,4},{24,8},{28,12},{1,17},{... | collective-permute-start | bytes 49160 | tf_op jit(solution)/shard_map/ppermute | solution.py:34
  139.5 1.9 weights.1
  143.0 3.3 %collective-permute-done.20.refs_6_.refs_20_ = bf16[14,32,128]{2,1,0:T(8,128)(2,1)S(1)} collective-permute-done((bf16[14,32,128]{2,1,0:T(8,128)(2,1)S(1)}, bf16[14,32,128]{2,1,0:T(8,128)(2,1)S(1)}, u32[]{:S(2)}, u32[]{:S(2)}) %collective-permute-start.20) | collective-permute-done | bytes 114720 | tf_op jit(solution)/shard_map/ppermute | solution.py:34
  147.6 4.2 %terms_far.1 = (bf16[7,128,512]{2,1,0:T(8,128)(2,1)S(1)}, bf16[7,128,512]{2,1,0:T(8,128)(2,1)S(1)}) custom-call(s32[28]{0:T(128)S(1)} %select_reduce_fusion.3.refs_0_.refs_1_, s32[28]{0:T(128)S(1)} %select_reduce_fusion.2.refs_1_, s32[1]{0:T(128)} %bitcast.refs_2_, bf16[7,128,1024]{2,1,0:T(8,128)(2,1)S(1)} %bitcast.51, ...), custom_call_target="tpu_custom_call" | custom-call | flops 234881 | bytes 5963 | tf_op jit(solution)/shard_map/terms_far/pallas_call | solution.py:49
  154.6 6.5 %collective-permute-done.17.refs_16_.refs_6_ = bf16[28,32,128]{2,1,0:T(8,128)(2,1)S(1)} collective-permute-done((bf16[28,32,128]{2,1,0:T(8,128)(2,1)S(1)}, bf16[28,32,128]{2,1,0:T(8,128)(2,1)S(1)}, u32[]{:S(2)}, u32[]{:S(2)}) %collective-permute-start.17) | collective-permute-done | bytes 229408 | tf_op jit(solution)/shard_map/ppermute | solution.py:34
  161.6 2.1 collective-permute-done.14.refs_12_
  165.0 8.2 %grads_lead.1 = (bf16[7,128,1024]{2,1,0:T(8,128)(2,1)S(1)}, bf16[7,128,1024]{2,1,0:T(8,128)(2,1)S(1)}) custom-call(s32[28]{0:T(128)S(1)} %select_reduce_fusion.3.refs_0_.refs_1_, s32[28]{0:T(128)S(1)} %select_reduce_fusion.2.refs_1_, s32[1]{0:T(128)} %bitcast.refs_2_, bf16[7,128,1024]{2,1,0:T(8,128)(2,1)S(1)} %bitcast.52, ...), custom_call_target="tpu_custom_call" | custom-call | flops 469762 | bytes 16744 | tf_op jit(solution)/shard_map/grads_lead/pallas_call | solution.py:49
  173.3 3.0 %collective-permute-start.23 = (bf16[7,128,1024]{2,1,0:T(8,128)(2,1)S(1)}, bf16[7,128,1024]{2,1,0:T(8,128)(2,1)S(1)}, u32[]{:S(2)}, u32[]{:S(2)}) collective-permute-start(bf16[7,128,1024]{2,1,0:T(8,128)(2,1)S(1)} %get-tuple-element.44.refs_23_), channel_id=1, source_target_pairs={{0,16},{4,20},{8,24},{12,28},{16,0},{20,4},{24,8},{28,12},{1,17},{... | collective-permute-start | bytes 5505032 | tf_op jit(solution)/shard_map/ppermute | solution.py:34
  178.3 3.6 %term_2_1.1 = bf16[7,128,512]{2,1,0:T(8,128)(2,1)S(1)} custom-call(s32[28]{0:T(128)S(1)} %select_reduce_fusion.3.refs_0_.refs_1_, s32[28]{0:T(128)S(1)} %select_reduce_fusion.2.refs_1_, s32[1]{0:T(128)} %bitcast.refs_2_, bf16[7,128,1024]{2,1,0:T(8,128)(2,1)S(1)} %bitcast.53, bf16[7,128,1024]{2,1,0:T(8,128)(2,1)} %collective-permute-done.1.refs_4_, ...), custom_call_target="tpu_custom_call" | custom-call | flops 234881 | bytes 6422 | tf_op jit(solution)/shard_map/term_2_1/pallas_call | solution.py:49
  182.4 17.1 %collective-permute-done.26.refs_9_ = bf16[7,128,512]{2,1,0:T(8,128)(2,1)S(1)} collective-permute-done((bf16[7,128,512]{2,1,0:T(8,128)(2,1)S(1)}, bf16[7,128,512]{2,1,0:T(8,128)(2,1)S(1)}, u32[]{:S(2)}, u32[]{:S(2)}) %collective-permute-start.26) | collective-permute-done | bytes 917536 | tf_op jit(solution)/shard_map/ppermute | solution.py:34
  199.5 3.6 %term_2_0.1 = bf16[7,128,512]{2,1,0:T(8,128)(2,1)S(1)} custom-call(s32[28]{0:T(128)S(1)} %select_reduce_fusion.3.refs_0_.refs_1_, s32[28]{0:T(128)S(1)} %select_reduce_fusion.2.refs_1_, s32[1]{0:T(128)} %bitcast.refs_2_, bf16[7,128,1024]{2,1,0:T(8,128)(2,1)S(1)} %bitcast.54, bf16[7,128,1024]{2,1,0:T(8,128)(2,1)} %collective-permute-done.1.refs_4_, ...), custom_call_target="tpu_custom_call" | custom-call | flops 234881 | bytes 6422 | tf_op jit(solution)/shard_map/term_2_0/pallas_call | solution.py:49
  203.6 11.1 %grads_own.1 = (f32[7,128,1024]{2,1,0:T(8,128)S(1)}, f32[7,128,1024]{2,1,0:T(8,128)S(1)}) custom-call(s32[28]{0:T(128)S(1)} %select_reduce_fusion.3.refs_0_.refs_1_, s32[28]{0:T(128)S(1)} %select_reduce_fusion.2.refs_1_, s32[1]{0:T(128)} %bitcast.refs_2_, bf16[7,128,1024]{2,1,0:T(8,128)(2,1)S(1)} %bitcast.55, ...), custom_call_target="tpu_custom_call" | custom-call | flops 469762 | bytes 20414 | tf_op jit(solution)/shard_map/grads_own/pallas_call | solution.py:49
  214.8 41.1 %collective-permute-done.23.refs_2_ = bf16[7,128,1024]{2,1,0:T(8,128)(2,1)S(1)} collective-permute-done((bf16[7,128,1024]{2,1,0:T(8,128)(2,1)S(1)}, bf16[7,128,1024]{2,1,0:T(8,128)(2,1)S(1)}, u32[]{:S(2)}, u32[]{:S(2)}) %collective-permute-start.23) | collective-permute-done | bytes 1835040 | tf_op jit(solution)/shard_map/ppermute | solution.py:34
  256.5 6.1 %collective-permute-done.27.refs_3_ = bf16[7,128,512]{2,1,0:T(8,128)(2,1)S(1)} collective-permute-done((bf16[7,128,512]{2,1,0:T(8,128)(2,1)S(1)}, bf16[7,128,512]{2,1,0:T(8,128)(2,1)S(1)}, u32[]{:S(2)}, u32[]{:S(2)}) %collective-permute-start.27) | collective-permute-done | bytes 917536 | tf_op jit(solution)/shard_map/ppermute | solution.py:34
  266.0 2.3 collective-permute-done.30
  269.7 2.3 collective-permute-done.31
  271.9 3.6 %collective-permute-done.32 = f32[2,8,128]{2,1,0:T(8,128)S(1)} collective-permute-done((f32[2,8,128]{2,1,0:T(8,128)S(1)}, f32[2,8,128]{2,1,0:T(8,128)S(1)}, u32[]{:S(2)}, u32[]{:S(2)}) %collective-permute-start.32) | collective-permute-done | bytes 8224 | tf_op jit(solution)/shard_map/ppermute | solution.py:34
  275.6 4.5 %collective-permute-done.33 = f32[2,8,128]{2,1,0:T(8,128)S(1)} collective-permute-done((f32[2,8,128]{2,1,0:T(8,128)S(1)}, f32[2,8,128]{2,1,0:T(8,128)S(1)}, u32[]{:S(2)}, u32[]{:S(2)}) %collective-permute-start.33) | collective-permute-done | bytes 8224 | tf_op jit(solution)/shard_map/ppermute | solution.py:34
  282.2 3.0 %multiply_convert_fusion = (bf16[7,128,1024]{2,1,0:T(8,128)(2,1)}, bf16[7,128,1024]{2,1,0:T(8,128)(2,1)}) fusion(f32[7,128,1024]{2,1,0:T(8,128)S(1)} %get-tuple-element.54, f32[]{:T(128)} %bitcast.18, f32[7,128,1024]{2,1,0:T(8,128)S(1)} %get-tuple-element.46), kind=kLoop, calls=%fused_computation | loop fusion | flops 3670016 | bytes 11010052 | tf_op jit(solution)/shard_map/convert_element_type | solution.py:478
  (95 shorter events, 31.2 us)
Async XLA Ops:
  0.6 67.8 %collective-permute-start.2 = (bf16[7,128,1024]{2,1,0:T(8,128)(2,1)}, bf16[7,128,1024]{2,1,0:T(8,128)(2,1)}, u32[]{:S(2)}, u32[]{:S(2)}) collective-permute-start(bf16[7,128,1024]{2,1,0:T(8,128)(2,1)} %bitcast.56), channel_id=1, source_target_pairs={{0,4},{4,0},{8,12},{12,8},{16,20},{20,16},{24,28},{28,24},{1,5},{5... | collective-permute-start | bytes 5505032 | tf_op jit(solution)/shard_map/ppermute | solution.py:34
  3.7 9.4 %collective-permute-start = (s32[7,8]{1,0:T(8,128)}, s32[7,8]{1,0:T(8,128)S(1)}, u32[]{:S(2)}, u32[]{:S(2)}) collective-permute-start(s32[7,8]{1,0:T(8,128)} %param.5), channel_id=1, source_target_pairs={{0,16},{4,20},{8,24},{12,28},{16,0},{20,4},{24,8},{28,12},{1,17},{... | collective-permute-start | bytes 680 | tf_op jit(solution)/shard_map/ppermute | solution.py:34
  8.8 58.9 %collective-permute-start.3 = (bf16[7,128,768]{2,1,0:T(8,128)(2,1)}, bf16[7,128,768]{2,1,0:T(8,128)(2,1)S(1)}, u32[]{:S(2)}, u32[]{:S(2)}) collective-permute-start(bf16[7,128,768]{2,1,0:T(8,128)(2,1)} %split.8), channel_id=1, source_target_pairs={{0,8},{4,12},{8,0},{12,4},{16,24},{20,28},{24,16},{28,20},{1,9},{5... | collective-permute-start | bytes 4128776 | tf_op jit(solution)/shard_map/ppermute | solution.py:34
  10.4 81.3 %collective-permute-start.1 = (bf16[7,128,1024]{2,1,0:T(8,128)(2,1)S(1)}, bf16[7,128,1024]{2,1,0:T(8,128)(2,1)}, u32[]{:S(2)}, u32[]{:S(2)}) collective-permute-start(bf16[7,128,1024]{2,1,0:T(8,128)(2,1)S(1)} %bitcast.47), channel_id=1, source_target_pairs={{0,16},{4,20},{8,24},{12,28},{16,0},{20,4},{24,8},{28,12},{1,17},{... | collective-permute-start | bytes 5505032 | tf_op jit(solution)/shard_map/ppermute | solution.py:34
  67.7 21.1 %collective-permute-start.4 = (bf16[7,128,256]{2,1,0:T(8,128)(2,1)}, bf16[7,128,256]{2,1,0:T(8,128)(2,1)S(1)}, u32[]{:S(2)}, u32[]{:S(2)}) collective-permute-start(bf16[7,128,256]{2,1,0:T(8,128)(2,1)} %split.9), channel_id=1, source_target_pairs={{0,8},{4,12},{8,0},{12,4},{16,24},{20,28},{24,16},{28,20},{1,9},{5... | collective-permute-start | bytes 1376264 | tf_op jit(solution)/shard_map/ppermute | solution.py:34
  67.7 42.2 %collective-permute-start.5 = (bf16[7,128,768]{2,1,0:T(8,128)(2,1)S(1)}, bf16[7,128,768]{2,1,0:T(8,128)(2,1)S(1)}, u32[]{:S(2)}, u32[]{:S(2)}) collective-permute-start(bf16[7,128,768]{2,1,0:T(8,128)(2,1)S(1)} %collective-permute-done.3.refs_7_), channel_id=1, source_target_pairs={{0,4},{4,0},{8,12},{12,8},{16,20},{20,16},{24,28},{28,24},{1,5},{5... | collective-permute-start | bytes 4128776 | tf_op jit(solution)/shard_map/ppermute | solution.py:34
  75.5 22.0 %collective-permute-start.7 = (f32[2,21,32,128]{3,2,1,0:T(8,128)S(1)}, f32[2,21,32,128]{3,2,1,0:T(8,128)S(1)}, u32[]{:S(2)}, u32[]{:S(2)}) collective-permute-start(f32[2,21,32,128]{3,2,1,0:T(8,128)S(1)} %get-tuple-element.34), channel_id=1, source_target_pairs={{0,1},{1,0},{2,3},{3,2},{4,5},{5,4},{6,7},{7,6},{8,9},{9,8},{10,11... | collective-permute-start | bytes 2064392 | tf_op jit(solution)/shard_map/ppermute | solution.py:34
  96.9 17.1 %collective-permute-start.9 = (f32[2,28,32,128]{3,2,1,0:T(8,128)S(1)}, f32[2,28,32,128]{3,2,1,0:T(8,128)S(1)}, u32[]{:S(2)}, u32[]{:S(2)}) collective-permute-start(f32[2,28,32,128]{3,2,1,0:T(8,128)S(1)} %get-tuple-element.36), channel_id=1, source_target_pairs={{0,1},{1,0},{2,3},{3,2},{4,5},{5,4},{6,7},{7,6},{8,9},{9,8},{10,11... | collective-permute-start | bytes 2752520 | tf_op jit(solution)/shard_map/ppermute | solution.py:34
  96.9 12.9 %collective-permute-start.6 = (bf16[7,128,256]{2,1,0:T(8,128)(2,1)S(1)}, bf16[7,128,256]{2,1,0:T(8,128)(2,1)S(1)}, u32[]{:S(2)}, u32[]{:S(2)}) collective-permute-start(bf16[7,128,256]{2,1,0:T(8,128)(2,1)S(1)} %collective-permute-done.4.refs_8_), channel_id=1, source_target_pairs={{0,4},{4,0},{8,12},{12,8},{16,20},{20,16},{24,28},{28,24},{1,5},{5... | collective-permute-start | bytes 1376264 | tf_op jit(solution)/shard_map/ppermute | solution.py:34
  97.7 18.0 %collective-permute-start.8 = (f32[1,21,32,128]{3,2,1,0:T(8,128)S(1)}, f32[1,21,32,128]{3,2,1,0:T(8,128)S(1)}, u32[]{:S(2)}, u32[]{:S(2)}) collective-permute-start(f32[1,21,32,128]{3,2,1,0:T(8,128)S(1)} %slice_bitcast_fusion.2), channel_id=1, source_target_pairs={{0,2},{1,3},{2,0},{3,1},{4,6},{5,7},{6,4},{7,5},{8,10},{9,11},{10,... | collective-permute-start | bytes 1032200 | tf_op jit(solution)/shard_map/ppermute | solution.py:34
  113.9 1.8 collective-permute-start.11
  114.2 13.4 %collective-permute-start.10 = (f32[1,28,32,128]{3,2,1,0:T(8,128)S(1)}, f32[1,28,32,128]{3,2,1,0:T(8,128)S(1)}, u32[]{:S(2)}, u32[]{:S(2)}) collective-permute-start(f32[1,28,32,128]{3,2,1,0:T(8,128)S(1)} %slice_bitcast_fusion), channel_id=1, source_target_pairs={{0,2},{1,3},{2,0},{3,1},{4,6},{5,7},{6,4},{7,5},{8,10},{9,11},{10,... | collective-permute-start | bytes 1376264 | tf_op jit(solution)/shard_map/ppermute | solution.py:34
  115.9 16.2 %collective-permute-start.12 = (f32[1,14,32,128]{3,2,1,0:T(8,128)S(1)}, f32[1,14,32,128]{3,2,1,0:T(8,128)S(1)}, u32[]{:S(2)}, u32[]{:S(2)}) collective-permute-start(f32[1,14,32,128]{3,2,1,0:T(8,128)S(1)} %slice_bitcast_fusion.4), channel_id=1, source_target_pairs={{0,2},{1,3},{2,0},{3,1},{4,6},{5,7},{6,4},{7,5},{8,10},{9,11},{10,... | collective-permute-start | bytes 688136 | tf_op jit(solution)/shard_map/ppermute | solution.py:34
  133.8 5.7 %collective-permute-start.13 = (f32[32,128]{1,0:T(8,128)S(1)}, f32[32,128]{1,0:T(8,128)S(1)}, u32[]{:S(2)}, u32[]{:S(2)}) collective-permute-start(f32[32,128]{1,0:T(8,128)S(1)} %row_stats.1.refs_3_), channel_id=1, source_target_pairs={{0,16},{4,20},{8,24},{12,28},{16,0},{20,4},{24,8},{28,12},{1,17},{... | collective-permute-start | bytes 49160 | tf_op jit(solution)/shard_map/ppermute | solution.py:34
  141.4 4.9 %collective-permute-start.20 = (bf16[14,32,128]{2,1,0:T(8,128)(2,1)S(1)}, bf16[14,32,128]{2,1,0:T(8,128)(2,1)S(1)}, u32[]{:S(2)}, u32[]{:S(2)}) collective-permute-start(bf16[14,32,128]{2,1,0:T(8,128)(2,1)S(1)} %get-tuple-element.42.refs_5_.refs_19_), channel_id=1, source_target_pairs={{0,2},{1,3},{2,0},{3,1},{4,6},{5,7},{6,4},{7,5},{8,10},{9,11},{10,... | collective-permute-start | bytes 344072 | tf_op jit(solution)/shard_map/ppermute | solution.py:34
  143.0 3.3 %collective-permute-start.21 = (bf16[14,32,128]{2,1,0:T(8,128)(2,1)S(1)}, bf16[14,32,128]{2,1,0:T(8,128)(2,1)S(1)}, u32[]{:S(2)}, u32[]{:S(2)}) collective-permute-start(bf16[14,32,128]{2,1,0:T(8,128)(2,1)S(1)} %get-tuple-element.42.refs_5_.refs_19_), channel_id=1, source_target_pairs={{0,1},{1,0},{2,3},{3,2},{4,5},{5,4},{6,7},{7,6},{8,9},{9,8},{10,11... | collective-permute-start | bytes 344072 | tf_op jit(solution)/shard_map/ppermute | solution.py:34
  151.8 25.8 %collective-permute-start.24 = (bf16[7,128,512]{2,1,0:T(8,128)(2,1)S(1)}, bf16[7,128,512]{2,1,0:T(8,128)(2,1)S(1)}, u32[]{:S(2)}, u32[]{:S(2)}) collective-permute-start(bf16[7,128,512]{2,1,0:T(8,128)(2,1)S(1)} %get-tuple-element.51), channel_id=1, source_target_pairs={{0,4},{4,0},{8,12},{12,8},{16,20},{20,16},{24,28},{28,24},{1,5},{5... | collective-permute-start | bytes 2752520 | tf_op jit(solution)/shard_map/ppermute | solution.py:34
  152.6 8.5 %collective-permute-start.17 = (bf16[28,32,128]{2,1,0:T(8,128)(2,1)S(1)}, bf16[28,32,128]{2,1,0:T(8,128)(2,1)S(1)}, u32[]{:S(2)}, u32[]{:S(2)}) collective-permute-start(bf16[28,32,128]{2,1,0:T(8,128)(2,1)S(1)} %get-tuple-element.41.refs_15_.refs_5_), channel_id=1, source_target_pairs={{0,2},{1,3},{2,0},{3,1},{4,6},{5,7},{6,4},{7,5},{8,10},{9,11},{10,... | collective-permute-start | bytes 688136 | tf_op jit(solution)/shard_map/ppermute | solution.py:34
  153.9 9.7 %collective-permute-start.14 = (bf16[21,32,128]{2,1,0:T(8,128)(2,1)S(1)}, bf16[21,32,128]{2,1,0:T(8,128)(2,1)S(1)}, u32[]{:S(2)}, u32[]{:S(2)}) collective-permute-start(bf16[21,32,128]{2,1,0:T(8,128)(2,1)S(1)} %get-tuple-element.40.refs_11_), channel_id=1, source_target_pairs={{0,2},{1,3},{2,0},{3,1},{4,6},{5,7},{6,4},{7,5},{8,10},{9,11},{10,... | collective-permute-start | bytes 516104 | tf_op jit(solution)/shard_map/ppermute | solution.py:34
  154.6 9.0 %collective-permute-start.18 = (bf16[28,32,128]{2,1,0:T(8,128)(2,1)S(1)}, bf16[28,32,128]{2,1,0:T(8,128)(2,1)S(1)}, u32[]{:S(2)}, u32[]{:S(2)}) collective-permute-start(bf16[28,32,128]{2,1,0:T(8,128)(2,1)S(1)} %get-tuple-element.41.refs_15_.refs_5_), channel_id=1, source_target_pairs={{0,1},{1,0},{2,3},{3,2},{4,5},{5,4},{6,7},{7,6},{8,9},{9,8},{10,11... | collective-permute-start | bytes 688136 | tf_op jit(solution)/shard_map/ppermute | solution.py:34
  161.0 4.0 %collective-permute-start.19 = (bf16[28,32,128]{2,1,0:T(8,128)(2,1)S(1)}, bf16[28,32,128]{2,1,0:T(8,128)(2,1)S(1)}, u32[]{:S(2)}, u32[]{:S(2)}) collective-permute-start(bf16[28,32,128]{2,1,0:T(8,128)(2,1)S(1)} %collective-permute-done.17.refs_16_.refs_6_), channel_id=1, source_target_pairs={{0,1},{1,0},{2,3},{3,2},{4,5},{5,4},{6,7},{7,6},{8,9},{9,8},{10,11... | collective-permute-start | bytes 688136 | tf_op jit(solution)/shard_map/ppermute | solution.py:34
  161.0 2.6 collective-permute-start.15
  163.6 1.4 collective-permute-start.16
  173.3 82.6 %collective-permute-start.23 = (bf16[7,128,1024]{2,1,0:T(8,128)(2,1)S(1)}, bf16[7,128,1024]{2,1,0:T(8,128)(2,1)S(1)}, u32[]{:S(2)}, u32[]{:S(2)}) collective-permute-start(bf16[7,128,1024]{2,1,0:T(8,128)(2,1)S(1)} %get-tuple-element.44.refs_23_), channel_id=1, source_target_pairs={{0,16},{4,20},{8,24},{12,28},{16,0},{20,4},{24,8},{28,12},{1,17},{... | collective-permute-start | bytes 5505032 | tf_op jit(solution)/shard_map/ppermute | solution.py:34
  176.3 23.2 %collective-permute-start.26 = (bf16[7,128,512]{2,1,0:T(8,128)(2,1)S(1)}, bf16[7,128,512]{2,1,0:T(8,128)(2,1)S(1)}, u32[]{:S(2)}, u32[]{:S(2)}) collective-permute-start(bf16[7,128,512]{2,1,0:T(8,128)(2,1)S(1)} %get-tuple-element.43.refs_23_), channel_id=1, source_target_pairs={{0,4},{4,0},{8,12},{12,8},{16,20},{20,16},{24,28},{28,24},{1,5},{5... | collective-permute-start | bytes 2752520 | tf_op jit(solution)/shard_map/ppermute | solution.py:34
  177.6 84.9 %collective-permute-start.25 = (bf16[7,128,1024]{2,1,0:T(8,128)(2,1)S(1)}, bf16[7,128,1024]{2,1,0:T(8,128)(2,1)S(1)}, u32[]{:S(2)}, u32[]{:S(2)}) collective-permute-start(bf16[7,128,1024]{2,1,0:T(8,128)(2,1)S(1)} %get-tuple-element.52), channel_id=1, source_target_pairs={{0,4},{4,0},{8,12},{12,8},{16,20},{20,16},{24,28},{28,24},{1,5},{5... | collective-permute-start | bytes 5505032 | tf_op jit(solution)/shard_map/ppermute | solution.py:34
  181.9 74.6 %collective-permute-start.28 = (bf16[7,128,512]{2,1,0:T(8,128)(2,1)S(1)}, bf16[7,128,512]{2,1,0:T(8,128)(2,1)S(1)}, u32[]{:S(2)}, u32[]{:S(2)}) collective-permute-start(bf16[7,128,512]{2,1,0:T(8,128)(2,1)S(1)} %term_2_1.1), channel_id=1, source_target_pairs={{0,8},{4,12},{8,0},{12,4},{16,24},{20,28},{24,16},{28,20},{1,9},{5... | collective-permute-start | bytes 2752520 | tf_op jit(solution)/shard_map/ppermute | solution.py:34
  203.1 59.4 %collective-permute-start.27 = (bf16[7,128,512]{2,1,0:T(8,128)(2,1)S(1)}, bf16[7,128,512]{2,1,0:T(8,128)(2,1)S(1)}, u32[]{:S(2)}, u32[]{:S(2)}) collective-permute-start(bf16[7,128,512]{2,1,0:T(8,128)(2,1)S(1)} %term_2_0.1), channel_id=1, source_target_pairs={{0,8},{4,12},{8,0},{12,4},{16,24},{20,28},{24,16},{28,20},{1,9},{5... | collective-permute-start | bytes 2752520 | tf_op jit(solution)/shard_map/ppermute | solution.py:34
  264.6 3.7 %collective-permute-start.30 = (f32[2,8,128]{2,1,0:T(8,128)S(1)}, f32[2,8,128]{2,1,0:T(8,128)S(1)}, u32[]{:S(2)}, u32[]{:S(2)}) collective-permute-start(f32[2,8,128]{2,1,0:T(8,128)S(1)} %fusion.12), channel_id=1, source_target_pairs={{0,2},{1,3},{2,0},{3,1},{4,6},{5,7},{6,4},{7,5},{8,10},{9,11},{10,... | collective-permute-start | bytes 24584 | tf_op jit(solution)/shard_map/ppermute | solution.py:34
  268.3 3.7 %collective-permute-start.31 = (f32[2,8,128]{2,1,0:T(8,128)S(1)}, f32[2,8,128]{2,1,0:T(8,128)S(1)}, u32[]{:S(2)}, u32[]{:S(2)}) collective-permute-start(f32[2,8,128]{2,1,0:T(8,128)S(1)} %fusion.14), channel_id=1, source_target_pairs={{0,4},{4,0},{8,12},{12,8},{16,20},{20,16},{24,28},{28,24},{1,5},{5... | collective-permute-start | bytes 24584 | tf_op jit(solution)/shard_map/ppermute | solution.py:34
  271.9 3.7 %collective-permute-start.32 = (f32[2,8,128]{2,1,0:T(8,128)S(1)}, f32[2,8,128]{2,1,0:T(8,128)S(1)}, u32[]{:S(2)}, u32[]{:S(2)}) collective-permute-start(f32[2,8,128]{2,1,0:T(8,128)S(1)} %add.143), channel_id=1, source_target_pairs={{0,8},{4,12},{8,0},{12,4},{16,24},{20,28},{24,16},{28,20},{1,9},{5... | collective-permute-start | bytes 24584 | tf_op jit(solution)/shard_map/ppermute | solution.py:34
  275.6 4.5 %collective-permute-start.33 = (f32[2,8,128]{2,1,0:T(8,128)S(1)}, f32[2,8,128]{2,1,0:T(8,128)S(1)}, u32[]{:S(2)}, u32[]{:S(2)}) collective-permute-start(f32[2,8,128]{2,1,0:T(8,128)S(1)} %add.144), channel_id=1, source_target_pairs={{0,16},{4,20},{8,24},{12,28},{16,0},{20,4},{24,8},{28,12},{1,17},{... | collective-permute-start | bytes 24584 | tf_op jit(solution)/shard_map/ppermute | solution.py:34
  (6 other events, 45.5 us)

commit v4 on v3

--- a/solution.py
+++ b/solution.py
@@ -332,6 +332,11 @@
         held[1] = [swap(own_keys, "dp", 1)]
     held[0] = [own_keys]
     other = swap(mine, "dp", parts)
+    step = jnp.zeros((8, CLUSTER), jnp.float32)
+    for _ in range(1):
+        step, _ = lax.optimization_barrier((step, other))
+        step = swap(step, "tensor", 1)
+    other, _ = lax.optimization_barrier((other, step))
 
     def table(asked):
         asked = asked.reshape(requests)
@@ -347,7 +352,7 @@
 
     unit = 2 * CLUSTER * CLUSTER * width
     rows = {0: mine, 1: other}
-    chunks, waits = [], ()
+    chunks, waits = [], (tab[1],)
     for n, (groups, count) in enumerate(plans):
         if n == 1 and parts > 1:
             for mask in far:
@@ -376,6 +381,7 @@
             got = swap(pairs[:, 1], "tensor", 1 << bit)
             bit += 1
         chunks.append((keep + got)[0])
+        waits += (chunks[0],) if len(chunks) == 1 else ()
 
     tile = jax.ShapeDtypeStruct((share, CLUSTER), f32)
     levels = pltpu.VMEM((2 * clusters + 1, share, CLUSTER), f32)

time: 287 us -> 285 us (level)
  waiting for transfers between devices: 190 us -> 180 us
  starting transfers between devices: 31.1 us -> 40.4 us
    ppermute x34, waiting for transfers between devices: 190 us -> 180 us  [swap(): return lax.ppermute(value, axis, [(i, i ^ mask) for i in range(size)])]
    ppermute x34, starting transfers between devices: 31.1 us -> 40.4 us  [swap(): return lax.ppermute(value, axis, [(i, i ^ mask) for i in range(size)])]
  transfers between devices with their start and end apart: 34 -> 34, of which waited for: 20 -> 21; matrix products, arithmetic and copies ran while one was open for 2% -> 1% of each run, Pallas kernels for 15% -> 13%
where the time goes in v4:
time: 285 us
  waiting for transfers between devices  180 us (63%)
  Pallas kernels  50.8 us (18%)
  starting transfers between devices  40.4 us (14%)
  local copies, waits for them, and re-layouts  5.26 us (2%)
  other arithmetic  4.79 us (2%)
  between operations  3.38 us (1%)
    ppermute x34, waiting for transfers between devices, swap(): return lax.ppermute(value, axis, [(i, i ^ mask) for i in range(size)])  180 us
    pallas_call x12, Pallas kernels, call(): pl.pallas_call(body, name=name, out_shape=out_shape, in_specs=[SM] * smem...  50.8 us
    ppermute x34, starting transfers between devices, swap(): return lax.ppermute(value, axis, [(i, i ^ mask) for i in range(size)])  40.4 us
  transfers between devices with their start and end apart: 34, of which 21 were waited for; matrix products, arithmetic and copies ran while one was open for 1% of the time, Pallas kernels for 13%

profile of v4, /device:TPU:0, one launch (start us, length us, event | category | flops | bytes accessed | tf_op | source)
XLA Modules:
  0.0 284.8 jit_solution(3777829108681654860)
XLA Ops:
  0.6 4.1 %collective-permute-start = (s32[7,8]{1,0:T(8,128)}, s32[7,8]{1,0:T(8,128)S(1)}, u32[]{:S(2)}, u32[]{:S(2)}) collective-permute-start(s32[7,8]{1,0:T(8,128)} %param.5), channel_id=1, source_target_pairs={{0,16},{4,20},{8,24},{12,28},{16,0},{20,4},{24,8},{28,12},{1,17},{... | collective-permute-start | bytes 680 | tf_op jit(solution)/shard_map/ppermute | solution.py:34
  6.3 2.5 split.8
  11.9 34.6 %collective-permute-done.2.refs_5_.refs_6_ = bf16[7,128,1024]{2,1,0:T(8,128)(2,1)} collective-permute-done((bf16[7,128,1024]{2,1,0:T(8,128)(2,1)}, bf16[7,128,1024]{2,1,0:T(8,128)(2,1)}, u32[]{:S(2)}, u32[]{:S(2)}) %collective-permute-start.2) | collective-permute-done | bytes 1835040 | tf_op jit(solution)/shard_map/ppermute | solution.py:34
  48.0 5.5 %logits_0.1 = (f32[2,21,32,128]{3,2,1,0:T(8,128)S(1)}, f32[2,21,32,128]{3,2,1,0:T(8,128)S(1)}, f32[8,128]{1,0:T(8,128)S(1)}) custom-call(s32[28]{0:T(128)S(1)} %select_reduce_fusion.3.refs_0_.refs_1_, s32[28]{0:T(128)S(1)} %select_reduce_fusion.3.refs_0_.refs_1_, s32[1]{0:T(128)} %bitcast.refs_2_, bf16[7,128,1024]{2,1,0:T(8,128)(2,1)S(1)} %bitcast.48, ...), custom_call_target="tpu_custom_call" | custom-call | flops 704643 | bytes 6885 | tf_op jit(solution)/shard_map/logits_0/pallas_call | solution.py:49
  53.7 14.1 %collective-permute-done.3.refs_7_ = bf16[7,128,768]{2,1,0:T(8,128)(2,1)S(1)} collective-permute-done((bf16[7,128,768]{2,1,0:T(8,128)(2,1)}, bf16[7,128,768]{2,1,0:T(8,128)(2,1)S(1)}, u32[]{:S(2)}, u32[]{:S(2)}) %collective-permute-start.3) | collective-permute-done | bytes 1376288 | tf_op jit(solution)/shard_map/ppermute | solution.py:34
  70.1 18.6 %collective-permute-done.4.refs_8_ = bf16[7,128,256]{2,1,0:T(8,128)(2,1)S(1)} collective-permute-done((bf16[7,128,256]{2,1,0:T(8,128)(2,1)S(1)}, bf16[7,128,256]{2,1,0:T(8,128)(2,1)S(1)}, u32[]{:S(2)}, u32[]{:S(2)}) %collective-permute-start.4) | collective-permute-done | bytes 458784 | tf_op jit(solution)/shard_map/ppermute | solution.py:34
  88.7 3.5 %collective-permute-start.6 = (bf16[7,128,256]{2,1,0:T(8,128)(2,1)S(1)}, bf16[7,128,256]{2,1,0:T(8,128)(2,1)S(1)}, u32[]{:S(2)}, u32[]{:S(2)}) collective-permute-start(bf16[7,128,256]{2,1,0:T(8,128)(2,1)S(1)} %collective-permute-done.4.refs_8_), channel_id=1, source_target_pairs={{0,4},{4,0},{8,12},{12,8},{16,20},{20,16},{24,28},{28,24},{1,5},{5... | collective-permute-start | bytes 1376264 | tf_op jit(solution)/shard_map/ppermute | solution.py:34
  92.3 5.2 %logits_1.1 = (f32[2,28,32,128]{3,2,1,0:T(8,128)S(1)}, f32[2,28,32,128]{3,2,1,0:T(8,128)S(1)}, f32[8,128]{1,0:T(8,128)S(1)}) custom-call(s32[28]{0:T(128)S(1)} %select_reduce_fusion.3.refs_0_.refs_1_, s32[28]{0:T(128)S(1)} %select_reduce_fusion.2.refs_6_.refs_1_, s32[1]{0:T(128)} %bitcast.refs_2_, bf16[7,128,1024]{2,1,0:T(8,128)(2,1)S(1)} %bitcast.49, ...), custom_call_target="tpu_custom_call" | custom-call | flops 939524 | bytes 11014 | tf_op jit(solution)/shard_map/logits_1/pallas_call | solution.py:49
  97.5 10.6 %collective-permute-done.6.refs_6_.refs_10_ = bf16[7,128,256]{2,1,0:T(8,128)(2,1)S(1)} collective-permute-done((bf16[7,128,256]{2,1,0:T(8,128)(2,1)S(1)}, bf16[7,128,256]{2,1,0:T(8,128)(2,1)S(1)}, u32[]{:S(2)}, u32[]{:S(2)}) %collective-permute-start.6) | collective-permute-done | bytes 458784 | tf_op jit(solution)/shard_map/ppermute | solution.py:34
  108.1 4.1 %logits_2.1 = (f32[2,14,32,128]{3,2,1,0:T(8,128)S(1)}, f32[2,14,32,128]{3,2,1,0:T(8,128)S(1)}, f32[8,128]{1,0:T(8,128)}) custom-call(s32[28]{0:T(128)S(1)} %select_reduce_fusion.3.refs_0_.refs_1_, s32[28]{0:T(128)S(1)} %select_reduce_fusion.2.refs_6_.refs_1_, s32[1]{0:T(128)} %bitcast.refs_2_, bf16[7,128,1024]{2,1,0:T(8,128)(2,1)S(1)} %bitcast.50, ...), custom_call_target="tpu_custom_call" | custom-call | flops 469762 | bytes 6426 | tf_op jit(solution)/shard_map/logits_2/pallas_call | solution.py:49
  117.1 5.5 %collective-permute-done.12 = f32[1,14,32,128]{3,2,1,0:T(8,128)S(1)} collective-permute-done((f32[1,14,32,128]{3,2,1,0:T(8,128)S(1)}, f32[1,14,32,128]{3,2,1,0:T(8,128)S(1)}, u32[]{:S(2)}, u32[]{:S(2)}) %collective-permute-start.12) | collective-permute-done | bytes 229408 | tf_op jit(solution)/shard_map/ppermute | solution.py:34
  122.6 9.0 %collective-permute-done.10 = f32[1,28,32,128]{3,2,1,0:T(8,128)S(1)} collective-permute-done((f32[1,28,32,128]{3,2,1,0:T(8,128)S(1)}, f32[1,28,32,128]{3,2,1,0:T(8,128)S(1)}, u32[]{:S(2)}, u32[]{:S(2)}) %collective-permute-start.10) | collective-permute-done | bytes 458784 | tf_op jit(solution)/shard_map/ppermute | solution.py:34
  133.4 3.6 %collective-permute-start.13 = (f32[32,128]{1,0:T(8,128)S(1)}, f32[32,128]{1,0:T(8,128)S(1)}, u32[]{:S(2)}, u32[]{:S(2)}) collective-permute-start(f32[32,128]{1,0:T(8,128)S(1)} %row_stats.1.refs_3_), channel_id=1, source_target_pairs={{0,16},{4,20},{8,24},{12,28},{16,0},{20,4},{24,8},{28,12},{1,17},{... | collective-permute-start | bytes 49160 | tf_op jit(solution)/shard_map/ppermute | solution.py:34
  142.2 3.3 %collective-permute-done.20.refs_6_.refs_20_ = bf16[14,32,128]{2,1,0:T(8,128)(2,1)S(1)} collective-permute-done((bf16[14,32,128]{2,1,0:T(8,128)(2,1)S(1)}, bf16[14,32,128]{2,1,0:T(8,128)(2,1)S(1)}, u32[]{:S(2)}, u32[]{:S(2)}) %collective-permute-start.20) | collective-permute-done | bytes 114720 | tf_op jit(solution)/shard_map/ppermute | solution.py:34
  146.8 4.2 %terms_far.1 = (bf16[7,128,512]{2,1,0:T(8,128)(2,1)S(1)}, bf16[7,128,512]{2,1,0:T(8,128)(2,1)S(1)}) custom-call(s32[28]{0:T(128)S(1)} %select_reduce_fusion.3.refs_0_.refs_1_, s32[28]{0:T(128)S(1)} %select_reduce_fusion.2.refs_6_.refs_1_, s32[1]{0:T(128)} %bitcast.refs_2_, bf16[7,128,1024]{2,1,0:T(8,128)(2,1)S(1)} %bitcast.51, ...), custom_call_target="tpu_custom_call" | custom-call | flops 234881 | bytes 5963 | tf_op jit(solution)/shard_map/terms_far/pallas_call | solution.py:49
  153.6 6.5 %collective-permute-done.17.refs_16_.refs_6_ = bf16[28,32,128]{2,1,0:T(8,128)(2,1)S(1)} collective-permute-done((bf16[28,32,128]{2,1,0:T(8,128)(2,1)S(1)}, bf16[28,32,128]{2,1,0:T(8,128)(2,1)S(1)}, u32[]{:S(2)}, u32[]{:S(2)}) %collective-permute-start.17) | collective-permute-done | bytes 229408 | tf_op jit(solution)/shard_map/ppermute | solution.py:34
  160.6 2.1 collective-permute-done.14.refs_12_
  164.1 8.3 %grads_lead.1 = (bf16[7,128,1024]{2,1,0:T(8,128)(2,1)S(1)}, bf16[7,128,1024]{2,1,0:T(8,128)(2,1)S(1)}) custom-call(s32[28]{0:T(128)S(1)} %select_reduce_fusion.3.refs_0_.refs_1_, s32[28]{0:T(128)S(1)} %select_reduce_fusion.2.refs_6_.refs_1_, s32[1]{0:T(128)} %bitcast.refs_2_, bf16[7,128,1024]{2,1,0:T(8,128)(2,1)S(1)} %bitcast.52, ...), custom_call_target="tpu_custom_call" | custom-call | flops 469762 | bytes 16744 | tf_op jit(solution)/shard_map/grads_lead/pallas_call | solution.py:49
  172.4 3.0 %collective-permute-start.23 = (bf16[7,128,1024]{2,1,0:T(8,128)(2,1)S(1)}, bf16[7,128,1024]{2,1,0:T(8,128)(2,1)S(1)}, u32[]{:S(2)}, u32[]{:S(2)}) collective-permute-start(bf16[7,128,1024]{2,1,0:T(8,128)(2,1)S(1)} %get-tuple-element.44.refs_23_), channel_id=1, source_target_pairs={{0,16},{4,20},{8,24},{12,28},{16,0},{20,4},{24,8},{28,12},{1,17},{... | collective-permute-start | bytes 5505032 | tf_op jit(solution)/shard_map/ppermute | solution.py:34
  177.4 3.6 %term_2_1.1 = bf16[7,128,512]{2,1,0:T(8,128)(2,1)S(1)} custom-call(s32[28]{0:T(128)S(1)} %select_reduce_fusion.3.refs_0_.refs_1_, s32[28]{0:T(128)S(1)} %select_reduce_fusion.2.refs_6_.refs_1_, s32[1]{0:T(128)} %bitcast.refs_2_, bf16[7,128,1024]{2,1,0:T(8,128)(2,1)S(1)} %bitcast.53, bf16[7,128,1024]{2,1,0:T(8,128)(2,1)} %collective-permute-done.1.refs_4_, ...), custom_call_target="tpu_custom_call" | custom-call | flops 234881 | bytes 6422 | tf_op jit(solution)/shard_map/term_2_1/pallas_call | solution.py:49
  181.0 2.6 collective-permute-start.28
  183.6 15.0 %collective-permute-done.26.refs_9_ = bf16[7,128,512]{2,1,0:T(8,128)(2,1)S(1)} collective-permute-done((bf16[7,128,512]{2,1,0:T(8,128)(2,1)S(1)}, bf16[7,128,512]{2,1,0:T(8,128)(2,1)S(1)}, u32[]{:S(2)}, u32[]{:S(2)}) %collective-permute-start.26) | collective-permute-done | bytes 917536 | tf_op jit(solution)/shard_map/ppermute | solution.py:34
  198.6 3.6 %term_2_0.1 = bf16[7,128,512]{2,1,0:T(8,128)(2,1)S(1)} custom-call(s32[28]{0:T(128)S(1)} %select_reduce_fusion.3.refs_0_.refs_1_, s32[28]{0:T(128)S(1)} %select_reduce_fusion.2.refs_6_.refs_1_, s32[1]{0:T(128)} %bitcast.refs_2_, bf16[7,128,1024]{2,1,0:T(8,128)(2,1)S(1)} %bitcast.54, bf16[7,128,1024]{2,1,0:T(8,128)(2,1)} %collective-permute-done.1.refs_4_, ...), custom_call_target="tpu_custom_call" | custom-call | flops 234881 | bytes 6422 | tf_op jit(solution)/shard_map/term_2_0/pallas_call | solution.py:49
  202.2 2.6 collective-permute-start.27
  204.8 11.2 %grads_own.1 = (f32[7,128,1024]{2,1,0:T(8,128)S(1)}, f32[7,128,1024]{2,1,0:T(8,128)S(1)}) custom-call(s32[28]{0:T(128)S(1)} %select_reduce_fusion.3.refs_0_.refs_1_, s32[28]{0:T(128)S(1)} %select_reduce_fusion.2.refs_6_.refs_1_, s32[1]{0:T(128)} %bitcast.refs_2_, bf16[7,128,1024]{2,1,0:T(8,128)(2,1)S(1)} %bitcast.55, ...), custom_call_target="tpu_custom_call" | custom-call | flops 469762 | bytes 20414 | tf_op jit(solution)/shard_map/grads_own/pallas_call | solution.py:49
  216.0 39.2 %collective-permute-done.23.refs_2_ = bf16[7,128,1024]{2,1,0:T(8,128)(2,1)S(1)} collective-permute-done((bf16[7,128,1024]{2,1,0:T(8,128)(2,1)S(1)}, bf16[7,128,1024]{2,1,0:T(8,128)(2,1)S(1)}, u32[]{:S(2)}, u32[]{:S(2)}) %collective-permute-start.23) | collective-permute-done | bytes 1835040 | tf_op jit(solution)/shard_map/ppermute | solution.py:34
  255.8 4.7 %collective-permute-done.27.refs_3_ = bf16[7,128,512]{2,1,0:T(8,128)(2,1)S(1)} collective-permute-done((bf16[7,128,512]{2,1,0:T(8,128)(2,1)S(1)}, bf16[7,128,512]{2,1,0:T(8,128)(2,1)S(1)}, u32[]{:S(2)}, u32[]{:S(2)}) %collective-permute-start.27) | collective-permute-done | bytes 917536 | tf_op jit(solution)/shard_map/ppermute | solution.py:34
  264.1 2.1 collective-permute-done.30
  267.8 2.1 collective-permute-done.31
  269.9 3.6 %collective-permute-done.32 = f32[2,8,128]{2,1,0:T(8,128)S(1)} collective-permute-done((f32[2,8,128]{2,1,0:T(8,128)S(1)}, f32[2,8,128]{2,1,0:T(8,128)S(1)}, u32[]{:S(2)}, u32[]{:S(2)}) %collective-permute-start.32) | collective-permute-done | bytes 8224 | tf_op jit(solution)/shard_map/ppermute | solution.py:34
  273.6 2.3 collective-permute-start.33
  275.8 2.3 collective-permute-done.33
  (95 shorter events, 38.4 us)
Async XLA Ops:
  0.6 10.5 %collective-permute-start = (s32[7,8]{1,0:T(8,128)}, s32[7,8]{1,0:T(8,128)S(1)}, u32[]{:S(2)}, u32[]{:S(2)}) collective-permute-start(s32[7,8]{1,0:T(8,128)} %param.5), channel_id=1, source_target_pairs={{0,16},{4,20},{8,24},{12,28},{16,0},{20,4},{24,8},{28,12},{1,17},{... | collective-permute-start | bytes 680 | tf_op jit(solution)/shard_map/ppermute | solution.py:34
  4.8 41.8 %collective-permute-start.2 = (bf16[7,128,1024]{2,1,0:T(8,128)(2,1)}, bf16[7,128,1024]{2,1,0:T(8,128)(2,1)}, u32[]{:S(2)}, u32[]{:S(2)}) collective-permute-start(bf16[7,128,1024]{2,1,0:T(8,128)(2,1)} %bitcast.56), channel_id=1, source_target_pairs={{0,4},{4,0},{8,12},{12,8},{16,20},{20,16},{24,28},{28,24},{1,5},{5... | collective-permute-start | bytes 5505032 | tf_op jit(solution)/shard_map/ppermute | solution.py:34
  8.8 58.9 %collective-permute-start.3 = (bf16[7,128,768]{2,1,0:T(8,128)(2,1)}, bf16[7,128,768]{2,1,0:T(8,128)(2,1)S(1)}, u32[]{:S(2)}, u32[]{:S(2)}) collective-permute-start(bf16[7,128,768]{2,1,0:T(8,128)(2,1)} %split.8), channel_id=1, source_target_pairs={{0,8},{4,12},{8,0},{12,4},{16,24},{20,28},{24,16},{28,20},{1,9},{5... | collective-permute-start | bytes 4128776 | tf_op jit(solution)/shard_map/ppermute | solution.py:34
  10.4 81.8 %collective-permute-start.1 = (bf16[7,128,1024]{2,1,0:T(8,128)(2,1)S(1)}, bf16[7,128,1024]{2,1,0:T(8,128)(2,1)}, u32[]{:S(2)}, u32[]{:S(2)}) collective-permute-start(bf16[7,128,1024]{2,1,0:T(8,128)(2,1)S(1)} %bitcast.47), channel_id=1, source_target_pairs={{0,16},{4,20},{8,24},{12,28},{16,0},{20,4},{24,8},{28,12},{1,17},{... | collective-permute-start | bytes 5505032 | tf_op jit(solution)/shard_map/ppermute | solution.py:34
  53.5 14.9 %collective-permute-start.7 = (f32[2,21,32,128]{3,2,1,0:T(8,128)S(1)}, f32[2,21,32,128]{3,2,1,0:T(8,128)S(1)}, u32[]{:S(2)}, u32[]{:S(2)}) collective-permute-start(f32[2,21,32,128]{3,2,1,0:T(8,128)S(1)} %get-tuple-element.34), channel_id=1, source_target_pairs={{0,1},{1,0},{2,3},{3,2},{4,5},{5,4},{6,7},{7,6},{8,9},{9,8},{10,11... | collective-permute-start | bytes 2064392 | tf_op jit(solution)/shard_map/ppermute | solution.py:34
  67.7 40.4 %collective-permute-start.5 = (bf16[7,128,768]{2,1,0:T(8,128)(2,1)S(1)}, bf16[7,128,768]{2,1,0:T(8,128)(2,1)S(1)}, u32[]{:S(2)}, u32[]{:S(2)}) collective-permute-start(bf16[7,128,768]{2,1,0:T(8,128)(2,1)S(1)} %collective-permute-done.3.refs_7_), channel_id=1, source_target_pairs={{0,4},{4,0},{8,12},{12,8},{16,20},{20,16},{24,28},{28,24},{1,5},{5... | collective-permute-start | bytes 4128776 | tf_op jit(solution)/shard_map/ppermute | solution.py:34
  68.4 20.3 %collective-permute-start.4 = (bf16[7,128,256]{2,1,0:T(8,128)(2,1)S(1)}, bf16[7,128,256]{2,1,0:T(8,128)(2,1)S(1)}, u32[]{:S(2)}, u32[]{:S(2)}) collective-permute-start(bf16[7,128,256]{2,1,0:T(8,128)(2,1)S(1)} %split.9), channel_id=1, source_target_pairs={{0,8},{4,12},{8,0},{12,4},{16,24},{20,28},{24,16},{28,20},{1,9},{5... | collective-permute-start | bytes 1376264 | tf_op jit(solution)/shard_map/ppermute | solution.py:34
  68.5 23.7 %collective-permute-start.8 = (f32[1,21,32,128]{3,2,1,0:T(8,128)S(1)}, f32[1,21,32,128]{3,2,1,0:T(8,128)S(1)}, u32[]{:S(2)}, u32[]{:S(2)}) collective-permute-start(f32[1,21,32,128]{3,2,1,0:T(8,128)S(1)} %slice_bitcast_fusion.2), channel_id=1, source_target_pairs={{0,2},{1,3},{2,0},{3,1},{4,6},{5,7},{6,4},{7,5},{8,10},{9,11},{10,... | collective-permute-start | bytes 1032200 | tf_op jit(solution)/shard_map/ppermute | solution.py:34
  88.7 19.4 %collective-permute-start.6 = (bf16[7,128,256]{2,1,0:T(8,128)(2,1)S(1)}, bf16[7,128,256]{2,1,0:T(8,128)(2,1)S(1)}, u32[]{:S(2)}, u32[]{:S(2)}) collective-permute-start(bf16[7,128,256]{2,1,0:T(8,128)(2,1)S(1)} %collective-permute-done.4.refs_8_), channel_id=1, source_target_pairs={{0,4},{4,0},{8,12},{12,8},{16,20},{20,16},{24,28},{28,24},{1,5},{5... | collective-permute-start | bytes 1376264 | tf_op jit(solution)/shard_map/ppermute | solution.py:34
  112.2 1.8 collective-permute-start.11
  112.2 3.5 %collective-permute-start.9 = (f32[2,28,32,128]{3,2,1,0:T(8,128)S(1)}, f32[2,28,32,128]{3,2,1,0:T(8,128)S(1)}, u32[]{:S(2)}, u32[]{:S(2)}) collective-permute-start(f32[2,28,32,128]{3,2,1,0:T(8,128)S(1)} %get-tuple-element.36), channel_id=1, source_target_pairs={{0,1},{1,0},{2,3},{3,2},{4,5},{5,4},{6,7},{7,6},{8,9},{9,8},{10,11... | collective-permute-start | bytes 2752520 | tf_op jit(solution)/shard_map/ppermute | solution.py:34
  114.1 8.5 %collective-permute-start.12 = (f32[1,14,32,128]{3,2,1,0:T(8,128)S(1)}, f32[1,14,32,128]{3,2,1,0:T(8,128)S(1)}, u32[]{:S(2)}, u32[]{:S(2)}) collective-permute-start(f32[1,14,32,128]{3,2,1,0:T(8,128)S(1)} %slice_bitcast_fusion.4), channel_id=1, source_target_pairs={{0,2},{1,3},{2,0},{3,1},{4,6},{5,7},{6,4},{7,5},{8,10},{9,11},{10,... | collective-permute-start | bytes 688136 | tf_op jit(solution)/shard_map/ppermute | solution.py:34
  115.9 15.8 %collective-permute-start.10 = (f32[1,28,32,128]{3,2,1,0:T(8,128)S(1)}, f32[1,28,32,128]{3,2,1,0:T(8,128)S(1)}, u32[]{:S(2)}, u32[]{:S(2)}) collective-permute-start(f32[1,28,32,128]{3,2,1,0:T(8,128)S(1)} %slice_bitcast_fusion), channel_id=1, source_target_pairs={{0,2},{1,3},{2,0},{3,1},{4,6},{5,7},{6,4},{7,5},{8,10},{9,11},{10,... | collective-permute-start | bytes 1376264 | tf_op jit(solution)/shard_map/ppermute | solution.py:34
  133.4 5.3 %collective-permute-start.13 = (f32[32,128]{1,0:T(8,128)S(1)}, f32[32,128]{1,0:T(8,128)S(1)}, u32[]{:S(2)}, u32[]{:S(2)}) collective-permute-start(f32[32,128]{1,0:T(8,128)S(1)} %row_stats.1.refs_3_), channel_id=1, source_target_pairs={{0,16},{4,20},{8,24},{12,28},{16,0},{20,4},{24,8},{28,12},{1,17},{... | collective-permute-start | bytes 49160 | tf_op jit(solution)/shard_map/ppermute | solution.py:34
  140.7 4.9 %collective-permute-start.20 = (bf16[14,32,128]{2,1,0:T(8,128)(2,1)S(1)}, bf16[14,32,128]{2,1,0:T(8,128)(2,1)S(1)}, u32[]{:S(2)}, u32[]{:S(2)}) collective-permute-start(bf16[14,32,128]{2,1,0:T(8,128)(2,1)S(1)} %get-tuple-element.42.refs_5_.refs_19_), channel_id=1, source_target_pairs={{0,2},{1,3},{2,0},{3,1},{4,6},{5,7},{6,4},{7,5},{8,10},{9,11},{10,... | collective-permute-start | bytes 344072 | tf_op jit(solution)/shard_map/ppermute | solution.py:34
  142.2 3.3 %collective-permute-start.21 = (bf16[14,32,128]{2,1,0:T(8,128)(2,1)S(1)}, bf16[14,32,128]{2,1,0:T(8,128)(2,1)S(1)}, u32[]{:S(2)}, u32[]{:S(2)}) collective-permute-start(bf16[14,32,128]{2,1,0:T(8,128)(2,1)S(1)} %get-tuple-element.42.refs_5_.refs_19_), channel_id=1, source_target_pairs={{0,1},{1,0},{2,3},{3,2},{4,5},{5,4},{6,7},{7,6},{8,9},{9,8},{10,11... | collective-permute-start | bytes 344072 | tf_op jit(solution)/shard_map/ppermute | solution.py:34
  151.0 25.9 %collective-permute-start.24 = (bf16[7,128,512]{2,1,0:T(8,128)(2,1)S(1)}, bf16[7,128,512]{2,1,0:T(8,128)(2,1)S(1)}, u32[]{:S(2)}, u32[]{:S(2)}) collective-permute-start(bf16[7,128,512]{2,1,0:T(8,128)(2,1)S(1)} %get-tuple-element.51), channel_id=1, source_target_pairs={{0,4},{4,0},{8,12},{12,8},{16,20},{20,16},{24,28},{28,24},{1,5},{5... | collective-permute-start | bytes 2752520 | tf_op jit(solution)/shard_map/ppermute | solution.py:34
  151.6 8.5 %collective-permute-start.17 = (bf16[28,32,128]{2,1,0:T(8,128)(2,1)S(1)}, bf16[28,32,128]{2,1,0:T(8,128)(2,1)S(1)}, u32[]{:S(2)}, u32[]{:S(2)}) collective-permute-start(bf16[28,32,128]{2,1,0:T(8,128)(2,1)S(1)} %get-tuple-element.41.refs_15_.refs_5_), channel_id=1, source_target_pairs={{0,2},{1,3},{2,0},{3,1},{4,6},{5,7},{6,4},{7,5},{8,10},{9,11},{10,... | collective-permute-start | bytes 688136 | tf_op jit(solution)/shard_map/ppermute | solution.py:34
  153.1 9.6 %collective-permute-start.14 = (bf16[21,32,128]{2,1,0:T(8,128)(2,1)S(1)}, bf16[21,32,128]{2,1,0:T(8,128)(2,1)S(1)}, u32[]{:S(2)}, u32[]{:S(2)}) collective-permute-start(bf16[21,32,128]{2,1,0:T(8,128)(2,1)S(1)} %get-tuple-element.40.refs_11_), channel_id=1, source_target_pairs={{0,2},{1,3},{2,0},{3,1},{4,6},{5,7},{6,4},{7,5},{8,10},{9,11},{10,... | collective-permute-start | bytes 516104 | tf_op jit(solution)/shard_map/ppermute | solution.py:34
  153.6 9.1 %collective-permute-start.18 = (bf16[28,32,128]{2,1,0:T(8,128)(2,1)S(1)}, bf16[28,32,128]{2,1,0:T(8,128)(2,1)S(1)}, u32[]{:S(2)}, u32[]{:S(2)}) collective-permute-start(bf16[28,32,128]{2,1,0:T(8,128)(2,1)S(1)} %get-tuple-element.41.refs_15_.refs_5_), channel_id=1, source_target_pairs={{0,1},{1,0},{2,3},{3,2},{4,5},{5,4},{6,7},{7,6},{8,9},{9,8},{10,11... | collective-permute-start | bytes 688136 | tf_op jit(solution)/shard_map/ppermute | solution.py:34
  160.1 4.0 %collective-permute-start.19 = (bf16[28,32,128]{2,1,0:T(8,128)(2,1)S(1)}, bf16[28,32,128]{2,1,0:T(8,128)(2,1)S(1)}, u32[]{:S(2)}, u32[]{:S(2)}) collective-permute-start(bf16[28,32,128]{2,1,0:T(8,128)(2,1)S(1)} %collective-permute-done.17.refs_16_.refs_6_), channel_id=1, source_target_pairs={{0,1},{1,0},{2,3},{3,2},{4,5},{5,4},{6,7},{7,6},{8,9},{9,8},{10,11... | collective-permute-start | bytes 688136 | tf_op jit(solution)/shard_map/ppermute | solution.py:34
  160.1 2.6 collective-permute-start.15
  162.7 1.4 collective-permute-start.16
  172.4 82.8 %collective-permute-start.23 = (bf16[7,128,1024]{2,1,0:T(8,128)(2,1)S(1)}, bf16[7,128,1024]{2,1,0:T(8,128)(2,1)S(1)}, u32[]{:S(2)}, u32[]{:S(2)}) collective-permute-start(bf16[7,128,1024]{2,1,0:T(8,128)(2,1)S(1)} %get-tuple-element.44.refs_23_), channel_id=1, source_target_pairs={{0,16},{4,20},{8,24},{12,28},{16,0},{20,4},{24,8},{28,12},{1,17},{... | collective-permute-start | bytes 5505032 | tf_op jit(solution)/shard_map/ppermute | solution.py:34
  175.4 23.2 %collective-permute-start.26 = (bf16[7,128,512]{2,1,0:T(8,128)(2,1)S(1)}, bf16[7,128,512]{2,1,0:T(8,128)(2,1)S(1)}, u32[]{:S(2)}, u32[]{:S(2)}) collective-permute-start(bf16[7,128,512]{2,1,0:T(8,128)(2,1)S(1)} %get-tuple-element.43.refs_23_), channel_id=1, source_target_pairs={{0,4},{4,0},{8,12},{12,8},{16,20},{20,16},{24,28},{28,24},{1,5},{5... | collective-permute-start | bytes 2752520 | tf_op jit(solution)/shard_map/ppermute | solution.py:34
  176.9 83.6 %collective-permute-start.25 = (bf16[7,128,1024]{2,1,0:T(8,128)(2,1)S(1)}, bf16[7,128,1024]{2,1,0:T(8,128)(2,1)S(1)}, u32[]{:S(2)}, u32[]{:S(2)}) collective-permute-start(bf16[7,128,1024]{2,1,0:T(8,128)(2,1)S(1)} %get-tuple-element.52), channel_id=1, source_target_pairs={{0,4},{4,0},{8,12},{12,8},{16,20},{20,16},{24,28},{28,24},{1,5},{5... | collective-permute-start | bytes 5505032 | tf_op jit(solution)/shard_map/ppermute | solution.py:34
  181.0 74.8 %collective-permute-start.28 = (bf16[7,128,512]{2,1,0:T(8,128)(2,1)S(1)}, bf16[7,128,512]{2,1,0:T(8,128)(2,1)S(1)}, u32[]{:S(2)}, u32[]{:S(2)}) collective-permute-start(bf16[7,128,512]{2,1,0:T(8,128)(2,1)S(1)} %term_2_1.1), channel_id=1, source_target_pairs={{0,8},{4,12},{8,0},{12,4},{16,24},{20,28},{24,16},{28,20},{1,9},{5... | collective-permute-start | bytes 2752520 | tf_op jit(solution)/shard_map/ppermute | solution.py:34
  202.2 58.2 %collective-permute-start.27 = (bf16[7,128,512]{2,1,0:T(8,128)(2,1)S(1)}, bf16[7,128,512]{2,1,0:T(8,128)(2,1)S(1)}, u32[]{:S(2)}, u32[]{:S(2)}) collective-permute-start(bf16[7,128,512]{2,1,0:T(8,128)(2,1)S(1)} %term_2_0.1), channel_id=1, source_target_pairs={{0,8},{4,12},{8,0},{12,4},{16,24},{20,28},{24,16},{28,20},{1,9},{5... | collective-permute-start | bytes 2752520 | tf_op jit(solution)/shard_map/ppermute | solution.py:34
  262.6 3.7 %collective-permute-start.30 = (f32[2,8,128]{2,1,0:T(8,128)S(1)}, f32[2,8,128]{2,1,0:T(8,128)S(1)}, u32[]{:S(2)}, u32[]{:S(2)}) collective-permute-start(f32[2,8,128]{2,1,0:T(8,128)S(1)} %fusion.12), channel_id=1, source_target_pairs={{0,2},{1,3},{2,0},{3,1},{4,6},{5,7},{6,4},{7,5},{8,10},{9,11},{10,... | collective-permute-start | bytes 24584 | tf_op jit(solution)/shard_map/ppermute | solution.py:34
  266.3 3.7 %collective-permute-start.31 = (f32[2,8,128]{2,1,0:T(8,128)S(1)}, f32[2,8,128]{2,1,0:T(8,128)S(1)}, u32[]{:S(2)}, u32[]{:S(2)}) collective-permute-start(f32[2,8,128]{2,1,0:T(8,128)S(1)} %fusion.14), channel_id=1, source_target_pairs={{0,4},{4,0},{8,12},{12,8},{16,20},{20,16},{24,28},{28,24},{1,5},{5... | collective-permute-start | bytes 24584 | tf_op jit(solution)/shard_map/ppermute | solution.py:34
  269.9 3.7 %collective-permute-start.32 = (f32[2,8,128]{2,1,0:T(8,128)S(1)}, f32[2,8,128]{2,1,0:T(8,128)S(1)}, u32[]{:S(2)}, u32[]{:S(2)}) collective-permute-start(f32[2,8,128]{2,1,0:T(8,128)S(1)} %add.143), channel_id=1, source_target_pairs={{0,8},{4,12},{8,0},{12,4},{16,24},{20,28},{24,16},{28,20},{1,9},{5... | collective-permute-start | bytes 24584 | tf_op jit(solution)/shard_map/ppermute | solution.py:34
  273.6 4.5 %collective-permute-start.33 = (f32[2,8,128]{2,1,0:T(8,128)S(1)}, f32[2,8,128]{2,1,0:T(8,128)S(1)}, u32[]{:S(2)}, u32[]{:S(2)}) collective-permute-start(f32[2,8,128]{2,1,0:T(8,128)S(1)} %add.144), channel_id=1, source_target_pairs={{0,16},{4,20},{8,24},{12,28},{16,0},{20,4},{24,8},{28,12},{1,17},{... | collective-permute-start | bytes 24584 | tf_op jit(solution)/shard_map/ppermute | solution.py:34
  (6 other events, 29.5 us)

commit v5 on v4

--- a/solution.py
+++ b/solution.py
@@ -13,7 +13,7 @@
 VALID = 1 << 16
 VMEM_LIMIT = 56 * 1024 * 1024
 SLACK = 4 * 1024 * 1024
-COST = 1000
+COST = 1
 IN_CUT = 6
 OUT_CUT = 4
 
@@ -447,7 +447,7 @@
     odd = range(3, parts, 2)
     terms, waits = {}, ()
     if odd:
-        made = gradients("terms_far", [("term", m, 0, (cut, width - cut), []) for m in odd])
+        made = gradients("terms_far", [("term", m, 0, (cut, width - cut), []) for m in odd], (pieces[1][1],))
         terms = {m: made[2 * i : 2 * i + 2] for i, m in enumerate(odd)}
         waits = (made[0],)
     lead = [("query", 1)] + ([("term", 1, 0, (width,), [])] if parts > 1 else [])

time: 285 us -> 283 us (level)
  waiting for transfers between devices: 180 us -> 176 us
    ppermute x34, waiting for transfers between devices: 180 us -> 176 us  [swap(): return lax.ppermute(value, axis, [(i, i ^ mask) for i in range(size)])]
  transfers between devices with their start and end apart: 34 -> 34, of which waited for: 21 -> 21; matrix products, arithmetic and copies ran while one was open for 1% -> 2% of each run, Pallas kernels for 13% -> 13%
where the time goes in v5:
time: 283 us; the launch traced here: 282 us
  waiting for transfers between devices  176 us (62%)
  Pallas kernels  50.7 us (18%)
  starting transfers between devices  42 us (15%)
  local copies, waits for them, and re-layouts  5.26 us (2%)
  other arithmetic  4.78 us (2%)
  between operations  3.38 us (1%)
    ppermute x34, waiting for transfers between devices, swap(): return lax.ppermute(value, axis, [(i, i ^ mask) for i in range(size)])  176 us
    pallas_call x12, Pallas kernels, call(): pl.pallas_call(body, name=name, out_shape=out_shape, in_specs=[SM] * smem...  50.7 us
    ppermute x34, starting transfers between devices, swap(): return lax.ppermute(value, axis, [(i, i ^ mask) for i in range(size)])  42 us
  transfers between devices with their start and end apart: 34, of which 21 were waited for; matrix products, arithmetic and copies ran while one was open for 2% of the time, Pallas kernels for 13%

profile of v5, /device:TPU:0, one launch (start us, length us, event | category | flops | bytes accessed | tf_op | source)
XLA Modules:
  0.0 282.3 jit_solution(747188337031409339)
XLA Ops:
  0.6 4.1 %collective-permute-start = (s32[7,8]{1,0:T(8,128)}, s32[7,8]{1,0:T(8,128)S(1)}, u32[]{:S(2)}, u32[]{:S(2)}) collective-permute-start(s32[7,8]{1,0:T(8,128)} %param.5), channel_id=1, source_target_pairs={{0,16},{4,20},{8,24},{12,28},{16,0},{20,4},{24,8},{28,12},{1,17},{... | collective-permute-start | bytes 680 | tf_op jit(solution)/shard_map/ppermute | solution.py:34
  6.3 2.5 split.8
  11.9 34.6 %collective-permute-done.2.refs_5_.refs_6_ = bf16[7,128,1024]{2,1,0:T(8,128)(2,1)} collective-permute-done((bf16[7,128,1024]{2,1,0:T(8,128)(2,1)}, bf16[7,128,1024]{2,1,0:T(8,128)(2,1)}, u32[]{:S(2)}, u32[]{:S(2)}) %collective-permute-start.2) | collective-permute-done | bytes 1835040 | tf_op jit(solution)/shard_map/ppermute | solution.py:34
  48.0 5.5 %logits_0.1 = (f32[2,21,32,128]{3,2,1,0:T(8,128)S(1)}, f32[2,21,32,128]{3,2,1,0:T(8,128)S(1)}, f32[8,128]{1,0:T(8,128)S(1)}) custom-call(s32[28]{0:T(128)S(1)} %select_reduce_fusion.3.refs_0_.refs_1_, s32[28]{0:T(128)S(1)} %select_reduce_fusion.3.refs_0_.refs_1_, s32[1]{0:T(128)} %bitcast.refs_2_, bf16[7,128,1024]{2,1,0:T(8,128)(2,1)S(1)} %bitcast.48, ...), custom_call_target="tpu_custom_call" | custom-call | flops 704643072 | bytes 6885376 | tf_op jit(solution)/shard_map/logits_0/pallas_call | solution.py:49
  53.7 14.1 %collective-permute-done.3.refs_7_ = bf16[7,128,768]{2,1,0:T(8,128)(2,1)S(1)} collective-permute-done((bf16[7,128,768]{2,1,0:T(8,128)(2,1)}, bf16[7,128,768]{2,1,0:T(8,128)(2,1)S(1)}, u32[]{:S(2)}, u32[]{:S(2)}) %collective-permute-start.3) | collective-permute-done | bytes 1376288 | tf_op jit(solution)/shard_map/ppermute | solution.py:34
  70.1 18.6 %collective-permute-done.4.refs_8_ = bf16[7,128,256]{2,1,0:T(8,128)(2,1)S(1)} collective-permute-done((bf16[7,128,256]{2,1,0:T(8,128)(2,1)S(1)}, bf16[7,128,256]{2,1,0:T(8,128)(2,1)S(1)}, u32[]{:S(2)}, u32[]{:S(2)}) %collective-permute-start.4) | collective-permute-done | bytes 458784 | tf_op jit(solution)/shard_map/ppermute | solution.py:34
  88.7 3.5 %collective-permute-start.6 = (bf16[7,128,256]{2,1,0:T(8,128)(2,1)S(1)}, bf16[7,128,256]{2,1,0:T(8,128)(2,1)S(1)}, u32[]{:S(2)}, u32[]{:S(2)}) collective-permute-start(bf16[7,128,256]{2,1,0:T(8,128)(2,1)S(1)} %collective-permute-done.4.refs_8_), channel_id=1, source_target_pairs={{0,4},{4,0},{8,12},{12,8},{16,20},{20,16},{24,28},{28,24},{1,5},{5... | collective-permute-start | bytes 1376264 | tf_op jit(solution)/shard_map/ppermute | solution.py:34
  92.3 5.2 %logits_1.1 = (f32[2,28,32,128]{3,2,1,0:T(8,128)S(1)}, f32[2,28,32,128]{3,2,1,0:T(8,128)S(1)}, f32[8,128]{1,0:T(8,128)S(1)}) custom-call(s32[28]{0:T(128)S(1)} %select_reduce_fusion.3.refs_0_.refs_1_, s32[28]{0:T(128)S(1)} %select_reduce_fusion.2.refs_6_.refs_1_, s32[1]{0:T(128)} %bitcast.refs_2_, bf16[7,128,1024]{2,1,0:T(8,128)(2,1)S(1)} %bitcast.49, ...), custom_call_target="tpu_custom_call" | custom-call | flops 939524096 | bytes 11014144 | tf_op jit(solution)/shard_map/logits_1/pallas_call | solution.py:49
  97.5 10.6 %collective-permute-done.6.refs_6_.refs_10_ = bf16[7,128,256]{2,1,0:T(8,128)(2,1)S(1)} collective-permute-done((bf16[7,128,256]{2,1,0:T(8,128)(2,1)S(1)}, bf16[7,128,256]{2,1,0:T(8,128)(2,1)S(1)}, u32[]{:S(2)}, u32[]{:S(2)}) %collective-permute-start.6) | collective-permute-done | bytes 458784 | tf_op jit(solution)/shard_map/ppermute | solution.py:34
  108.1 4.1 %logits_2.1 = (f32[2,14,32,128]{3,2,1,0:T(8,128)S(1)}, f32[2,14,32,128]{3,2,1,0:T(8,128)S(1)}, f32[8,128]{1,0:T(8,128)}) custom-call(s32[28]{0:T(128)S(1)} %select_reduce_fusion.3.refs_0_.refs_1_, s32[28]{0:T(128)S(1)} %select_reduce_fusion.2.refs_6_.refs_1_, s32[1]{0:T(128)} %bitcast.refs_2_, bf16[7,128,1024]{2,1,0:T(8,128)(2,1)S(1)} %bitcast.50, ...), custom_call_target="tpu_custom_call" | custom-call | flops 469762048 | bytes 6426624 | tf_op jit(solution)/shard_map/logits_2/pallas_call | solution.py:49
  117.1 5.5 %collective-permute-done.12 = f32[1,14,32,128]{3,2,1,0:T(8,128)S(1)} collective-permute-done((f32[1,14,32,128]{3,2,1,0:T(8,128)S(1)}, f32[1,14,32,128]{3,2,1,0:T(8,128)S(1)}, u32[]{:S(2)}, u32[]{:S(2)}) %collective-permute-start.12) | collective-permute-done | bytes 229408 | tf_op jit(solution)/shard_map/ppermute | solution.py:34
  122.6 9.0 %collective-permute-done.10 = f32[1,28,32,128]{3,2,1,0:T(8,128)S(1)} collective-permute-done((f32[1,28,32,128]{3,2,1,0:T(8,128)S(1)}, f32[1,28,32,128]{3,2,1,0:T(8,128)S(1)}, u32[]{:S(2)}, u32[]{:S(2)}) %collective-permute-start.10) | collective-permute-done | bytes 458784 | tf_op jit(solution)/shard_map/ppermute | solution.py:34
  133.4 3.6 %collective-permute-start.13 = (f32[32,128]{1,0:T(8,128)S(1)}, f32[32,128]{1,0:T(8,128)S(1)}, u32[]{:S(2)}, u32[]{:S(2)}) collective-permute-start(f32[32,128]{1,0:T(8,128)S(1)} %row_stats.1.refs_3_), channel_id=1, source_target_pairs={{0,16},{4,20},{8,24},{12,28},{16,0},{20,4},{24,8},{28,12},{1,17},{... | collective-permute-start | bytes 49160 | tf_op jit(solution)/shard_map/ppermute | solution.py:34
  138.7 1.9 weights.1
  142.7 3.9 %collective-permute-done.20.refs_6_.refs_20_ = bf16[14,32,128]{2,1,0:T(8,128)(2,1)S(1)} collective-permute-done((bf16[14,32,128]{2,1,0:T(8,128)(2,1)S(1)}, bf16[14,32,128]{2,1,0:T(8,128)(2,1)S(1)}, u32[]{:S(2)}, u32[]{:S(2)}) %collective-permute-start.20) | collective-permute-done | bytes 114720 | tf_op jit(solution)/shard_map/ppermute | solution.py:34
  149.1 4.2 %terms_far.1 = (bf16[7,128,512]{2,1,0:T(8,128)(2,1)S(1)}, bf16[7,128,512]{2,1,0:T(8,128)(2,1)S(1)}) custom-call(s32[28]{0:T(128)S(1)} %select_reduce_fusion.3.refs_0_.refs_1_, s32[28]{0:T(128)S(1)} %select_reduce_fusion.2.refs_6_.refs_1_, s32[1]{0:T(128)} %bitcast.refs_2_, bf16[7,128,1024]{2,1,0:T(8,128)(2,1)S(1)} %bitcast.51, ...), custom_call_target="tpu_custom_call" | custom-call | flops 234881024 | bytes 5963776 | tf_op jit(solution)/shard_map/terms_far/pallas_call | solution.py:49
  155.9 3.4 %collective-permute-done.14.refs_12_ = bf16[21,32,128]{2,1,0:T(8,128)(2,1)S(1)} collective-permute-done((bf16[21,32,128]{2,1,0:T(8,128)(2,1)S(1)}, bf16[21,32,128]{2,1,0:T(8,128)(2,1)S(1)}, u32[]{:S(2)}, u32[]{:S(2)}) %collective-permute-start.14) | collective-permute-done | bytes 172064 | tf_op jit(solution)/shard_map/ppermute | solution.py:34
  160.9 8.3 %grads_lead.1 = (bf16[7,128,1024]{2,1,0:T(8,128)(2,1)S(1)}, bf16[7,128,1024]{2,1,0:T(8,128)(2,1)S(1)}) custom-call(s32[28]{0:T(128)S(1)} %select_reduce_fusion.3.refs_0_.refs_1_, s32[28]{0:T(128)S(1)} %select_reduce_fusion.2.refs_6_.refs_1_, s32[1]{0:T(128)} %bitcast.refs_2_, bf16[7,128,1024]{2,1,0:T(8,128)(2,1)S(1)} %bitcast.52, ...), custom_call_target="tpu_custom_call" | custom-call | flops 469762048 | bytes 16744448 | tf_op jit(solution)/shard_map/grads_lead/pallas_call | solution.py:49
  169.2 2.7 collective-permute-start.23
  171.9 4.8 %collective-permute-done.24.refs_9_ = bf16[7,128,512]{2,1,0:T(8,128)(2,1)S(1)} collective-permute-done((bf16[7,128,512]{2,1,0:T(8,128)(2,1)S(1)}, bf16[7,128,512]{2,1,0:T(8,128)(2,1)S(1)}, u32[]{:S(2)}, u32[]{:S(2)}) %collective-permute-start.24) | collective-permute-done | bytes 917536 | tf_op jit(solution)/shard_map/ppermute | solution.py:34
  177.2 3.6 %term_2_1.1 = bf16[7,128,512]{2,1,0:T(8,128)(2,1)S(1)} custom-call(s32[28]{0:T(128)S(1)} %select_reduce_fusion.3.refs_0_.refs_1_, s32[28]{0:T(128)S(1)} %select_reduce_fusion.2.refs_6_.refs_1_, s32[1]{0:T(128)} %bitcast.refs_2_, bf16[7,128,1024]{2,1,0:T(8,128)(2,1)S(1)} %bitcast.53, bf16[7,128,1024]{2,1,0:T(8,128)(2,1)} %collective-permute-done.1.refs_4_, ...), custom_call_target="tpu_custom_call" | custom-call | flops 234881024 | bytes 6422528 | tf_op jit(solution)/shard_map/term_2_1/pallas_call | solution.py:49
  180.8 2.5 collective-permute-start.28
  183.4 13.0 %collective-permute-done.26.refs_9_ = bf16[7,128,512]{2,1,0:T(8,128)(2,1)S(1)} collective-permute-done((bf16[7,128,512]{2,1,0:T(8,128)(2,1)S(1)}, bf16[7,128,512]{2,1,0:T(8,128)(2,1)S(1)}, u32[]{:S(2)}, u32[]{:S(2)}) %collective-permute-start.26) | collective-permute-done | bytes 917536 | tf_op jit(solution)/shard_map/ppermute | solution.py:34
  196.4 3.6 %term_2_0.1 = bf16[7,128,512]{2,1,0:T(8,128)(2,1)S(1)} custom-call(s32[28]{0:T(128)S(1)} %select_reduce_fusion.3.refs_0_.refs_1_, s32[28]{0:T(128)S(1)} %select_reduce_fusion.2.refs_6_.refs_1_, s32[1]{0:T(128)} %bitcast.refs_2_, bf16[7,128,1024]{2,1,0:T(8,128)(2,1)S(1)} %bitcast.54, bf16[7,128,1024]{2,1,0:T(8,128)(2,1)} %collective-permute-done.1.refs_4_, ...), custom_call_target="tpu_custom_call" | custom-call | flops 234881024 | bytes 6422528 | tf_op jit(solution)/shard_map/term_2_0/pallas_call | solution.py:49
  200.0 2.5 collective-permute-start.27
  202.5 11.2 %grads_own.1 = (f32[7,128,1024]{2,1,0:T(8,128)S(1)}, f32[7,128,1024]{2,1,0:T(8,128)S(1)}) custom-call(s32[28]{0:T(128)S(1)} %select_reduce_fusion.3.refs_0_.refs_1_, s32[28]{0:T(128)S(1)} %select_reduce_fusion.2.refs_6_.refs_1_, s32[1]{0:T(128)} %bitcast.refs_2_, bf16[7,128,1024]{2,1,0:T(8,128)(2,1)S(1)} %bitcast.55, ...), custom_call_target="tpu_custom_call" | custom-call | flops 469762048 | bytes 20414464 | tf_op jit(solution)/shard_map/grads_own/pallas_call | solution.py:49
  213.7 38.0 %collective-permute-done.23.refs_2_ = bf16[7,128,1024]{2,1,0:T(8,128)(2,1)S(1)} collective-permute-done((bf16[7,128,1024]{2,1,0:T(8,128)(2,1)S(1)}, bf16[7,128,1024]{2,1,0:T(8,128)(2,1)S(1)}, u32[]{:S(2)}, u32[]{:S(2)}) %collective-permute-start.23) | collective-permute-done | bytes 1835040 | tf_op jit(solution)/shard_map/ppermute | solution.py:34
  252.3 4.4 %collective-permute-done.27.refs_3_ = bf16[7,128,512]{2,1,0:T(8,128)(2,1)S(1)} collective-permute-done((bf16[7,128,512]{2,1,0:T(8,128)(2,1)S(1)}, bf16[7,128,512]{2,1,0:T(8,128)(2,1)S(1)}, u32[]{:S(2)}, u32[]{:S(2)}) %collective-permute-start.27) | collective-permute-done | bytes 917536 | tf_op jit(solution)/shard_map/ppermute | solution.py:34
  260.3 2.2 collective-permute-done.30
  263.9 2.1 collective-permute-done.31
  266.1 3.6 %collective-permute-done.32 = f32[2,8,128]{2,1,0:T(8,128)S(1)} collective-permute-done((f32[2,8,128]{2,1,0:T(8,128)S(1)}, f32[2,8,128]{2,1,0:T(8,128)S(1)}, u32[]{:S(2)}, u32[]{:S(2)}) %collective-permute-start.32) | collective-permute-done | bytes 8224 | tf_op jit(solution)/shard_map/ppermute | solution.py:34
  269.7 4.3 %collective-permute-start.33 = (f32[2,8,128]{2,1,0:T(8,128)S(1)}, f32[2,8,128]{2,1,0:T(8,128)S(1)}, u32[]{:S(2)}, u32[]{:S(2)}) collective-permute-start(f32[2,8,128]{2,1,0:T(8,128)S(1)} %add.144), channel_id=1, source_target_pairs={{0,16},{4,20},{8,24},{12,28},{16,0},{20,4},{24,8},{28,12},{1,17},{... | collective-permute-start | bytes 24584 | tf_op jit(solution)/shard_map/ppermute | solution.py:34
  (95 shorter events, 37.6 us)
Async XLA Ops:
  0.6 10.5 %collective-permute-start = (s32[7,8]{1,0:T(8,128)}, s32[7,8]{1,0:T(8,128)S(1)}, u32[]{:S(2)}, u32[]{:S(2)}) collective-permute-start(s32[7,8]{1,0:T(8,128)} %param.5), channel_id=1, source_target_pairs={{0,16},{4,20},{8,24},{12,28},{16,0},{20,4},{24,8},{28,12},{1,17},{... | collective-permute-start | bytes 680 | tf_op jit(solution)/shard_map/ppermute | solution.py:34
  4.8 41.8 %collective-permute-start.2 = (bf16[7,128,1024]{2,1,0:T(8,128)(2,1)}, bf16[7,128,1024]{2,1,0:T(8,128)(2,1)}, u32[]{:S(2)}, u32[]{:S(2)}) collective-permute-start(bf16[7,128,1024]{2,1,0:T(8,128)(2,1)} %bitcast.56), channel_id=1, source_target_pairs={{0,4},{4,0},{8,12},{12,8},{16,20},{20,16},{24,28},{28,24},{1,5},{5... | collective-permute-start | bytes 5505032 | tf_op jit(solution)/shard_map/ppermute | solution.py:34
  8.8 58.9 %collective-permute-start.3 = (bf16[7,128,768]{2,1,0:T(8,128)(2,1)}, bf16[7,128,768]{2,1,0:T(8,128)(2,1)S(1)}, u32[]{:S(2)}, u32[]{:S(2)}) collective-permute-start(bf16[7,128,768]{2,1,0:T(8,128)(2,1)} %split.8), channel_id=1, source_target_pairs={{0,8},{4,12},{8,0},{12,4},{16,24},{20,28},{24,16},{28,20},{1,9},{5... | collective-permute-start | bytes 4128776 | tf_op jit(solution)/shard_map/ppermute | solution.py:34
  10.4 81.8 %collective-permute-start.1 = (bf16[7,128,1024]{2,1,0:T(8,128)(2,1)S(1)}, bf16[7,128,1024]{2,1,0:T(8,128)(2,1)}, u32[]{:S(2)}, u32[]{:S(2)}) collective-permute-start(bf16[7,128,1024]{2,1,0:T(8,128)(2,1)S(1)} %bitcast.47), channel_id=1, source_target_pairs={{0,16},{4,20},{8,24},{12,28},{16,0},{20,4},{24,8},{28,12},{1,17},{... | collective-permute-start | bytes 5505032 | tf_op jit(solution)/shard_map/ppermute | solution.py:34
  53.5 14.9 %collective-permute-start.7 = (f32[2,21,32,128]{3,2,1,0:T(8,128)S(1)}, f32[2,21,32,128]{3,2,1,0:T(8,128)S(1)}, u32[]{:S(2)}, u32[]{:S(2)}) collective-permute-start(f32[2,21,32,128]{3,2,1,0:T(8,128)S(1)} %get-tuple-element.34), channel_id=1, source_target_pairs={{0,1},{1,0},{2,3},{3,2},{4,5},{5,4},{6,7},{7,6},{8,9},{9,8},{10,11... | collective-permute-start | bytes 2064392 | tf_op jit(solution)/shard_map/ppermute | solution.py:34
  67.7 40.4 %collective-permute-start.5 = (bf16[7,128,768]{2,1,0:T(8,128)(2,1)S(1)}, bf16[7,128,768]{2,1,0:T(8,128)(2,1)S(1)}, u32[]{:S(2)}, u32[]{:S(2)}) collective-permute-start(bf16[7,128,768]{2,1,0:T(8,128)(2,1)S(1)} %collective-permute-done.3.refs_7_), channel_id=1, source_target_pairs={{0,4},{4,0},{8,12},{12,8},{16,20},{20,16},{24,28},{28,24},{1,5},{5... | collective-permute-start | bytes 4128776 | tf_op jit(solution)/shard_map/ppermute | solution.py:34
  68.4 20.3 %collective-permute-start.4 = (bf16[7,128,256]{2,1,0:T(8,128)(2,1)S(1)}, bf16[7,128,256]{2,1,0:T(8,128)(2,1)S(1)}, u32[]{:S(2)}, u32[]{:S(2)}) collective-permute-start(bf16[7,128,256]{2,1,0:T(8,128)(2,1)S(1)} %split.9), channel_id=1, source_target_pairs={{0,8},{4,12},{8,0},{12,4},{16,24},{20,28},{24,16},{28,20},{1,9},{5... | collective-permute-start | bytes 1376264 | tf_op jit(solution)/shard_map/ppermute | solution.py:34
  68.5 23.7 %collective-permute-start.8 = (f32[1,21,32,128]{3,2,1,0:T(8,128)S(1)}, f32[1,21,32,128]{3,2,1,0:T(8,128)S(1)}, u32[]{:S(2)}, u32[]{:S(2)}) collective-permute-start(f32[1,21,32,128]{3,2,1,0:T(8,128)S(1)} %slice_bitcast_fusion.2), channel_id=1, source_target_pairs={{0,2},{1,3},{2,0},{3,1},{4,6},{5,7},{6,4},{7,5},{8,10},{9,11},{10,... | collective-permute-start | bytes 1032200 | tf_op jit(solution)/shard_map/ppermute | solution.py:34
  88.7 19.4 %collective-permute-start.6 = (bf16[7,128,256]{2,1,0:T(8,128)(2,1)S(1)}, bf16[7,128,256]{2,1,0:T(8,128)(2,1)S(1)}, u32[]{:S(2)}, u32[]{:S(2)}) collective-permute-start(bf16[7,128,256]{2,1,0:T(8,128)(2,1)S(1)} %collective-permute-done.4.refs_8_), channel_id=1, source_target_pairs={{0,4},{4,0},{8,12},{12,8},{16,20},{20,16},{24,28},{28,24},{1,5},{5... | collective-permute-start | bytes 1376264 | tf_op jit(solution)/shard_map/ppermute | solution.py:34
  112.2 1.8 collective-permute-start.11
  112.2 3.5 %collective-permute-start.9 = (f32[2,28,32,128]{3,2,1,0:T(8,128)S(1)}, f32[2,28,32,128]{3,2,1,0:T(8,128)S(1)}, u32[]{:S(2)}, u32[]{:S(2)}) collective-permute-start(f32[2,28,32,128]{3,2,1,0:T(8,128)S(1)} %get-tuple-element.36), channel_id=1, source_target_pairs={{0,1},{1,0},{2,3},{3,2},{4,5},{5,4},{6,7},{7,6},{8,9},{9,8},{10,11... | collective-permute-start | bytes 2752520 | tf_op jit(solution)/shard_map/ppermute | solution.py:34
  114.1 8.5 %collective-permute-start.12 = (f32[1,14,32,128]{3,2,1,0:T(8,128)S(1)}, f32[1,14,32,128]{3,2,1,0:T(8,128)S(1)}, u32[]{:S(2)}, u32[]{:S(2)}) collective-permute-start(f32[1,14,32,128]{3,2,1,0:T(8,128)S(1)} %slice_bitcast_fusion.4), channel_id=1, source_target_pairs={{0,2},{1,3},{2,0},{3,1},{4,6},{5,7},{6,4},{7,5},{8,10},{9,11},{10,... | collective-permute-start | bytes 688136 | tf_op jit(solution)/shard_map/ppermute | solution.py:34
  115.9 15.8 %collective-permute-start.10 = (f32[1,28,32,128]{3,2,1,0:T(8,128)S(1)}, f32[1,28,32,128]{3,2,1,0:T(8,128)S(1)}, u32[]{:S(2)}, u32[]{:S(2)}) collective-permute-start(f32[1,28,32,128]{3,2,1,0:T(8,128)S(1)} %slice_bitcast_fusion), channel_id=1, source_target_pairs={{0,2},{1,3},{2,0},{3,1},{4,6},{5,7},{6,4},{7,5},{8,10},{9,11},{10,... | collective-permute-start | bytes 1376264 | tf_op jit(solution)/shard_map/ppermute | solution.py:34
  133.4 5.3 %collective-permute-start.13 = (f32[32,128]{1,0:T(8,128)S(1)}, f32[32,128]{1,0:T(8,128)S(1)}, u32[]{:S(2)}, u32[]{:S(2)}) collective-permute-start(f32[32,128]{1,0:T(8,128)S(1)} %row_stats.1.refs_3_), channel_id=1, source_target_pairs={{0,16},{4,20},{8,24},{12,28},{16,0},{20,4},{24,8},{28,12},{1,17},{... | collective-permute-start | bytes 49160 | tf_op jit(solution)/shard_map/ppermute | solution.py:34
  140.7 6.0 %collective-permute-start.20 = (bf16[14,32,128]{2,1,0:T(8,128)(2,1)S(1)}, bf16[14,32,128]{2,1,0:T(8,128)(2,1)S(1)}, u32[]{:S(2)}, u32[]{:S(2)}) collective-permute-start(bf16[14,32,128]{2,1,0:T(8,128)(2,1)S(1)} %get-tuple-element.42.refs_5_.refs_19_), channel_id=1, source_target_pairs={{0,2},{1,3},{2,0},{3,1},{4,6},{5,7},{6,4},{7,5},{8,10},{9,11},{10,... | collective-permute-start | bytes 344072 | tf_op jit(solution)/shard_map/ppermute | solution.py:34
  142.2 6.9 %collective-permute-start.17 = (bf16[28,32,128]{2,1,0:T(8,128)(2,1)S(1)}, bf16[28,32,128]{2,1,0:T(8,128)(2,1)S(1)}, u32[]{:S(2)}, u32[]{:S(2)}) collective-permute-start(bf16[28,32,128]{2,1,0:T(8,128)(2,1)S(1)} %get-tuple-element.41.refs_15_.refs_5_), channel_id=1, source_target_pairs={{0,2},{1,3},{2,0},{3,1},{4,6},{5,7},{6,4},{7,5},{8,10},{9,11},{10,... | collective-permute-start | bytes 688136 | tf_op jit(solution)/shard_map/ppermute | solution.py:34
  142.7 3.9 %collective-permute-start.21 = (bf16[14,32,128]{2,1,0:T(8,128)(2,1)S(1)}, bf16[14,32,128]{2,1,0:T(8,128)(2,1)S(1)}, u32[]{:S(2)}, u32[]{:S(2)}) collective-permute-start(bf16[14,32,128]{2,1,0:T(8,128)(2,1)S(1)} %get-tuple-element.42.refs_5_.refs_19_), channel_id=1, source_target_pairs={{0,1},{1,0},{2,3},{3,2},{4,5},{5,4},{6,7},{7,6},{8,9},{9,8},{10,11... | collective-permute-start | bytes 344072 | tf_op jit(solution)/shard_map/ppermute | solution.py:34
  153.3 23.4 %collective-permute-start.24 = (bf16[7,128,512]{2,1,0:T(8,128)(2,1)S(1)}, bf16[7,128,512]{2,1,0:T(8,128)(2,1)S(1)}, u32[]{:S(2)}, u32[]{:S(2)}) collective-permute-start(bf16[7,128,512]{2,1,0:T(8,128)(2,1)S(1)} %get-tuple-element.51), channel_id=1, source_target_pairs={{0,4},{4,0},{8,12},{12,8},{16,20},{20,16},{24,28},{28,24},{1,5},{5... | collective-permute-start | bytes 2752520 | tf_op jit(solution)/shard_map/ppermute | solution.py:34
  153.9 5.4 %collective-permute-start.14 = (bf16[21,32,128]{2,1,0:T(8,128)(2,1)S(1)}, bf16[21,32,128]{2,1,0:T(8,128)(2,1)S(1)}, u32[]{:S(2)}, u32[]{:S(2)}) collective-permute-start(bf16[21,32,128]{2,1,0:T(8,128)(2,1)S(1)} %get-tuple-element.40.refs_11_), channel_id=1, source_target_pairs={{0,2},{1,3},{2,0},{3,1},{4,6},{5,7},{6,4},{7,5},{8,10},{9,11},{10,... | collective-permute-start | bytes 516104 | tf_op jit(solution)/shard_map/ppermute | solution.py:34
  155.4 5.4 %collective-permute-start.18 = (bf16[28,32,128]{2,1,0:T(8,128)(2,1)S(1)}, bf16[28,32,128]{2,1,0:T(8,128)(2,1)S(1)}, u32[]{:S(2)}, u32[]{:S(2)}) collective-permute-start(bf16[28,32,128]{2,1,0:T(8,128)(2,1)S(1)} %get-tuple-element.41.refs_15_.refs_5_), channel_id=1, source_target_pairs={{0,1},{1,0},{2,3},{3,2},{4,5},{5,4},{6,7},{7,6},{8,9},{9,8},{10,11... | collective-permute-start | bytes 688136 | tf_op jit(solution)/shard_map/ppermute | solution.py:34
  155.4 5.5 %collective-permute-start.19 = (bf16[28,32,128]{2,1,0:T(8,128)(2,1)S(1)}, bf16[28,32,128]{2,1,0:T(8,128)(2,1)S(1)}, u32[]{:S(2)}, u32[]{:S(2)}) collective-permute-start(bf16[28,32,128]{2,1,0:T(8,128)(2,1)S(1)} %collective-permute-done.17.refs_9_.refs_16_.refs_6_), channel_id=1, source_target_pairs={{0,1},{1,0},{2,3},{3,2},{4,5},{5,4},{6,7},{7,6},{8,9},{9,8},{10,11... | collective-permute-start | bytes 688136 | tf_op jit(solution)/shard_map/ppermute | solution.py:34
  155.9 3.4 %collective-permute-start.15 = (bf16[21,32,128]{2,1,0:T(8,128)(2,1)S(1)}, bf16[21,32,128]{2,1,0:T(8,128)(2,1)S(1)}, u32[]{:S(2)}, u32[]{:S(2)}) collective-permute-start(bf16[21,32,128]{2,1,0:T(8,128)(2,1)S(1)} %get-tuple-element.40.refs_11_), channel_id=1, source_target_pairs={{0,1},{1,0},{2,3},{3,2},{4,5},{5,4},{6,7},{7,6},{8,9},{9,8},{10,11... | collective-permute-start | bytes 516104 | tf_op jit(solution)/shard_map/ppermute | solution.py:34
  159.3 1.5 collective-permute-start.16
  159.3 37.0 %collective-permute-start.26 = (bf16[7,128,512]{2,1,0:T(8,128)(2,1)S(1)}, bf16[7,128,512]{2,1,0:T(8,128)(2,1)S(1)}, u32[]{:S(2)}, u32[]{:S(2)}) collective-permute-start(bf16[7,128,512]{2,1,0:T(8,128)(2,1)S(1)} %get-tuple-element.43.refs_23_), channel_id=1, source_target_pairs={{0,4},{4,0},{8,12},{12,8},{16,20},{20,16},{24,28},{28,24},{1,5},{5... | collective-permute-start | bytes 2752520 | tf_op jit(solution)/shard_map/ppermute | solution.py:34
  169.2 82.5 %collective-permute-start.23 = (bf16[7,128,1024]{2,1,0:T(8,128)(2,1)S(1)}, bf16[7,128,1024]{2,1,0:T(8,128)(2,1)S(1)}, u32[]{:S(2)}, u32[]{:S(2)}) collective-permute-start(bf16[7,128,1024]{2,1,0:T(8,128)(2,1)S(1)} %get-tuple-element.44.refs_23_), channel_id=1, source_target_pairs={{0,16},{4,20},{8,24},{12,28},{16,0},{20,4},{24,8},{28,12},{1,17},{... | collective-permute-start | bytes 5505032 | tf_op jit(solution)/shard_map/ppermute | solution.py:34
  176.7 80.0 %collective-permute-start.25 = (bf16[7,128,1024]{2,1,0:T(8,128)(2,1)S(1)}, bf16[7,128,1024]{2,1,0:T(8,128)(2,1)S(1)}, u32[]{:S(2)}, u32[]{:S(2)}) collective-permute-start(bf16[7,128,1024]{2,1,0:T(8,128)(2,1)S(1)} %get-tuple-element.52), channel_id=1, source_target_pairs={{0,4},{4,0},{8,12},{12,8},{16,20},{20,16},{24,28},{28,24},{1,5},{5... | collective-permute-start | bytes 5505032 | tf_op jit(solution)/shard_map/ppermute | solution.py:34
  180.8 71.4 %collective-permute-start.28 = (bf16[7,128,512]{2,1,0:T(8,128)(2,1)S(1)}, bf16[7,128,512]{2,1,0:T(8,128)(2,1)S(1)}, u32[]{:S(2)}, u32[]{:S(2)}) collective-permute-start(bf16[7,128,512]{2,1,0:T(8,128)(2,1)S(1)} %term_2_1.1), channel_id=1, source_target_pairs={{0,8},{4,12},{8,0},{12,4},{16,24},{20,28},{24,16},{28,20},{1,9},{5... | collective-permute-start | bytes 2752520 | tf_op jit(solution)/shard_map/ppermute | solution.py:34
  200.0 56.7 %collective-permute-start.27 = (bf16[7,128,512]{2,1,0:T(8,128)(2,1)S(1)}, bf16[7,128,512]{2,1,0:T(8,128)(2,1)S(1)}, u32[]{:S(2)}, u32[]{:S(2)}) collective-permute-start(bf16[7,128,512]{2,1,0:T(8,128)(2,1)S(1)} %term_2_0.1), channel_id=1, source_target_pairs={{0,8},{4,12},{8,0},{12,4},{16,24},{20,28},{24,16},{28,20},{1,9},{5... | collective-permute-start | bytes 2752520 | tf_op jit(solution)/shard_map/ppermute | solution.py:34
  258.8 3.7 %collective-permute-start.30 = (f32[2,8,128]{2,1,0:T(8,128)S(1)}, f32[2,8,128]{2,1,0:T(8,128)S(1)}, u32[]{:S(2)}, u32[]{:S(2)}) collective-permute-start(f32[2,8,128]{2,1,0:T(8,128)S(1)} %fusion.12), channel_id=1, source_target_pairs={{0,2},{1,3},{2,0},{3,1},{4,6},{5,7},{6,4},{7,5},{8,10},{9,11},{10,... | collective-permute-start | bytes 24584 | tf_op jit(solution)/shard_map/ppermute | solution.py:34
  262.4 3.7 %collective-permute-start.31 = (f32[2,8,128]{2,1,0:T(8,128)S(1)}, f32[2,8,128]{2,1,0:T(8,128)S(1)}, u32[]{:S(2)}, u32[]{:S(2)}) collective-permute-start(f32[2,8,128]{2,1,0:T(8,128)S(1)} %fusion.14), channel_id=1, source_target_pairs={{0,4},{4,0},{8,12},{12,8},{16,20},{20,16},{24,28},{28,24},{1,5},{5... | collective-permute-start | bytes 24584 | tf_op jit(solution)/shard_map/ppermute | solution.py:34
  266.1 3.7 %collective-permute-start.32 = (f32[2,8,128]{2,1,0:T(8,128)S(1)}, f32[2,8,128]{2,1,0:T(8,128)S(1)}, u32[]{:S(2)}, u32[]{:S(2)}) collective-permute-start(f32[2,8,128]{2,1,0:T(8,128)S(1)} %add.143), channel_id=1, source_target_pairs={{0,8},{4,12},{8,0},{12,4},{16,24},{20,28},{24,16},{28,20},{1,9},{5... | collective-permute-start | bytes 24584 | tf_op jit(solution)/shard_map/ppermute | solution.py:34
  269.7 5.9 %collective-permute-start.33 = (f32[2,8,128]{2,1,0:T(8,128)S(1)}, f32[2,8,128]{2,1,0:T(8,128)S(1)}, u32[]{:S(2)}, u32[]{:S(2)}) collective-permute-start(f32[2,8,128]{2,1,0:T(8,128)S(1)} %add.144), channel_id=1, source_target_pairs={{0,16},{4,20},{8,24},{12,28},{16,0},{20,4},{24,8},{28,12},{1,17},{... | collective-permute-start | bytes 24584 | tf_op jit(solution)/shard_map/ppermute | solution.py:34
  (6 other events, 29.5 us)

commit v6 on v5

--- a/solution.py
+++ b/solution.py
@@ -14,7 +14,7 @@
 VMEM_LIMIT = 56 * 1024 * 1024
 SLACK = 4 * 1024 * 1024
 COST = 1
-IN_CUT = 6
+IN_CUT = 4
 OUT_CUT = 4
 
 VM = pl.BlockSpec(memory_space=pltpu.VMEM)

time: 283 us -> 282 us (level)
  starting transfers between devices: 42 us -> 33.1 us
  waiting for transfers between devices: 176 us -> 184 us
    ppermute x34, starting transfers between devices: 42 us -> 33.1 us  [swap(): return lax.ppermute(value, axis, [(i, i ^ mask) for i in range(size)])]
    ppermute x34, waiting for transfers between devices: 176 us -> 184 us  [swap(): return lax.ppermute(value, axis, [(i, i ^ mask) for i in range(size)])]
  transfers between devices with their start and end apart: 34 -> 34, of which waited for: 21 -> 23; matrix products, arithmetic and copies ran while one was open for 2% -> 2% of each run, Pallas kernels for 13% -> 13%
where the time goes in v6:
time: 282 us
  waiting for transfers between devices  184 us (65%)
  Pallas kernels  50.7 us (18%)
  starting transfers between devices  33.1 us (12%)
  local copies, waits for them, and re-layouts  5.47 us (2%)
  other arithmetic  4.78 us (2%)
  between operations  3.37 us (1%)
    ppermute x34, waiting for transfers between devices, swap(): return lax.ppermute(value, axis, [(i, i ^ mask) for i in range(size)])  184 us
    pallas_call x12, Pallas kernels, call(): pl.pallas_call(body, name=name, out_shape=out_shape, in_specs=[SM] * smem...  50.7 us
    ppermute x34, starting transfers between devices, swap(): return lax.ppermute(value, axis, [(i, i ^ mask) for i in range(size)])  33.1 us
  transfers between devices with their start and end apart: 34, of which 23 were waited for; matrix products, arithmetic and copies ran while one was open for 2% of the time, Pallas kernels for 13%

profile of v6, /device:TPU:0, one launch (start us, length us, event | category | flops | bytes accessed | tf_op | source)
XLA Modules:
  0.0 281.8 jit_solution(4477245509364618313)
XLA Ops:
  0.6 4.1 %collective-permute-start = (s32[7,8]{1,0:T(8,128)}, s32[7,8]{1,0:T(8,128)S(1)}, u32[]{:S(2)}, u32[]{:S(2)}) collective-permute-start(s32[7,8]{1,0:T(8,128)} %param.5), channel_id=1, source_target_pairs={{0,16},{4,20},{8,24},{12,28},{16,0},{20,4},{24,8},{28,12},{1,17},{... | collective-permute-start | bytes 680 | tf_op jit(solution)/shard_map/ppermute | solution.py:34
  6.3 2.8 fusion.13
  11.9 36.4 %collective-permute-done.3.refs_7_ = bf16[7,128,512]{2,1,0:T(8,128)(2,1)S(1)} collective-permute-done((bf16[7,128,512]{2,1,0:T(8,128)(2,1)}, bf16[7,128,512]{2,1,0:T(8,128)(2,1)S(1)}, u32[]{:S(2)}, u32[]{:S(2)}) %collective-permute-start.3) | collective-permute-done | bytes 917536 | tf_op jit(solution)/shard_map/ppermute | solution.py:34
  50.1 5.3 %logits_0.1 = (f32[2,21,32,128]{3,2,1,0:T(8,128)S(1)}, f32[2,21,32,128]{3,2,1,0:T(8,128)S(1)}, f32[8,128]{1,0:T(8,128)S(1)}) custom-call(s32[28]{0:T(128)S(1)} %select_reduce_fusion.3.refs_0_.refs_1_, s32[28]{0:T(128)S(1)} %select_reduce_fusion.3.refs_0_.refs_1_, s32[1]{0:T(128)} %bitcast.refs_2_, bf16[7,128,1024]{2,1,0:T(8,128)(2,1)S(1)} %bitcast.48, ...), custom_call_target="tpu_custom_call" | custom-call | flops 704643072 | bytes 6885376 | tf_op jit(solution)/shard_map/logits_0/pallas_call | solution.py:49
  56.2 32.8 %collective-permute-done.4.refs_8_ = bf16[7,128,512]{2,1,0:T(8,128)(2,1)S(1)} collective-permute-done((bf16[7,128,512]{2,1,0:T(8,128)(2,1)}, bf16[7,128,512]{2,1,0:T(8,128)(2,1)S(1)}, u32[]{:S(2)}, u32[]{:S(2)}) %collective-permute-start.4) | collective-permute-done | bytes 917536 | tf_op jit(solution)/shard_map/ppermute | solution.py:34
  91.9 6.0 %collective-permute-done.8 = f32[1,21,32,128]{3,2,1,0:T(8,128)S(1)} collective-permute-done((f32[1,21,32,128]{3,2,1,0:T(8,128)S(1)}, f32[1,21,32,128]{3,2,1,0:T(8,128)S(1)}, u32[]{:S(2)}, u32[]{:S(2)}) %collective-permute-start.8) | collective-permute-done | bytes 344096 | tf_op jit(solution)/shard_map/ppermute | solution.py:34
  98.0 5.3 %logits_1.1 = (f32[2,28,32,128]{3,2,1,0:T(8,128)S(1)}, f32[2,28,32,128]{3,2,1,0:T(8,128)S(1)}, f32[8,128]{1,0:T(8,128)S(1)}) custom-call(s32[28]{0:T(128)S(1)} %select_reduce_fusion.3.refs_0_.refs_1_, s32[28]{0:T(128)S(1)} %select_reduce_fusion.2.refs_6_.refs_1_, s32[1]{0:T(128)} %bitcast.refs_2_, bf16[7,128,1024]{2,1,0:T(8,128)(2,1)S(1)} %bitcast.49, ...), custom_call_target="tpu_custom_call" | custom-call | flops 939524096 | bytes 11014144 | tf_op jit(solution)/shard_map/logits_1/pallas_call | solution.py:49
  103.3 6.3 %collective-permute-done.6.refs_6_.refs_10_ = bf16[7,128,512]{2,1,0:T(8,128)(2,1)S(1)} collective-permute-done((bf16[7,128,512]{2,1,0:T(8,128)(2,1)S(1)}, bf16[7,128,512]{2,1,0:T(8,128)(2,1)S(1)}, u32[]{:S(2)}, u32[]{:S(2)}) %collective-permute-start.6) | collective-permute-done | bytes 917536 | tf_op jit(solution)/shard_map/ppermute | solution.py:34
  109.6 4.1 %logits_2.1 = (f32[2,14,32,128]{3,2,1,0:T(8,128)S(1)}, f32[2,14,32,128]{3,2,1,0:T(8,128)S(1)}, f32[8,128]{1,0:T(8,128)}) custom-call(s32[28]{0:T(128)S(1)} %select_reduce_fusion.3.refs_0_.refs_1_, s32[28]{0:T(128)S(1)} %select_reduce_fusion.2.refs_6_.refs_1_, s32[1]{0:T(128)} %bitcast.refs_2_, bf16[7,128,1024]{2,1,0:T(8,128)(2,1)S(1)} %bitcast.50, ...), custom_call_target="tpu_custom_call" | custom-call | flops 469762048 | bytes 6426624 | tf_op jit(solution)/shard_map/logits_2/pallas_call | solution.py:49
  118.7 5.5 %collective-permute-done.12 = f32[1,14,32,128]{3,2,1,0:T(8,128)S(1)} collective-permute-done((f32[1,14,32,128]{3,2,1,0:T(8,128)S(1)}, f32[1,14,32,128]{3,2,1,0:T(8,128)S(1)}, u32[]{:S(2)}, u32[]{:S(2)}) %collective-permute-start.12) | collective-permute-done | bytes 229408 | tf_op jit(solution)/shard_map/ppermute | solution.py:34
  124.2 9.0 %collective-permute-done.10 = f32[1,28,32,128]{3,2,1,0:T(8,128)S(1)} collective-permute-done((f32[1,28,32,128]{3,2,1,0:T(8,128)S(1)}, f32[1,28,32,128]{3,2,1,0:T(8,128)S(1)}, u32[]{:S(2)}, u32[]{:S(2)}) %collective-permute-start.10) | collective-permute-done | bytes 458784 | tf_op jit(solution)/shard_map/ppermute | solution.py:34
  136.3 3.4 %collective-permute-done.13.refs_4_ = f32[32,128]{1,0:T(8,128)S(1)} collective-permute-done((f32[32,128]{1,0:T(8,128)S(1)}, f32[32,128]{1,0:T(8,128)S(1)}, u32[]{:S(2)}, u32[]{:S(2)}) %collective-permute-start.13) | collective-permute-done | bytes 16416 | tf_op jit(solution)/shard_map/ppermute | solution.py:34
  139.7 1.9 weights.1
  143.7 3.6 %collective-permute-done.20.refs_6_.refs_20_ = bf16[14,32,128]{2,1,0:T(8,128)(2,1)S(1)} collective-permute-done((bf16[14,32,128]{2,1,0:T(8,128)(2,1)S(1)}, bf16[14,32,128]{2,1,0:T(8,128)(2,1)S(1)}, u32[]{:S(2)}, u32[]{:S(2)}) %collective-permute-start.20) | collective-permute-done | bytes 114720 | tf_op jit(solution)/shard_map/ppermute | solution.py:34
  149.8 4.2 %terms_far.1 = (bf16[7,128,512]{2,1,0:T(8,128)(2,1)S(1)}, bf16[7,128,512]{2,1,0:T(8,128)(2,1)S(1)}) custom-call(s32[28]{0:T(128)S(1)} %select_reduce_fusion.3.refs_0_.refs_1_, s32[28]{0:T(128)S(1)} %select_reduce_fusion.2.refs_6_.refs_1_, s32[1]{0:T(128)} %bitcast.refs_2_, bf16[7,128,1024]{2,1,0:T(8,128)(2,1)S(1)} %bitcast.51, ...), custom_call_target="tpu_custom_call" | custom-call | flops 234881024 | bytes 5963776 | tf_op jit(solution)/shard_map/terms_far/pallas_call | solution.py:49
  156.8 3.4 %collective-permute-done.14.refs_12_ = bf16[21,32,128]{2,1,0:T(8,128)(2,1)S(1)} collective-permute-done((bf16[21,32,128]{2,1,0:T(8,128)(2,1)S(1)}, bf16[21,32,128]{2,1,0:T(8,128)(2,1)S(1)}, u32[]{:S(2)}, u32[]{:S(2)}) %collective-permute-start.14) | collective-permute-done | bytes 172064 | tf_op jit(solution)/shard_map/ppermute | solution.py:34
  161.6 8.3 %grads_lead.1 = (bf16[7,128,1024]{2,1,0:T(8,128)(2,1)S(1)}, bf16[7,128,1024]{2,1,0:T(8,128)(2,1)S(1)}) custom-call(s32[28]{0:T(128)S(1)} %select_reduce_fusion.3.refs_0_.refs_1_, s32[28]{0:T(128)S(1)} %select_reduce_fusion.2.refs_6_.refs_1_, s32[1]{0:T(128)} %bitcast.refs_2_, bf16[7,128,1024]{2,1,0:T(8,128)(2,1)S(1)} %bitcast.52, ...), custom_call_target="tpu_custom_call" | custom-call | flops 469762048 | bytes 16744448 | tf_op jit(solution)/shard_map/grads_lead/pallas_call | solution.py:49
  171.4 6.0 %collective-permute-done.24.refs_9_ = bf16[7,128,512]{2,1,0:T(8,128)(2,1)S(1)} collective-permute-done((bf16[7,128,512]{2,1,0:T(8,128)(2,1)S(1)}, bf16[7,128,512]{2,1,0:T(8,128)(2,1)S(1)}, u32[]{:S(2)}, u32[]{:S(2)}) %collective-permute-start.24) | collective-permute-done | bytes 917536 | tf_op jit(solution)/shard_map/ppermute | solution.py:34
  178.1 3.6 %term_2_1.1 = bf16[7,128,512]{2,1,0:T(8,128)(2,1)S(1)} custom-call(s32[28]{0:T(128)S(1)} %select_reduce_fusion.3.refs_0_.refs_1_, s32[28]{0:T(128)S(1)} %select_reduce_fusion.2.refs_6_.refs_1_, s32[1]{0:T(128)} %bitcast.refs_2_, bf16[7,128,1024]{2,1,0:T(8,128)(2,1)S(1)} %bitcast.53, bf16[7,128,1024]{2,1,0:T(8,128)(2,1)} %collective-permute-done.1.refs_4_, ...), custom_call_target="tpu_custom_call" | custom-call | flops 234881024 | bytes 6422528 | tf_op jit(solution)/shard_map/term_2_1/pallas_call | solution.py:49
  181.7 2.5 collective-permute-start.28
  184.2 12.9 %collective-permute-done.26.refs_9_ = bf16[7,128,512]{2,1,0:T(8,128)(2,1)S(1)} collective-permute-done((bf16[7,128,512]{2,1,0:T(8,128)(2,1)S(1)}, bf16[7,128,512]{2,1,0:T(8,128)(2,1)S(1)}, u32[]{:S(2)}, u32[]{:S(2)}) %collective-permute-start.26) | collective-permute-done | bytes 917536 | tf_op jit(solution)/shard_map/ppermute | solution.py:34
  197.1 3.6 %term_2_0.1 = bf16[7,128,512]{2,1,0:T(8,128)(2,1)S(1)} custom-call(s32[28]{0:T(128)S(1)} %select_reduce_fusion.3.refs_0_.refs_1_, s32[28]{0:T(128)S(1)} %select_reduce_fusion.2.refs_6_.refs_1_, s32[1]{0:T(128)} %bitcast.refs_2_, bf16[7,128,1024]{2,1,0:T(8,128)(2,1)S(1)} %bitcast.54, bf16[7,128,1024]{2,1,0:T(8,128)(2,1)} %collective-permute-done.1.refs_4_, ...), custom_call_target="tpu_custom_call" | custom-call | flops 234881024 | bytes 6422528 | tf_op jit(solution)/shard_map/term_2_0/pallas_call | solution.py:49
  200.7 2.5 collective-permute-start.27
  203.2 11.2 %grads_own.1 = (f32[7,128,1024]{2,1,0:T(8,128)S(1)}, f32[7,128,1024]{2,1,0:T(8,128)S(1)}) custom-call(s32[28]{0:T(128)S(1)} %select_reduce_fusion.3.refs_0_.refs_1_, s32[28]{0:T(128)S(1)} %select_reduce_fusion.2.refs_6_.refs_1_, s32[1]{0:T(128)} %bitcast.refs_2_, bf16[7,128,1024]{2,1,0:T(8,128)(2,1)S(1)} %bitcast.55, ...), custom_call_target="tpu_custom_call" | custom-call | flops 469762048 | bytes 20414464 | tf_op jit(solution)/shard_map/grads_own/pallas_call | solution.py:49
  214.4 38.1 %collective-permute-done.23.refs_2_ = bf16[7,128,1024]{2,1,0:T(8,128)(2,1)S(1)} collective-permute-done((bf16[7,128,1024]{2,1,0:T(8,128)(2,1)S(1)}, bf16[7,128,1024]{2,1,0:T(8,128)(2,1)S(1)}, u32[]{:S(2)}, u32[]{:S(2)}) %collective-permute-start.23) | collective-permute-done | bytes 1835040 | tf_op jit(solution)/shard_map/ppermute | solution.py:34
  253.0 4.5 %collective-permute-done.27.refs_3_ = bf16[7,128,512]{2,1,0:T(8,128)(2,1)S(1)} collective-permute-done((bf16[7,128,512]{2,1,0:T(8,128)(2,1)S(1)}, bf16[7,128,512]{2,1,0:T(8,128)(2,1)S(1)}, u32[]{:S(2)}, u32[]{:S(2)}) %collective-permute-start.27) | collective-permute-done | bytes 917536 | tf_op jit(solution)/shard_map/ppermute | solution.py:34
  261.1 2.2 collective-permute-done.30
  264.7 2.3 collective-permute-done.31
  267.0 3.6 %collective-permute-done.32 = f32[2,8,128]{2,1,0:T(8,128)S(1)} collective-permute-done((f32[2,8,128]{2,1,0:T(8,128)S(1)}, f32[2,8,128]{2,1,0:T(8,128)S(1)}, u32[]{:S(2)}, u32[]{:S(2)}) %collective-permute-start.32) | collective-permute-done | bytes 8224 | tf_op jit(solution)/shard_map/ppermute | solution.py:34
  270.6 1.8 collective-permute-start.33
  272.5 2.7 collective-permute-done.33
  276.6 1.8 multiply_convert_fusion
  (94 shorter events, 36.5 us)
Async XLA Ops:
  0.6 10.8 %collective-permute-start = (s32[7,8]{1,0:T(8,128)}, s32[7,8]{1,0:T(8,128)S(1)}, u32[]{:S(2)}, u32[]{:S(2)}) collective-permute-start(s32[7,8]{1,0:T(8,128)} %param.5), channel_id=1, source_target_pairs={{0,16},{4,20},{8,24},{12,28},{16,0},{20,4},{24,8},{28,12},{1,17},{... | collective-permute-start | bytes 680 | tf_op jit(solution)/shard_map/ppermute | solution.py:34
  4.7 43.8 %collective-permute-start.2 = (bf16[7,128,1024]{2,1,0:T(8,128)(2,1)}, bf16[7,128,1024]{2,1,0:T(8,128)(2,1)}, u32[]{:S(2)}, u32[]{:S(2)}) collective-permute-start(bf16[7,128,1024]{2,1,0:T(8,128)(2,1)} %bitcast.56), channel_id=1, source_target_pairs={{0,4},{4,0},{8,12},{12,8},{16,20},{20,16},{24,28},{28,24},{1,5},{5... | collective-permute-start | bytes 5505032 | tf_op jit(solution)/shard_map/ppermute | solution.py:34
  9.1 39.3 %collective-permute-start.3 = (bf16[7,128,512]{2,1,0:T(8,128)(2,1)}, bf16[7,128,512]{2,1,0:T(8,128)(2,1)S(1)}, u32[]{:S(2)}, u32[]{:S(2)}) collective-permute-start(bf16[7,128,512]{2,1,0:T(8,128)(2,1)} %get-tuple-element.56), channel_id=1, source_target_pairs={{0,8},{4,12},{8,0},{12,4},{16,24},{20,28},{24,16},{28,20},{1,9},{5... | collective-permute-start | bytes 2752520 | tf_op jit(solution)/shard_map/ppermute | solution.py:34
  10.7 81.3 %collective-permute-start.1 = (bf16[7,128,1024]{2,1,0:T(8,128)(2,1)S(1)}, bf16[7,128,1024]{2,1,0:T(8,128)(2,1)}, u32[]{:S(2)}, u32[]{:S(2)}) collective-permute-start(bf16[7,128,1024]{2,1,0:T(8,128)(2,1)S(1)} %bitcast.47), channel_id=1, source_target_pairs={{0,16},{4,20},{8,24},{12,28},{16,0},{20,4},{24,8},{28,12},{1,17},{... | collective-permute-start | bytes 5505032 | tf_op jit(solution)/shard_map/ppermute | solution.py:34
  48.4 40.7 %collective-permute-start.4 = (bf16[7,128,512]{2,1,0:T(8,128)(2,1)}, bf16[7,128,512]{2,1,0:T(8,128)(2,1)S(1)}, u32[]{:S(2)}, u32[]{:S(2)}) collective-permute-start(bf16[7,128,512]{2,1,0:T(8,128)(2,1)} %get-tuple-element.30), channel_id=1, source_target_pairs={{0,8},{4,12},{8,0},{12,4},{16,24},{20,28},{24,16},{28,20},{1,9},{5... | collective-permute-start | bytes 2752520 | tf_op jit(solution)/shard_map/ppermute | solution.py:34
  55.4 34.2 %collective-permute-start.7 = (f32[2,21,32,128]{3,2,1,0:T(8,128)S(1)}, f32[2,21,32,128]{3,2,1,0:T(8,128)S(1)}, u32[]{:S(2)}, u32[]{:S(2)}) collective-permute-start(f32[2,21,32,128]{3,2,1,0:T(8,128)S(1)} %get-tuple-element.34), channel_id=1, source_target_pairs={{0,1},{1,0},{2,3},{3,2},{4,5},{5,4},{6,7},{7,6},{8,9},{9,8},{10,11... | collective-permute-start | bytes 2064392 | tf_op jit(solution)/shard_map/ppermute | solution.py:34
  55.5 47.8 %collective-permute-start.5 = (bf16[7,128,512]{2,1,0:T(8,128)(2,1)S(1)}, bf16[7,128,512]{2,1,0:T(8,128)(2,1)S(1)}, u32[]{:S(2)}, u32[]{:S(2)}) collective-permute-start(bf16[7,128,512]{2,1,0:T(8,128)(2,1)S(1)} %collective-permute-done.3.refs_7_), channel_id=1, source_target_pairs={{0,4},{4,0},{8,12},{12,8},{16,20},{20,16},{24,28},{28,24},{1,5},{5... | collective-permute-start | bytes 2752520 | tf_op jit(solution)/shard_map/ppermute | solution.py:34
  89.0 20.6 %collective-permute-start.6 = (bf16[7,128,512]{2,1,0:T(8,128)(2,1)S(1)}, bf16[7,128,512]{2,1,0:T(8,128)(2,1)S(1)}, u32[]{:S(2)}, u32[]{:S(2)}) collective-permute-start(bf16[7,128,512]{2,1,0:T(8,128)(2,1)S(1)} %collective-permute-done.4.refs_8_), channel_id=1, source_target_pairs={{0,4},{4,0},{8,12},{12,8},{16,20},{20,16},{24,28},{28,24},{1,5},{5... | collective-permute-start | bytes 2752520 | tf_op jit(solution)/shard_map/ppermute | solution.py:34
  89.8 8.2 %collective-permute-start.8 = (f32[1,21,32,128]{3,2,1,0:T(8,128)S(1)}, f32[1,21,32,128]{3,2,1,0:T(8,128)S(1)}, u32[]{:S(2)}, u32[]{:S(2)}) collective-permute-start(f32[1,21,32,128]{3,2,1,0:T(8,128)S(1)} %slice_bitcast_fusion.2), channel_id=1, source_target_pairs={{0,2},{1,3},{2,0},{3,1},{4,6},{5,7},{6,4},{7,5},{8,10},{9,11},{10,... | collective-permute-start | bytes 1032200 | tf_op jit(solution)/shard_map/ppermute | solution.py:34
  113.8 1.8 collective-permute-start.11
  113.8 3.5 %collective-permute-start.9 = (f32[2,28,32,128]{3,2,1,0:T(8,128)S(1)}, f32[2,28,32,128]{3,2,1,0:T(8,128)S(1)}, u32[]{:S(2)}, u32[]{:S(2)}) collective-permute-start(f32[2,28,32,128]{3,2,1,0:T(8,128)S(1)} %get-tuple-element.36), channel_id=1, source_target_pairs={{0,1},{1,0},{2,3},{3,2},{4,5},{5,4},{6,7},{7,6},{8,9},{9,8},{10,11... | collective-permute-start | bytes 2752520 | tf_op jit(solution)/shard_map/ppermute | solution.py:34
  115.7 8.5 %collective-permute-start.12 = (f32[1,14,32,128]{3,2,1,0:T(8,128)S(1)}, f32[1,14,32,128]{3,2,1,0:T(8,128)S(1)}, u32[]{:S(2)}, u32[]{:S(2)}) collective-permute-start(f32[1,14,32,128]{3,2,1,0:T(8,128)S(1)} %slice_bitcast_fusion.4), channel_id=1, source_target_pairs={{0,2},{1,3},{2,0},{3,1},{4,6},{5,7},{6,4},{7,5},{8,10},{9,11},{10,... | collective-permute-start | bytes 688136 | tf_op jit(solution)/shard_map/ppermute | solution.py:34
  117.5 15.8 %collective-permute-start.10 = (f32[1,28,32,128]{3,2,1,0:T(8,128)S(1)}, f32[1,28,32,128]{3,2,1,0:T(8,128)S(1)}, u32[]{:S(2)}, u32[]{:S(2)}) collective-permute-start(f32[1,28,32,128]{3,2,1,0:T(8,128)S(1)} %slice_bitcast_fusion), channel_id=1, source_target_pairs={{0,2},{1,3},{2,0},{3,1},{4,6},{5,7},{6,4},{7,5},{8,10},{9,11},{10,... | collective-permute-start | bytes 1376264 | tf_op jit(solution)/shard_map/ppermute | solution.py:34
  135.0 4.7 %collective-permute-start.13 = (f32[32,128]{1,0:T(8,128)S(1)}, f32[32,128]{1,0:T(8,128)S(1)}, u32[]{:S(2)}, u32[]{:S(2)}) collective-permute-start(f32[32,128]{1,0:T(8,128)S(1)} %row_stats.1.refs_3_), channel_id=1, source_target_pairs={{0,16},{4,20},{8,24},{12,28},{16,0},{20,4},{24,8},{28,12},{1,17},{... | collective-permute-start | bytes 49160 | tf_op jit(solution)/shard_map/ppermute | solution.py:34
  141.7 5.7 %collective-permute-start.20 = (bf16[14,32,128]{2,1,0:T(8,128)(2,1)S(1)}, bf16[14,32,128]{2,1,0:T(8,128)(2,1)S(1)}, u32[]{:S(2)}, u32[]{:S(2)}) collective-permute-start(bf16[14,32,128]{2,1,0:T(8,128)(2,1)S(1)} %get-tuple-element.42.refs_5_.refs_19_), channel_id=1, source_target_pairs={{0,2},{1,3},{2,0},{3,1},{4,6},{5,7},{6,4},{7,5},{8,10},{9,11},{10,... | collective-permute-start | bytes 344072 | tf_op jit(solution)/shard_map/ppermute | solution.py:34
  143.2 6.6 %collective-permute-start.17 = (bf16[28,32,128]{2,1,0:T(8,128)(2,1)S(1)}, bf16[28,32,128]{2,1,0:T(8,128)(2,1)S(1)}, u32[]{:S(2)}, u32[]{:S(2)}) collective-permute-start(bf16[28,32,128]{2,1,0:T(8,128)(2,1)S(1)} %get-tuple-element.41.refs_15_.refs_5_), channel_id=1, source_target_pairs={{0,2},{1,3},{2,0},{3,1},{4,6},{5,7},{6,4},{7,5},{8,10},{9,11},{10,... | collective-permute-start | bytes 688136 | tf_op jit(solution)/shard_map/ppermute | solution.py:34
  143.7 3.6 %collective-permute-start.21 = (bf16[14,32,128]{2,1,0:T(8,128)(2,1)S(1)}, bf16[14,32,128]{2,1,0:T(8,128)(2,1)S(1)}, u32[]{:S(2)}, u32[]{:S(2)}) collective-permute-start(bf16[14,32,128]{2,1,0:T(8,128)(2,1)S(1)} %get-tuple-element.42.refs_5_.refs_19_), channel_id=1, source_target_pairs={{0,1},{1,0},{2,3},{3,2},{4,5},{5,4},{6,7},{7,6},{8,9},{9,8},{10,11... | collective-permute-start | bytes 344072 | tf_op jit(solution)/shard_map/ppermute | solution.py:34
  154.0 23.4 %collective-permute-start.24 = (bf16[7,128,512]{2,1,0:T(8,128)(2,1)S(1)}, bf16[7,128,512]{2,1,0:T(8,128)(2,1)S(1)}, u32[]{:S(2)}, u32[]{:S(2)}) collective-permute-start(bf16[7,128,512]{2,1,0:T(8,128)(2,1)S(1)} %get-tuple-element.51), channel_id=1, source_target_pairs={{0,4},{4,0},{8,12},{12,8},{16,20},{20,16},{24,28},{28,24},{1,5},{5... | collective-permute-start | bytes 2752520 | tf_op jit(solution)/shard_map/ppermute | solution.py:34
  154.8 5.4 %collective-permute-start.14 = (bf16[21,32,128]{2,1,0:T(8,128)(2,1)S(1)}, bf16[21,32,128]{2,1,0:T(8,128)(2,1)S(1)}, u32[]{:S(2)}, u32[]{:S(2)}) collective-permute-start(bf16[21,32,128]{2,1,0:T(8,128)(2,1)S(1)} %get-tuple-element.40.refs_11_), channel_id=1, source_target_pairs={{0,2},{1,3},{2,0},{3,1},{4,6},{5,7},{6,4},{7,5},{8,10},{9,11},{10,... | collective-permute-start | bytes 516104 | tf_op jit(solution)/shard_map/ppermute | solution.py:34
  156.3 5.3 %collective-permute-start.18 = (bf16[28,32,128]{2,1,0:T(8,128)(2,1)S(1)}, bf16[28,32,128]{2,1,0:T(8,128)(2,1)S(1)}, u32[]{:S(2)}, u32[]{:S(2)}) collective-permute-start(bf16[28,32,128]{2,1,0:T(8,128)(2,1)S(1)} %get-tuple-element.41.refs_15_.refs_5_), channel_id=1, source_target_pairs={{0,1},{1,0},{2,3},{3,2},{4,5},{5,4},{6,7},{7,6},{8,9},{9,8},{10,11... | collective-permute-start | bytes 688136 | tf_op jit(solution)/shard_map/ppermute | solution.py:34
  156.3 5.3 %collective-permute-start.19 = (bf16[28,32,128]{2,1,0:T(8,128)(2,1)S(1)}, bf16[28,32,128]{2,1,0:T(8,128)(2,1)S(1)}, u32[]{:S(2)}, u32[]{:S(2)}) collective-permute-start(bf16[28,32,128]{2,1,0:T(8,128)(2,1)S(1)} %collective-permute-done.17.refs_9_.refs_16_.refs_6_), channel_id=1, source_target_pairs={{0,1},{1,0},{2,3},{3,2},{4,5},{5,4},{6,7},{7,6},{8,9},{9,8},{10,11... | collective-permute-start | bytes 688136 | tf_op jit(solution)/shard_map/ppermute | solution.py:34
  156.8 3.4 %collective-permute-start.15 = (bf16[21,32,128]{2,1,0:T(8,128)(2,1)S(1)}, bf16[21,32,128]{2,1,0:T(8,128)(2,1)S(1)}, u32[]{:S(2)}, u32[]{:S(2)}) collective-permute-start(bf16[21,32,128]{2,1,0:T(8,128)(2,1)S(1)} %get-tuple-element.40.refs_11_), channel_id=1, source_target_pairs={{0,1},{1,0},{2,3},{3,2},{4,5},{5,4},{6,7},{7,6},{8,9},{9,8},{10,11... | collective-permute-start | bytes 516104 | tf_op jit(solution)/shard_map/ppermute | solution.py:34
  160.2 1.4 collective-permute-start.16
  160.2 36.9 %collective-permute-start.26 = (bf16[7,128,512]{2,1,0:T(8,128)(2,1)S(1)}, bf16[7,128,512]{2,1,0:T(8,128)(2,1)S(1)}, u32[]{:S(2)}, u32[]{:S(2)}) collective-permute-start(bf16[7,128,512]{2,1,0:T(8,128)(2,1)S(1)} %get-tuple-element.43.refs_23_), channel_id=1, source_target_pairs={{0,4},{4,0},{8,12},{12,8},{16,20},{20,16},{24,28},{28,24},{1,5},{5... | collective-permute-start | bytes 2752520 | tf_op jit(solution)/shard_map/ppermute | solution.py:34
  170.0 82.5 %collective-permute-start.23 = (bf16[7,128,1024]{2,1,0:T(8,128)(2,1)S(1)}, bf16[7,128,1024]{2,1,0:T(8,128)(2,1)S(1)}, u32[]{:S(2)}, u32[]{:S(2)}) collective-permute-start(bf16[7,128,1024]{2,1,0:T(8,128)(2,1)S(1)} %get-tuple-element.44.refs_23_), channel_id=1, source_target_pairs={{0,16},{4,20},{8,24},{12,28},{16,0},{20,4},{24,8},{28,12},{1,17},{... | collective-permute-start | bytes 5505032 | tf_op jit(solution)/shard_map/ppermute | solution.py:34
  177.4 80.1 %collective-permute-start.25 = (bf16[7,128,1024]{2,1,0:T(8,128)(2,1)S(1)}, bf16[7,128,1024]{2,1,0:T(8,128)(2,1)S(1)}, u32[]{:S(2)}, u32[]{:S(2)}) collective-permute-start(bf16[7,128,1024]{2,1,0:T(8,128)(2,1)S(1)} %get-tuple-element.52), channel_id=1, source_target_pairs={{0,4},{4,0},{8,12},{12,8},{16,20},{20,16},{24,28},{28,24},{1,5},{5... | collective-permute-start | bytes 5505032 | tf_op jit(solution)/shard_map/ppermute | solution.py:34
  181.7 71.3 %collective-permute-start.28 = (bf16[7,128,512]{2,1,0:T(8,128)(2,1)S(1)}, bf16[7,128,512]{2,1,0:T(8,128)(2,1)S(1)}, u32[]{:S(2)}, u32[]{:S(2)}) collective-permute-start(bf16[7,128,512]{2,1,0:T(8,128)(2,1)S(1)} %term_2_1.1), channel_id=1, source_target_pairs={{0,8},{4,12},{8,0},{12,4},{16,24},{20,28},{24,16},{28,20},{1,9},{5... | collective-permute-start | bytes 2752520 | tf_op jit(solution)/shard_map/ppermute | solution.py:34
  200.7 56.9 %collective-permute-start.27 = (bf16[7,128,512]{2,1,0:T(8,128)(2,1)S(1)}, bf16[7,128,512]{2,1,0:T(8,128)(2,1)S(1)}, u32[]{:S(2)}, u32[]{:S(2)}) collective-permute-start(bf16[7,128,512]{2,1,0:T(8,128)(2,1)S(1)} %term_2_0.1), channel_id=1, source_target_pairs={{0,8},{4,12},{8,0},{12,4},{16,24},{20,28},{24,16},{28,20},{1,9},{5... | collective-permute-start | bytes 2752520 | tf_op jit(solution)/shard_map/ppermute | solution.py:34
  259.7 3.7 %collective-permute-start.30 = (f32[2,8,128]{2,1,0:T(8,128)S(1)}, f32[2,8,128]{2,1,0:T(8,128)S(1)}, u32[]{:S(2)}, u32[]{:S(2)}) collective-permute-start(f32[2,8,128]{2,1,0:T(8,128)S(1)} %fusion.12), channel_id=1, source_target_pairs={{0,2},{1,3},{2,0},{3,1},{4,6},{5,7},{6,4},{7,5},{8,10},{9,11},{10,... | collective-permute-start | bytes 24584 | tf_op jit(solution)/shard_map/ppermute | solution.py:34
  263.3 3.7 %collective-permute-start.31 = (f32[2,8,128]{2,1,0:T(8,128)S(1)}, f32[2,8,128]{2,1,0:T(8,128)S(1)}, u32[]{:S(2)}, u32[]{:S(2)}) collective-permute-start(f32[2,8,128]{2,1,0:T(8,128)S(1)} %fusion.15), channel_id=1, source_target_pairs={{0,4},{4,0},{8,12},{12,8},{16,20},{20,16},{24,28},{28,24},{1,5},{5... | collective-permute-start | bytes 24584 | tf_op jit(solution)/shard_map/ppermute | solution.py:34
  267.0 3.7 %collective-permute-start.32 = (f32[2,8,128]{2,1,0:T(8,128)S(1)}, f32[2,8,128]{2,1,0:T(8,128)S(1)}, u32[]{:S(2)}, u32[]{:S(2)}) collective-permute-start(f32[2,8,128]{2,1,0:T(8,128)S(1)} %add.143), channel_id=1, source_target_pairs={{0,8},{4,12},{8,0},{12,4},{16,24},{20,28},{24,16},{28,20},{1,9},{5... | collective-permute-start | bytes 24584 | tf_op jit(solution)/shard_map/ppermute | solution.py:34
  270.6 4.5 %collective-permute-start.33 = (f32[2,8,128]{2,1,0:T(8,128)S(1)}, f32[2,8,128]{2,1,0:T(8,128)S(1)}, u32[]{:S(2)}, u32[]{:S(2)}) collective-permute-start(f32[2,8,128]{2,1,0:T(8,128)S(1)} %add.144), channel_id=1, source_target_pairs={{0,16},{4,20},{8,24},{12,28},{16,0},{20,4},{24,8},{28,12},{1,17},{... | collective-permute-start | bytes 24584 | tf_op jit(solution)/shard_map/ppermute | solution.py:34
  (6 other events, 24.6 us)
